TPU v7x, 32 devices: a whole 2x2x4 slice. The times are simulated.
32 devices in a mesh: tile: 2 (over y), strip: 4 (over x, core), focus: 4 (over z).
Axes of the slice: x: 2, y: 2, z: 4, core: 2. Of those that a mesh axis runs over, the one named last changes fastest.
Arguments:
- phi: float32 [512, 2048], P(('tile', 'strip')), parts along dimension 0, may hold values from -6 to 6
- target: int32 [512, 2048], P(('tile', 'strip')), parts along dimension 0, may hold values 0 or 1
- defocus_ids: int32 [8], P(('tile', 'focus')), parts along dimension 0, may hold values from 0 to 30
- kernels: float32 [2, 4, 48, 512], replicated, may hold values from -16 to 16
- psi: float32 [48, 512], replicated, may hold values from -3.140625 to 3.140625
- row_freqs: int32 [48], replicated, may hold values from -96 to 95, as said below
- col_freqs: int32 [512], replicated, may hold values from -1024 to 1023, as said below
Outputs:
- phi_next: float32 [512, 2048], P(('tile', 'strip')), parts along dimension 0
There are 2 independent parts, one for each index of `tile`. A program takes and returns all parts, laid end to end along the dimension named above; an argument that names none is the same for every part. Nothing has to cross between parts.
Inputs may be any that keep to these rules, and one draw needn't show every extreme that they name: `row_freqs`: distinct whole frequencies; the lowest and highest of the range are always among them. `col_freqs`: distinct whole frequencies; the lowest and highest of the range are always among them.
All inputs are finite; a program needn't handle non-finite values. No bound on the sum of `target` on one device may be relied on, other than what follows from the above.
Results may differ from a plain program's by a relative error of at most 0.02.
Values may be sent and summed in bfloat16 or wider, within the bound.
No kernel may reach another device: no remote copies, remote signals or barrier semaphores. Data moves between devices by JAX's collectives and lax.ppermute only.
A program may use at most 64 MiB of HBM per device.

v0:
```python
import jax
import jax.numpy as jnp
from jax import lax
from jax.sharding import PartitionSpec as P

MARGIN = 64
LEVELS = 31
SWEEPS = 2


slope_resist = 4.0
level_resist = 0.5
step_size = 1.0
flow_rate = 0.2


def padded_2(block, sides, width):
    for axis, dim in sides:
        count = lax.axis_size(axis)
        forward = [(i, i + 1) for i in range(count - 1)]
        backward = [(target, source) for source, target in forward]
        low = lax.ppermute(
            lax.slice_in_dim(block, block.shape[dim] - width, None, axis=dim), axis, forward
        )
        high = lax.ppermute(lax.slice_in_dim(block, 0, width, axis=dim), axis, backward)
        block = jnp.concatenate([low, block, high], axis=dim)
    return block


def tables(freq_list, period, length):
    positions = jnp.arange(length, dtype=jnp.int32)
    phase_int = jnp.mod(freq_list[:, None] * positions[None, :], period)
    angles = phase_int.astype(jnp.float32) * (2.0 * jnp.pi / period)
    return (jnp.cos(angles).astype(jnp.bfloat16), jnp.sin(angles).astype(jnp.bfloat16))


def product(lhs_mat, rhs_mat):
    return jnp.dot(lhs_mat, rhs_mat, preferred_element_type=jnp.float32)


def product_t(lhs_mat, rhs_mat):
    return lax.dot_general(
        lhs_mat, rhs_mat, (((1,), (1,)), ((), ())), preferred_element_type=jnp.float32
    )


def exact_t(lhs_mat, rhs_mat):
    return lax.dot_general(
        lhs_mat.astype(jnp.float32),
        rhs_mat,
        (((0,), (0,)), ((), ())),
        precision=lax.Precision.HIGHEST,
        preferred_element_type=jnp.float32,
    )


def spectral_rows(cos_part, sin_part, y_re, y_im):
    z_re = exact_t(cos_part, y_re) - exact_t(sin_part, y_im)
    z_im = exact_t(cos_part, y_im) + exact_t(sin_part, y_re)
    return jnp.concatenate([z_re, z_im], axis=1).astype(jnp.bfloat16)


def curvature_step(extended):
    padded = jnp.pad(extended, ((0, 0), (1, 1)))
    center = padded[1:-1, 1:-1]
    upper_row = padded[2:, 1:-1]
    lower_row = padded[:-2, 1:-1]
    right_col = padded[1:-1, 2:]
    left_col = padded[1:-1, :-2]
    diagonal = padded[2:, 2:] - padded[2:, :-2] - padded[:-2, 2:] + padded[:-2, :-2]
    grad_x = 0.5 * (upper_row - lower_row)
    grad_y = 0.5 * (right_col - left_col)
    second_x = upper_row - 2.0 * center + lower_row
    second_y = right_col - 2.0 * center + left_col
    cross_term = 0.25 * diagonal
    flow_term = (
        second_x * grad_y * grad_y - 2.0 * grad_x * grad_y * cross_term + second_y * grad_x * grad_x
    ) / (1.0 + grad_x * grad_x + grad_y * grad_y)
    return center + flow_rate * flow_term


def on_device(phi, target, defocus_ids, kernels, psi, row_freqs, col_freqs):
    strip_rows, col_count = phi.shape
    spectrum = psi.shape[1]
    kernel_count = kernels.shape[1]
    window_rows = strip_rows + 2 * MARGIN
    scale_norm = 1.0 / jnp.sqrt(jnp.float32(window_rows * col_count))
    row_cos, row_sin = tables(row_freqs, window_rows, window_rows)
    col_cos, col_sin = tables(col_freqs, col_count, col_count)
    forward = jnp.concatenate([col_cos, -col_sin], axis=0)
    adjoint = jnp.concatenate([col_sin, col_cos], axis=0)
    inner_cos = row_cos[:, MARGIN : MARGIN + strip_rows]
    inner_sin = row_sin[:, MARGIN : MARGIN + strip_rows]
    mask_bf = jnp.tanh(phi).astype(jnp.bfloat16)
    window = padded_2(mask_bf, (("strip", 0),), MARGIN)
    spec_pair = product_t(window, forward).astype(jnp.bfloat16)
    cos_half = product(row_cos, spec_pair)
    sin_half = product(row_sin, spec_pair)
    s_re = scale_norm * (cos_half[:, :spectrum] + sin_half[:, spectrum:])
    s_im = scale_norm * (cos_half[:, spectrum:] - sin_half[:, :spectrum])
    middle = (LEVELS - 1) / 2.0
    defocus = (defocus_ids[0].astype(jnp.float32) - middle) / middle
    phase_turn = defocus * psi
    cos_turn = jnp.cos(phase_turn)
    sin_turn = jnp.sin(phase_turn)
    k_re = kernels[0] * cos_turn - kernels[1] * sin_turn
    k_im = kernels[0] * sin_turn + kernels[1] * cos_turn
    g_pair = jnp.concatenate([k_re * s_re - k_im * s_im, k_re * s_im + k_im * s_re], axis=2).astype(
        jnp.bfloat16
    )
    head_part = jnp.einsum("fr,kfc->krc", inner_cos, g_pair, preferred_element_type=jnp.float32)
    tail_part = jnp.einsum("fr,kfc->krc", inner_sin, g_pair, preferred_element_type=jnp.float32)
    q_re = head_part[..., :spectrum] - tail_part[..., spectrum:]
    q_im = head_part[..., spectrum:] + tail_part[..., :spectrum]
    q_pair = (
        jnp.concatenate([q_re, q_im], axis=2)
        .astype(jnp.bfloat16)
        .reshape(kernel_count * strip_rows, 2 * spectrum)
    )
    e_re = (scale_norm * product(q_pair, forward)).reshape(kernel_count, strip_rows, col_count)
    e_im = (scale_norm * product(q_pair, adjoint)).reshape(kernel_count, strip_rows, col_count)
    intensity = jnp.mean(e_re * e_re + e_im * e_im, axis=0)
    resist = jax.nn.sigmoid(slope_resist * (intensity - level_resist))
    weight = (
        4.0
        * slope_resist
        / kernel_count
        * (resist - target.astype(jnp.float32))
        * resist
        * (1.0 - resist)
    )
    v_re = (weight * e_re).astype(jnp.bfloat16).reshape(kernel_count * strip_rows, col_count)
    v_im = (weight * e_im).astype(jnp.bfloat16).reshape(kernel_count * strip_rows, col_count)
    u_pair = (
        (product_t(v_re, forward) + product_t(v_im, adjoint))
        .astype(jnp.bfloat16)
        .reshape(kernel_count, strip_rows, 2 * spectrum)
    )
    head_back = jnp.einsum("fr,krc->kfc", inner_cos, u_pair, preferred_element_type=jnp.float32)
    tail_back = jnp.einsum("fr,krc->kfc", inner_sin, u_pair, preferred_element_type=jnp.float32)
    w_re = scale_norm * (head_back[..., :spectrum] + tail_back[..., spectrum:])
    w_im = scale_norm * (head_back[..., spectrum:] - tail_back[..., :spectrum])
    y_re = jnp.sum(k_re * w_re + k_im * w_im, axis=0)
    y_im = jnp.sum(k_re * w_im - k_im * w_re, axis=0)
    y_re, y_im = (
        lax.psum(y_re.astype(jnp.bfloat16), "focus").astype(jnp.float32),
        lax.psum(y_im.astype(jnp.bfloat16), "focus").astype(jnp.float32),
    )
    stacked = jnp.stack([y_re, y_im])[None]
    beside_all = padded_2(stacked.astype(jnp.bfloat16), (("strip", 0),), 1).astype(stacked.dtype)
    own_rows = spectral_rows(inner_cos, inner_sin, y_re, y_im)
    prev_rows = spectral_rows(
        row_cos[:, MARGIN + strip_rows :],
        row_sin[:, MARGIN + strip_rows :],
        beside_all[0, 0],
        beside_all[0, 1],
    )
    next_rows = spectral_rows(
        row_cos[:, :MARGIN], row_sin[:, :MARGIN], beside_all[2, 0], beside_all[2, 1]
    )
    grad_rows = scale_norm * product(
        jnp.concatenate([own_rows, prev_rows, next_rows], axis=0), forward
    )
    folded = grad_rows[:strip_rows]
    folded = (
        folded.at[:MARGIN]
        .add(grad_rows[strip_rows : strip_rows + MARGIN])
        .at[strip_rows - MARGIN :]
        .add(grad_rows[strip_rows + MARGIN :])
    )
    mask_slope = 1.0 - jnp.tanh(phi) * jnp.tanh(phi)
    level_set = phi - step_size * mask_slope * folded
    for counter in range(SWEEPS):
        extended_set = padded_2(level_set.astype(jnp.bfloat16), (("strip", 0),), 1).astype(
            level_set.dtype
        )
        level_set = curvature_step(extended_set)
    return level_set


def solution(mesh):
    return jax.shard_map(
        on_device,
        mesh=mesh,
        in_specs=(
            P(("tile", "strip"), None),
            P(("tile", "strip"), None),
            P(("tile", "focus")),
            P(),
            P(),
            P(),
            P(),
        ),
        out_specs=P(("tile", "strip"), None),
        check_vma=False,
    )
```

profile of v0, /device:TPU:0, one launch (start us, length us, event | category | flops | bytes accessed | tf_op | source)
XLA Modules:
  0.0 140.9 jit_solution(1823749973720386125)
XLA Ops:
  6.5 1.1 tanh_convert_fusion
  7.7 1.3 collective-permute-start.1
  9.0 3.0 %collective-permute-start = (bf16[64,2048]{1,0:T(8,128)(2,1)S(1)}, bf16[64,2048]{1,0:T(8,128)(2,1)S(1)}, u32[]{:S(2)}, u32[]{:S(2)}) collective-permute-start(bf16[64,2048]{1,0:T(8,128)(2,1)S(1)} %tanh_convert_fusion), channel_id=1, source_target_pairs={{0,4},{4,8},{8,12},{1,5},{5,9},{9,13},{2,6},{6,10},{10,14},{3,7},{... | collective-permute-start | bytes 786440 | tf_op jit(solution)/shard_map/ppermute | solution.py:22
  12.0 18.9 %sine_convert_fusion = (bf16[512,2048]{1,0:T(8,128)(2,1)S(1)}, bf16[512,2048]{1,0:T(8,128)(2,1)S(1)}) fusion(s32[512]{0:T(512)} %param.21), kind=kLoop, calls=%fused_computation.8 | loop fusion | flops 16777216 | bytes 4196352 | tf_op jit(solution)/shard_map/convert_element_type | solution.py:34
  30.9 16.9 %fusion.22 = bf16[512,2048]{1,0:T(8,128)(2,1)S(1)} fusion(s32[512]{0:T(512)S(1)} %copy-done.9), kind=kLoop, calls=%fused_computation.50 | loop fusion | flops 18874368 | bytes 2099200 | tf_op jit(solution)/shard_map/neg | solution.py:90
  48.8 1.5 %convolution_convert_fusion = bf16[192,1024]{1,0:T(8,128)(2,1)S(1)} fusion(bf16[64,2048]{1,0:T(8,128)(2,1)S(1)} %collective-permute-done.1, bf16[64,2048]{1,0:T(8,128)(2,1)S(1)} %tanh_convert_fusion, bf16[64,2048]{1,0:T(8,128)(2,1)S(1)} %collective-permute-done, bf16[512,2048]{1,0:T(8,128)(2,1)S(1)} %fusion.22, bf16[512,2048]{1,0:T(8,128)(2,1)S(1)} %get-tuple-element.65), kind=kOutput, calls=%fused_computation.28 | convolution fusion | flops 816250880 | bytes 5373952 | tf_op jit(solution)/shard_map/dot_general | solution.py:42
  51.9 0.4 convolution_bitcast_fusion
  53.0 1.3 convolution_multiply_fusion.1
  54.3 3.0 %multiply_add_fusion = (f32[256,2048]{1,0:T(8,128)}, f32[256,2048]{1,0:T(8,128)}) fusion(f32[256,2048]{1,0:T(8,128)S(1)} %convolution_multiply_fusion.1, bf16[512,2048]{1,0:T(8,128)(2,1)S(1)} %get-tuple-element.65, bf16[512,2048]{1,0:T(8,128)(2,1)S(1)} %get-tuple-element.64, bf16[256,512]{1,0:T(8,128)(2,1)S(1)} %bitcast.84, bf16[256,512]{1,0:T(8,128)(2,1)S(1)} %bitcast.82), kind=kOutput, calls=%fused_computation.21 | convolution fusion | flops 1085276160 | bytes 11010048 | tf_op jit(solution)/shard_map/dot_general | solution.py:38
  57.3 1.8 %reduce_sum.27 = f32[64,2048]{1,0:T(8,128)S(1)} reduce(f32[4,64,2048]{2,1,0:T(8,128)} %bitcast.76, f32[]{:T(128)} %constant.126.clone.1), dimensions={0}, to_apply=%region_0.1 | reduce | flops 393216 | bytes 2621444 | tf_op jit(solution)/shard_map/reduce_sum | solution.py:122
  59.1 1.3 subtract_multiply_fusion
  60.3 2.9 %fusion.8 = (bf16[256,2048]{1,0:T(8,128)(2,1)S(1)}, bf16[256,2048]{1,0:T(8,128)(2,1)S(1)}) fusion(f32[256,2048]{1,0:T(8,128)} %get-tuple-element.69, f32[64,2048]{1,0:T(8,128)S(1)} %subtract_multiply_fusion, f32[256,2048]{1,0:T(8,128)} %copy-done), kind=kLoop, calls=%fused_computation.20 | loop fusion | flops 2097152 | bytes 6815744 | tf_op jit(solution)/shard_map/convert_element_type | solution.py:133
  63.3 1.3 fusion.107
  64.9 1.3 fusion.10
  66.8 0.9 add_reduce_fusion
  67.7 37.4 %all-reduce.5.cloned.1.call-done = (bf16[48,512]{1,0:T(8,128)(2,1)}, bf16[48,512]{1,0:T(8,128)(2,1)}) async-done(((bf16[48,512]{1,0:T(8,128)(2,1)}, bf16[48,512]{1,0:T(8,128)(2,1)}), (bf16[48,512]{1,0:T(8,128)(2,1)}, bf16[48,512]{1,0:T(8,128)(2,1)})) %all-reduce.5.cloned.1.call-update) | async-done | bytes 98320 | tf_op jit(solution)/shard_map/psum | solution.py:147
  105.1 1.0 pad_maximum_fusion.14
  106.1 1.3 collective-permute-start.3
  107.4 3.2 %collective-permute-start.2 = (bf16[1,2,48,512]{3,2,1,0:T(8,128)(2,1)S(1)}, bf16[1,2,48,512]{3,2,1,0:T(8,128)(2,1)S(1)}, u32[]{:S(2)}, u32[]{:S(2)}) collective-permute-start(bf16[1,2,48,512]{3,2,1,0:T(8,128)(2,1)S(1)} %pad_maximum_fusion.14), channel_id=1, source_target_pairs={{0,4},{4,8},{8,12},{1,5},{5,9},{9,13},{2,6},{6,10},{10,14},{3,7},{... | collective-permute-start | bytes 294920 | tf_op jit(solution)/shard_map/ppermute | solution.py:22
  110.6 1.0 fusion.89
  111.7 1.0 fusion.87
  112.8 1.1 fusion.12
  113.8 1.1 fusion.11
  116.4 1.0 convolution_multiply_fusion.2
  117.7 3.0 %collective-permute-start.4 = (bf16[1,2048]{1,0:T(2,128)(2,1)S(1)}, bf16[1,2048]{1,0:T(2,128)(2,1)S(1)}, u32[]{:S(2)}, u32[]{:S(2)}) collective-permute-start(bf16[1,2048]{1,0:T(2,128)(2,1)S(1)} %get-tuple-element.60), channel_id=1, source_target_pairs={{0,4},{4,8},{8,12},{1,5},{5,9},{9,13},{2,6},{6,10},{10,14},{3,7},{... | collective-permute-start | bytes 12296 | tf_op jit(solution)/shard_map/ppermute | solution.py:22
  120.7 1.3 collective-permute-start.5
  122.0 1.8 %collective-permute-done.5 = bf16[1,2048]{1,0:T(2,128)(2,1)S(1)} collective-permute-done((bf16[1,2048]{1,0:T(2,128)(2,1)S(1)}, bf16[1,2048]{1,0:T(2,128)(2,1)S(1)}, u32[]{:S(2)}, u32[]{:S(2)}) %collective-permute-start.5) | collective-permute-done | bytes 4128 | tf_op jit(solution)/shard_map/ppermute | solution.py:25
  123.8 1.0 add_convert_fusion
  124.9 4.3 %collective-permute-start.6 = (bf16[1,2048]{1,0:T(2,128)(2,1)S(1)}, bf16[1,2048]{1,0:T(2,128)(2,1)S(1)}, u32[]{:S(2)}, u32[]{:S(2)}) collective-permute-start(bf16[1,2048]{1,0:T(2,128)(2,1)S(1)} %get-tuple-element.58), channel_id=1, source_target_pairs={{0,4},{4,8},{8,12},{1,5},{5,9},{9,13},{2,6},{6,10},{10,14},{3,7},{... | collective-permute-start | bytes 12296 | tf_op jit(solution)/shard_map/ppermute | solution.py:22
  129.2 1.3 collective-permute-start.7
  130.5 1.8 %collective-permute-done.7 = bf16[1,2048]{1,0:T(2,128)(2,1)S(1)} collective-permute-done((bf16[1,2048]{1,0:T(2,128)(2,1)S(1)}, bf16[1,2048]{1,0:T(2,128)(2,1)S(1)}, u32[]{:S(2)}, u32[]{:S(2)}) %collective-permute-start.7) | collective-permute-done | bytes 4128 | tf_op jit(solution)/shard_map/ppermute | solution.py:25
  132.3 1.8 %multiply_add_fusion.1 = f32[64,2048]{1,0:T(8,128)} fusion(f32[66,2048]{1,0:T(8,128)S(1)} %maximum_convert_fusion.1), kind=kLoop, calls=%fused_computation.89 | loop fusion | flops 3670016 | bytes 2686976 | tf_op jit(solution)/shard_map/add | solution.py:79
  (53 shorter events, 5.2 us)
Async XLA Ops:
  6.5 98.6 %all-reduce.5.cloned.1.call-start = ((), (), s32[]{:S(2)}) async-start(), calls=%async_computation | async-start | bytes 196608 | tf_op jit(solution)/shard_map/psum | solution.py:147
  7.7 23.2 %copy-start.9 = (s32[512]{0:T(512)S(1)}, s32[512]{0:T(512)}, u32[]{:S(2)}) copy-start(s32[512]{0:T(512)} %param.21) | copy-start | bytes 6148
  7.7 41.1 %collective-permute-start.1 = (bf16[64,2048]{1,0:T(8,128)(2,1)S(1)}, bf16[64,2048]{1,0:T(8,128)(2,1)S(1)}, u32[]{:S(2)}, u32[]{:S(2)}) collective-permute-start(bf16[64,2048]{1,0:T(8,128)(2,1)S(1)} %tanh_convert_fusion), channel_id=1, source_target_pairs={{4,0},{8,4},{12,8},{5,1},{9,5},{13,9},{6,2},{10,6},{14,10},{7,3},{... | collective-permute-start | bytes 786440 | tf_op jit(solution)/shard_map/ppermute | solution.py:25
  9.0 39.9 %collective-permute-start = (bf16[64,2048]{1,0:T(8,128)(2,1)S(1)}, bf16[64,2048]{1,0:T(8,128)(2,1)S(1)}, u32[]{:S(2)}, u32[]{:S(2)}) collective-permute-start(bf16[64,2048]{1,0:T(8,128)(2,1)S(1)} %tanh_convert_fusion), channel_id=1, source_target_pairs={{0,4},{4,8},{8,12},{1,5},{5,9},{9,13},{2,6},{6,10},{10,14},{3,7},{... | collective-permute-start | bytes 786440 | tf_op jit(solution)/shard_map/ppermute | solution.py:22
  30.9 23.4 %copy-start.1 = (bf16[512,2048]{1,0:T(8,128)(2,1)}, bf16[512,2048]{1,0:T(8,128)(2,1)S(1)}, u32[]{:S(2)}) copy-start(bf16[512,2048]{1,0:T(8,128)(2,1)S(1)} %get-tuple-element.65) | copy-start | bytes 6291460
  30.9 23.4 %copy-start.4 = (bf16[512,2048]{1,0:T(8,128)(2,1)}, bf16[512,2048]{1,0:T(8,128)(2,1)S(1)}, u32[]{:S(2)}) copy-start(bf16[512,2048]{1,0:T(8,128)(2,1)S(1)} %get-tuple-element.64) | copy-start | bytes 6291460
  30.9 17.6 %copy-start.10 = (s32[48]{0:T(128)S(1)}, s32[48]{0:T(128)}, u32[]{:S(2)}) copy-start(s32[48]{0:T(128)} %param.20) | copy-start | bytes 580
  48.8 2.4 %copy-start.8 = (f32[48,512]{1,0:T(8,128)S(1)}, f32[48,512]{1,0:T(8,128)}, u32[]{:S(2)}) copy-start(f32[48,512]{1,0:T(8,128)} %param.19) | copy-start | bytes 294916
  50.4 1.2 copy-start.7
  54.3 3.0 %copy-start = (f32[256,2048]{1,0:T(8,128)}, f32[256,2048]{1,0:T(8,128)S(1)}, u32[]{:S(2)}) copy-start(f32[256,2048]{1,0:T(8,128)S(1)} %convolution_multiply_fusion.1) | copy-start | bytes 6291460
  60.3 2.9 %copy-start.2 = (bf16[512,2048]{1,0:T(8,128)(2,1)S(1)}, bf16[512,2048]{1,0:T(8,128)(2,1)}, u32[]{:S(2)}) copy-start(bf16[512,2048]{1,0:T(8,128)(2,1)} %copy-done.1) | copy-start | bytes 6291460
  63.3 1.6 %copy-start.5 = (bf16[512,2048]{1,0:T(8,128)(2,1)S(1)}, bf16[512,2048]{1,0:T(8,128)(2,1)}, u32[]{:S(2)}) copy-start(bf16[512,2048]{1,0:T(8,128)(2,1)} %copy-done.4) | copy-start | bytes 6291460
  105.1 11.3 %copy-start.3 = (bf16[512,2048]{1,0:T(8,128)(2,1)S(1)}, bf16[512,2048]{1,0:T(8,128)(2,1)}, u32[]{:S(2)}) copy-start(bf16[512,2048]{1,0:T(8,128)(2,1)} %copy-done.1) | copy-start | bytes 6291460
  106.1 9.1 %collective-permute-start.3 = (bf16[1,2,48,512]{3,2,1,0:T(8,128)(2,1)S(1)}, bf16[1,2,48,512]{3,2,1,0:T(8,128)(2,1)S(1)}, u32[]{:S(2)}, u32[]{:S(2)}) collective-permute-start(bf16[1,2,48,512]{3,2,1,0:T(8,128)(2,1)S(1)} %pad_maximum_fusion.14), channel_id=1, source_target_pairs={{4,0},{8,4},{12,8},{5,1},{9,5},{13,9},{6,2},{10,6},{14,10},{7,3},{... | collective-permute-start | bytes 294920 | tf_op jit(solution)/shard_map/ppermute | solution.py:25
  107.4 7.5 %collective-permute-start.2 = (bf16[1,2,48,512]{3,2,1,0:T(8,128)(2,1)S(1)}, bf16[1,2,48,512]{3,2,1,0:T(8,128)(2,1)S(1)}, u32[]{:S(2)}, u32[]{:S(2)}) collective-permute-start(bf16[1,2,48,512]{3,2,1,0:T(8,128)(2,1)S(1)} %pad_maximum_fusion.14), channel_id=1, source_target_pairs={{0,4},{4,8},{8,12},{1,5},{5,9},{9,13},{2,6},{6,10},{10,14},{3,7},{... | collective-permute-start | bytes 294920 | tf_op jit(solution)/shard_map/ppermute | solution.py:22
  116.4 1.1 copy-start.6
  117.7 4.3 %collective-permute-start.4 = (bf16[1,2048]{1,0:T(2,128)(2,1)S(1)}, bf16[1,2048]{1,0:T(2,128)(2,1)S(1)}, u32[]{:S(2)}, u32[]{:S(2)}) collective-permute-start(bf16[1,2048]{1,0:T(2,128)(2,1)S(1)} %get-tuple-element.60), channel_id=1, source_target_pairs={{0,4},{4,8},{8,12},{1,5},{5,9},{9,13},{2,6},{6,10},{10,14},{3,7},{... | collective-permute-start | bytes 12296 | tf_op jit(solution)/shard_map/ppermute | solution.py:22
  120.7 3.1 %collective-permute-start.5 = (bf16[1,2048]{1,0:T(2,128)(2,1)S(1)}, bf16[1,2048]{1,0:T(2,128)(2,1)S(1)}, u32[]{:S(2)}, u32[]{:S(2)}) collective-permute-start(bf16[1,2048]{1,0:T(2,128)(2,1)S(1)} %get-tuple-element.61), channel_id=1, source_target_pairs={{4,0},{8,4},{12,8},{5,1},{9,5},{13,9},{6,2},{10,6},{14,10},{7,3},{... | collective-permute-start | bytes 12296 | tf_op jit(solution)/shard_map/ppermute | solution.py:25
  124.9 5.6 %collective-permute-start.6 = (bf16[1,2048]{1,0:T(2,128)(2,1)S(1)}, bf16[1,2048]{1,0:T(2,128)(2,1)S(1)}, u32[]{:S(2)}, u32[]{:S(2)}) collective-permute-start(bf16[1,2048]{1,0:T(2,128)(2,1)S(1)} %get-tuple-element.58), channel_id=1, source_target_pairs={{0,4},{4,8},{8,12},{1,5},{5,9},{9,13},{2,6},{6,10},{10,14},{3,7},{... | collective-permute-start | bytes 12296 | tf_op jit(solution)/shard_map/ppermute | solution.py:22
  129.2 3.1 %collective-permute-start.7 = (bf16[1,2048]{1,0:T(2,128)(2,1)S(1)}, bf16[1,2048]{1,0:T(2,128)(2,1)S(1)}, u32[]{:S(2)}, u32[]{:S(2)}) collective-permute-start(bf16[1,2048]{1,0:T(2,128)(2,1)S(1)} %get-tuple-element.59), channel_id=1, source_target_pairs={{4,0},{8,4},{12,8},{5,1},{9,5},{13,9},{6,2},{10,6},{14,10},{7,3},{... | collective-permute-start | bytes 12296 | tf_op jit(solution)/shard_map/ppermute | solution.py:25
Sparse Core Ops, SparseCore 0:
  67.8 37.2 all-reduce.4
where the time goes:
time: 143 us; the launch traced here: 141 us
  other arithmetic  49 us (34%)
  waiting for transfers between devices  41 us (29%)
  starting transfers between devices  18.7 us (13%)
  matrix products  17.2 us (12%)
  between operations  14.6 us (10%)
    psum x1, waiting for transfers between devices, on_device(): lax.psum(y_im.astype(jnp.bfloat16), 'focus').astype(jnp.float32)  37.4 us
    convert_element_type x1, other arithmetic, tables(): jnp.sin(angles).astype(jnp.bfloat16)  18.9 us
    neg x1, other arithmetic, on_device(): forward = jnp.concatenate([col_cos, -col_sin], axis=0)  16.9 us
    ppermute x4, starting transfers between devices, padded_2(): lax.ppermute(lax.slice_in_dim(block, block.shape[dim] - width, None, axis...  13.6 us
    dot_general x5, matrix products, product(): return jnp.dot(lhs_mat, rhs_mat, preferred_element_type=jnp.float32)  6.07 us
    dot_general x12, matrix products, exact_t(): lax.dot_general(lhs_mat.astype(jnp.float32), rhs_mat, (((0,), (0,)), ((),...  5.64 us
    ppermute x4, starting transfers between devices, padded_2(): lax.ppermute(lax.slice_in_dim(block, 0, width, axis=dim), axis, backward)  5.17 us
    dot_general x3, matrix products, product_t(): lax.dot_general(lhs_mat, rhs_mat, (((1,), (1,)), ((), ())), preferred_ele...  4.11 us
  transfers between devices with their start and end apart: 9, of which 3 were waited for; matrix products, arithmetic and copies ran while one was open for 29% of the time, Pallas kernels for 0%

commit v1 on v0

--- a/solution.py
+++ b/solution.py
@@ -6,6 +6,7 @@
 MARGIN = 64
 LEVELS = 31
 SWEEPS = 2
+HALO = SWEEPS
 
 
 slope_resist = 4.0
@@ -14,24 +15,46 @@
 flow_rate = 0.2
 
 
-def padded_2(block, sides, width):
-    for axis, dim in sides:
-        count = lax.axis_size(axis)
-        forward = [(i, i + 1) for i in range(count - 1)]
-        backward = [(target, source) for source, target in forward]
-        low = lax.ppermute(
-            lax.slice_in_dim(block, block.shape[dim] - width, None, axis=dim), axis, forward
-        )
-        high = lax.ppermute(lax.slice_in_dim(block, 0, width, axis=dim), axis, backward)
-        block = jnp.concatenate([low, block, high], axis=dim)
-    return block
-
-
-def tables(freq_list, period, length):
-    positions = jnp.arange(length, dtype=jnp.int32)
+def ring_shift(block, axis, step):
+    count = lax.axis_size(axis)
+    return lax.ppermute(block, axis, [(i, (i + step) % count) for i in range(count)])
+
+
+def focus_sum(part):
+    count = lax.axis_size("focus")
+    total = part
+    step = 1
+    while step < count:
+        held = lax.optimization_barrier(total.astype(jnp.bfloat16))
+        other = lax.ppermute(held, "focus", [(i, i ^ step) for i in range(count)])
+        total = held.astype(jnp.float32) + other.astype(jnp.float32)
+        step *= 2
+    return total
+
+
+SIN_TERMS = (1.0, -1.0 / 6, 1.0 / 120, -1.0 / 5040, 1.0 / 362880, -1.0 / 39916800)
+COS_TERMS = (1.0, -0.5, 1.0 / 24, -1.0 / 720, 1.0 / 40320, -1.0 / 3628800, 1.0 / 479001600)
+
+
+def cos_sin(angle):
+    half = 0.5 * angle
+    square = half * half
+    s = jnp.full_like(half, SIN_TERMS[-1])
+    for term in SIN_TERMS[-2::-1]:
+        s = s * square + term
+    s = s * half
+    c = jnp.full_like(half, COS_TERMS[-1])
+    for term in COS_TERMS[-2::-1]:
+        c = c * square + term
+    return 1.0 - 2.0 * s * s, 2.0 * s * c
+
+
+def tables(freq_list, positions, period):
     phase_int = jnp.mod(freq_list[:, None] * positions[None, :], period)
+    phase_int = jnp.where(2 * phase_int >= period, phase_int - period, phase_int)
     angles = phase_int.astype(jnp.float32) * (2.0 * jnp.pi / period)
-    return (jnp.cos(angles).astype(jnp.bfloat16), jnp.sin(angles).astype(jnp.bfloat16))
+    cos_part, sin_part = cos_sin(angles)
+    return cos_part.astype(jnp.bfloat16), sin_part.astype(jnp.bfloat16)
 
 
 def product(lhs_mat, rhs_mat):
@@ -42,22 +65,6 @@
     return lax.dot_general(
         lhs_mat, rhs_mat, (((1,), (1,)), ((), ())), preferred_element_type=jnp.float32
     )
-
-
-def exact_t(lhs_mat, rhs_mat):
-    return lax.dot_general(
-        lhs_mat.astype(jnp.float32),
-        rhs_mat,
-        (((0,), (0,)), ((), ())),
-        precision=lax.Precision.HIGHEST,
-        preferred_element_type=jnp.float32,
-    )
-
-
-def spectral_rows(cos_part, sin_part, y_re, y_im):
-    z_re = exact_t(cos_part, y_re) - exact_t(sin_part, y_im)
-    z_im = exact_t(cos_part, y_im) + exact_t(sin_part, y_re)
-    return jnp.concatenate([z_re, z_im], axis=1).astype(jnp.bfloat16)
 
 
 def curvature_step(extended):
@@ -85,14 +92,33 @@
     kernel_count = kernels.shape[1]
     window_rows = strip_rows + 2 * MARGIN
     scale_norm = 1.0 / jnp.sqrt(jnp.float32(window_rows * col_count))
-    row_cos, row_sin = tables(row_freqs, window_rows, window_rows)
-    col_cos, col_sin = tables(col_freqs, col_count, col_count)
+    strips = lax.axis_size("strip")
+    place = lax.axis_index("strip")
+    columns = jnp.arange(col_count, dtype=jnp.int32)
+    col_cos, col_sin = tables(col_freqs, columns, col_count)
+    row_cos, row_sin = tables(row_freqs, jnp.arange(window_rows, dtype=jnp.int32), window_rows)
     forward = jnp.concatenate([col_cos, -col_sin], axis=0)
     adjoint = jnp.concatenate([col_sin, col_cos], axis=0)
     inner_cos = row_cos[:, MARGIN : MARGIN + strip_rows]
     inner_sin = row_sin[:, MARGIN : MARGIN + strip_rows]
-    mask_bf = jnp.tanh(phi).astype(jnp.bfloat16)
-    window = padded_2(mask_bf, (("strip", 0),), MARGIN)
+    mask = jnp.tanh(phi)
+    mask_bf = mask.astype(jnp.bfloat16)
+    edges = jnp.concatenate([phi[:HALO], phi[strip_rows - HALO :]], axis=0)
+    edges_high = edges.astype(jnp.bfloat16)
+    edges_low = (edges - edges_high.astype(jnp.float32)).astype(jnp.bfloat16)
+    packet = jnp.concatenate([mask_bf, edges_high, edges_low], axis=0)
+    above = ring_shift(packet, "strip", 1)
+    below = ring_shift(packet, "strip", -1)
+    above = jnp.where(place > 0, above, jnp.zeros_like(above))
+    below = jnp.where(place < strips - 1, below, jnp.zeros_like(below))
+    window = jnp.concatenate(
+        [above[strip_rows - MARGIN : strip_rows], mask_bf, below[:MARGIN]], axis=0
+    )
+    above_edges = above[strip_rows:].astype(jnp.float32)
+    below_edges = below[strip_rows:].astype(jnp.float32)
+    above_phi = above_edges[HALO : 2 * HALO] + above_edges[3 * HALO :]
+    below_phi = below_edges[:HALO] + below_edges[2 * HALO : 3 * HALO]
+    tall_phi = jnp.concatenate([above_phi, phi, below_phi], axis=0)
     spec_pair = product_t(window, forward).astype(jnp.bfloat16)
     cos_half = product(row_cos, spec_pair)
     sin_half = product(row_sin, spec_pair)
@@ -101,8 +127,7 @@
     middle = (LEVELS - 1) / 2.0
     defocus = (defocus_ids[0].astype(jnp.float32) - middle) / middle
     phase_turn = defocus * psi
-    cos_turn = jnp.cos(phase_turn)
-    sin_turn = jnp.sin(phase_turn)
+    cos_turn, sin_turn = cos_sin(phase_turn)
     k_re = kernels[0] * cos_turn - kernels[1] * sin_turn
     k_im = kernels[0] * sin_turn + kernels[1] * cos_turn
     g_pair = jnp.concatenate([k_re * s_re - k_im * s_im, k_re * s_im + k_im * s_re], axis=2).astype(
@@ -142,39 +167,46 @@
     w_im = scale_norm * (head_back[..., spectrum:] - tail_back[..., :spectrum])
     y_re = jnp.sum(k_re * w_re + k_im * w_im, axis=0)
     y_im = jnp.sum(k_re * w_im - k_im * w_re, axis=0)
-    y_re, y_im = (
-        lax.psum(y_re.astype(jnp.bfloat16), "focus").astype(jnp.float32),
-        lax.psum(y_im.astype(jnp.bfloat16), "focus").astype(jnp.float32),
-    )
-    stacked = jnp.stack([y_re, y_im])[None]
-    beside_all = padded_2(stacked.astype(jnp.bfloat16), (("strip", 0),), 1).astype(stacked.dtype)
-    own_rows = spectral_rows(inner_cos, inner_sin, y_re, y_im)
-    prev_rows = spectral_rows(
-        row_cos[:, MARGIN + strip_rows :],
-        row_sin[:, MARGIN + strip_rows :],
-        beside_all[0, 0],
-        beside_all[0, 1],
-    )
-    next_rows = spectral_rows(
-        row_cos[:, :MARGIN], row_sin[:, :MARGIN], beside_all[2, 0], beside_all[2, 1]
-    )
-    grad_rows = scale_norm * product(
-        jnp.concatenate([own_rows, prev_rows, next_rows], axis=0), forward
-    )
-    folded = grad_rows[:strip_rows]
-    folded = (
-        folded.at[:MARGIN]
-        .add(grad_rows[strip_rows : strip_rows + MARGIN])
-        .at[strip_rows - MARGIN :]
-        .add(grad_rows[strip_rows + MARGIN :])
-    )
-    mask_slope = 1.0 - jnp.tanh(phi) * jnp.tanh(phi)
-    level_set = phi - step_size * mask_slope * folded
+    own = focus_sum(jnp.concatenate([y_re, y_im], axis=0)).astype(jnp.bfloat16)
+    reach = (MARGIN + HALO + strip_rows - 1) // strip_rows
+    rows = jnp.arange(-HALO, strip_rows + HALO, dtype=jnp.int32)
+    groups = {}
+    for offset in range(-reach, reach + 1):
+        groups.setdefault(offset % strips, []).append(offset)
+    z_pair = 0.0
+    for shift, offsets in groups.items():
+        spectra = own if shift == 0 else ring_shift(own, "strip", -shift)
+        kept = 0.0
+        for offset in offsets:
+            spot = rows - offset * strip_rows + MARGIN
+            valid = (spot >= 0) & (spot < window_rows)
+            valid = valid & (place + offset >= 0) & (place + offset < strips)
+            part_cos, part_sin = tables(row_freqs, spot, window_rows)
+            weight_row = valid.astype(jnp.float32)[None, :]
+            part = jnp.concatenate(
+                [
+                    jnp.concatenate([part_cos, part_sin], axis=1),
+                    jnp.concatenate([-part_sin, part_cos], axis=1),
+                ],
+                axis=0,
+            )
+            kept = kept + part * jnp.concatenate([weight_row, weight_row], axis=1)
+        z_pair = z_pair + lax.dot_general(
+            kept.astype(jnp.bfloat16),
+            spectra,
+            (((0,), (0,)), ((), ())),
+            preferred_element_type=jnp.float32,
+        )
+    tall = rows.shape[0]
+    z_pair = jnp.concatenate([z_pair[:tall], z_pair[tall:]], axis=1).astype(jnp.bfloat16)
+    gradient = scale_norm * product(z_pair, forward)
+    tall_mask = jnp.tanh(tall_phi)
+    level_set = tall_phi - step_size * (1.0 - tall_mask * tall_mask) * gradient
+    inside = (rows + place * strip_rows >= 0) & (rows + place * strip_rows < strips * strip_rows)
     for counter in range(SWEEPS):
-        extended_set = padded_2(level_set.astype(jnp.bfloat16), (("strip", 0),), 1).astype(
-            level_set.dtype
-        )
-        level_set = curvature_step(extended_set)
+        trim = slice(counter, tall - counter)
+        level_set = jnp.where(inside[trim, None], level_set, 0.0)
+        level_set = curvature_step(level_set)
     return level_set
 
 

time: 143 us -> 69.6 us (0.49); the launches traced: 141 us -> 69.1 us
  waiting for transfers between devices: 41 us -> 12.1 us
  other arithmetic: 49 us -> 31.1 us
  between operations: 14.6 us -> 1.42 us
  starting transfers between devices: 18.7 us -> 8.75 us
  matrix products: 17.2 us -> 12.4 us
  local copies, waits for them, and re-layouts: 0.39 us -> 3.45 us
    psum x1 -> x0, waiting for transfers between devices: 37.4 us -> none  [on_device(): lax.psum(y_im.astype(jnp.bfloat16), 'focus').astype(jnp.float32)]
    convert_element_type x7 -> x10, other arithmetic: 21.6 us -> 10.8 us  [the longest x3 8.86 us: tables(): return (cos_part.astype(jnp.bfloat16), sin_part.astype(jnp.bfloat16))]
    ppermute x8 -> x7, starting transfers between devices: 18.7 us -> 8.75 us  [the longest x5 4.45 us: ring_shift(): lax.ppermute(block, axis, [(i, (i + step) % count) for i in range(count)])]
    neg x1, other arithmetic: 16.9 us -> 7.23 us  [on_device(): forward = jnp.concatenate([col_cos, -col_sin], axis=0)]
    ppermute x8 -> x7, waiting for transfers between devices: 3.53 us -> 12.1 us  [the longest x2 8.07 us: focus_sum(): other = lax.ppermute(held, 'focus', [(i, i ^ step) for i in range(count)])]
    dot_general x12 -> x4, matrix products: 5.64 us -> 1.17 us  [on_device(): lax.dot_general(kept.astype(jnp.bfloat16), spectra, (((0,), (0,)), ((), (...]
    mul x1 -> x5, other arithmetic: 0.37 us -> 2.12 us  [on_device(): kept = kept + part * jnp.concatenate([weight_row, weight_row], axis=1)]
    slice x2 -> x5, local copies, waits for them, and re-layouts: 0.03 us -> 1.62 us  [the longest x1 0.9 us: on_device(): edges = jnp.concatenate([phi[:HALO], phi[strip_rows - HALO:]], axis=0)]
  transfers between devices with their start and end apart: 9 -> 7, of which waited for: 3 -> 5; matrix products, arithmetic and copies ran while one was open for 29% -> 31% of each run, Pallas kernels for 0% -> 0%
where the time goes in v1:
time: 69.6 us; the launch traced here: 69.1 us
  other arithmetic  31.1 us (45%)
  matrix products  12.4 us (18%)
  waiting for transfers between devices  12.1 us (17%)
  starting transfers between devices  8.75 us (13%)
  local copies, waits for them, and re-layouts  3.45 us (5%)
  between operations  1.42 us (2%)
    convert_element_type x3, other arithmetic, tables(): return (cos_part.astype(jnp.bfloat16), sin_part.astype(jnp.bfloat16))  8.86 us
    ppermute x2, waiting for transfers between devices, focus_sum(): other = lax.ppermute(held, 'focus', [(i, i ^ step) for i in range(count)])  8.07 us
    neg x1, other arithmetic, on_device(): forward = jnp.concatenate([col_cos, -col_sin], axis=0)  7.23 us
    dot_general x5, matrix products, product(): return jnp.dot(lhs_mat, rhs_mat, preferred_element_type=jnp.float32)  5.7 us
    ppermute x5, starting transfers between devices, ring_shift(): lax.ppermute(block, axis, [(i, (i + step) % count) for i in range(count)])  4.45 us
    ppermute x2, starting transfers between devices, focus_sum(): other = lax.ppermute(held, 'focus', [(i, i ^ step) for i in range(count)])  4.3 us
    dot_general x3, matrix products, product_t(): lax.dot_general(lhs_mat, rhs_mat, (((1,), (1,)), ((), ())), preferred_ele...  4.09 us
    ppermute x5, waiting for transfers between devices, ring_shift(): lax.ppermute(block, axis, [(i, (i + step) % count) for i in range(count)])  4.03 us
  transfers between devices with their start and end apart: 7, of which 5 were waited for; matrix products, arithmetic and copies ran while one was open for 31% of the time, Pallas kernels for 0%

profile of v1, /device:TPU:0, one launch (start us, length us, event | category | flops | bytes accessed | tf_op | source)
XLA Modules:
  0.0 69.1 jit_solution(15105531645168974401)
XLA Ops:
  0.0 0.9 %fusion.221 = (f32[2,2048]{1,0:T(2,128)S(1)}, f32[2,2048]{1,0:T(2,128)S(1)}) fusion(f32[64,2048]{1,0:T(8,128)} %param.7), kind=kLoop, calls=%fused_computation.374 | loop fusion | bytes 65536 | tf_op jit(solution)/shard_map/slice | solution.py:106
  1.0 1.1 %tanh_convert_fusion = bf16[64,2048]{1,0:T(8,128)(2,1)S(1)} fusion(f32[64,2048]{1,0:T(8,128)} %param.7), kind=kLoop, calls=%fused_computation.87 | loop fusion | flops 131072 | bytes 786432 | tf_op jit(solution)/shard_map/convert_element_type | solution.py:105
  2.1 2.5 %collective-permute-start.1 = (bf16[72,2048]{1,0:T(8,128)(2,1)S(1)}, bf16[72,2048]{1,0:T(8,128)(2,1)S(1)}, u32[]{:S(2)}, u32[]{:S(2)}) collective-permute-start(bf16[72,2048]{1,0:T(8,128)(2,1)S(1)} %pad_maximum_fusion.13), channel_id=1, source_target_pairs={{0,12},{4,0},{8,4},{12,8},{1,13},{5,1},{9,5},{13,9},{2,14},{6,2},{... | collective-permute-start | bytes 884744 | tf_op jit(solution)/shard_map/ppermute | solution.py:20
  4.6 7.2 %fusion.34 = bf16[512,2048]{1,0:T(8,128)(2,1)S(1)} fusion(s32[512]{0:T(512)} %param.13), kind=kLoop, calls=%fused_computation.65 | loop fusion | flops 50331648 | bytes 2099200 | tf_op jit(solution)/shard_map/neg | solution.py:100
  11.8 7.8 %fusion.2 = (bf16[512,2048]{1,0:T(8,128)(2,1)}, bf16[512,2048]{1,0:T(8,128)(2,1)}) fusion(s32[512]{0:T(512)S(1)} %copy-done.22), kind=kLoop, calls=%fused_computation.8 | loop fusion | flops 50331648 | bytes 4196352 | tf_op jit(solution)/shard_map/convert_element_type | solution.py:57
  20.8 0.7 add_convert_fusion.8
  21.4 0.7 add_convert_fusion.7
  22.2 0.7 slice.151
  22.9 0.9 %fusion.175 = (bf16[48,68]{1,0:T(8,128)(2,1)S(1)}, bf16[48,68]{1,0:T(8,128)(2,1)S(1)}, bf16[48,68]{1,0:T(8,128)(2,1)}, bf16[48,68]{1,0:T(8,128)(2,1)}, bf16[48,68]{1,0:T(8,128)(2,1)}) fusion(s32[68]{0:T(128)S(1)} %get-tuple-element.55, s32[48]{0:T(128)S(1)} %copy-done.23, s32[68]{0:T(128)S(1)} %get-tuple-element.56, s32[68]{0:T(128)S(1)} %get-tuple-element.54, ...), kind=kLoop, calls=%fused_computation.325 | loop fusion | flops 701760 | bytes 34192 | tf_op jit(solution)/shard_map/neg | solution.py:189
  23.7 0.7 add_convert_fusion.5
  24.4 0.9 %fusion.117 = (bf16[48,68]{1,0:T(8,128)(2,1)}, bf16[48,68]{1,0:T(8,128)(2,1)}, bf16[48,68]{1,0:T(8,128)(2,1)}, bf16[48,68]{1,0:T(8,128)(2,1)}, bf16[48,68]{1,0:T...) fusion(s32[68]{0:T(128)S(1)} %get-tuple-element.55, ...), kind=kLoop, calls=%fused_computation.224 | loop fusion | flops 701760 | bytes 66832 | tf_op jit(solution)/shard_map/convert_element_type | solution.py:57
  25.4 0.7 %copy-done.5 = bf16[72,2048]{1,0:T(8,128)(2,1)} copy-done((bf16[72,2048]{1,0:T(8,128)(2,1)}, bf16[72,2048]{1,0:T(8,128)(2,1)S(1)}, u32[]{:S(2)}) %copy-start.5) | copy-done | bytes 294936
  26.2 1.5 %convolution_convert_fusion = bf16[192,1024]{1,0:T(8,128)(2,1)S(1)} fusion(bf16[64,2048]{1,0:T(8,128)(2,1)S(1)} %slice.206, bf16[64,2048]{1,0:T(8,128)(2,1)S(1)} %tanh_convert_fusion, bf16[64,2048]{1,0:T(8,128)(2,1)S(1)} %slice.205, bf16[512,2048]{1,0:T(8,128)(2,1)S(1)} %fusion.34, bf16[512,2048]{1,0:T(8,128)(2,1)S(1)} %copy-done.1), kind=kOutput, calls=%fused_computation.43 | convolution fusion | flops 816250880 | bytes 5373952 | tf_op jit(solution)/shard_map/dot_general | solution.py:65
  30.2 1.3 %convolution_multiply_fusion.1 = f32[256,2048]{1,0:T(8,128)S(1)} fusion(bf16[256,512]{1,0:T(8,128)(2,1)S(1)} %bitcast.66, bf16[256,512]{1,0:T(8,128)(2,1)S(1)} %bitcast.64, bf16[512,2048]{1,0:T(8,128)(2,1)S(1)} %fusion.34, bf16[512,2048]{1,0:T(8,128)(2,1)S(1)} %copy-done.1), kind=kOutput, calls=%fused_computation.28 | convolution fusion | flops 1083703296 | bytes 6815744 | tf_op jit(solution)/shard_map/dot_general | solution.py:61
  31.8 2.9 %multiply_add_fusion = (f32[256,2048]{1,0:T(8,128)}, f32[256,2048]{1,0:T(8,128)}) fusion(f32[256,2048]{1,0:T(8,128)S(1)} %convolution_multiply_fusion.1, bf16[512,2048]{1,0:T(8,128)(2,1)S(1)} %copy-done.1, bf16[512,2048]{1,0:T(8,128)(2,1)S(1)} %copy-done.3, bf16[256,512]{1,0:T(8,128)(2,1)S(1)} %bitcast.67, bf16[256,512]{1,0:T(8,128)(2,1)S(1)} %bitcast.65), kind=kOutput, calls=%fused_computation.36 | convolution fusion | flops 1085276160 | bytes 11010048 | tf_op jit(solution)/shard_map/dot_general | solution.py:61
  34.7 1.8 %reduce_sum.27 = f32[64,2048]{1,0:T(8,128)S(1)} reduce(f32[4,64,2048]{2,1,0:T(8,128)} %bitcast.61, f32[]{:T(128)} %constant.110.clone.1), dimensions={0}, to_apply=%region_0.1 | reduce | flops 393216 | bytes 2621444 | tf_op jit(solution)/shard_map/reduce_sum | solution.py:147
  36.5 1.3 %subtract_multiply_fusion = f32[64,2048]{1,0:T(8,128)S(1)} fusion(s32[64,2048]{1,0:T(8,128)} %param.8, f32[64,2048]{1,0:T(8,128)S(1)} %reduce_sum.27), kind=kLoop, calls=%fused_computation.86 | loop fusion | flops 1572864 | bytes 1572864 | tf_op jit(solution)/shard_map/mul | solution.py:150
  37.7 2.9 %fusion.17 = (bf16[256,2048]{1,0:T(8,128)(2,1)S(1)}, bf16[256,2048]{1,0:T(8,128)(2,1)S(1)}) fusion(f32[256,2048]{1,0:T(8,128)} %get-tuple-element.50, f32[64,2048]{1,0:T(8,128)S(1)} %subtract_multiply_fusion, f32[256,2048]{1,0:T(8,128)} %copy-done), kind=kLoop, calls=%fused_computation.35 | loop fusion | flops 2097152 | bytes 6815744 | tf_op jit(solution)/shard_map/convert_element_type | solution.py:158
  40.7 1.3 %fusion.218 = f32[256,1024]{1,0:T(8,128)S(1)} fusion(bf16[256,2048]{1,0:T(8,128)(2,1)S(1)} %get-tuple-element.13, bf16[512,2048]{1,0:T(8,128)(2,1)S(1)} %fusion.34, bf16[512,2048]{1,0:T(8,128)(2,1)S(1)} %copy-done.2), kind=kOutput, calls=%fused_computation.373 | convolution fusion | flops 1082130432 | bytes 6291456 | tf_op jit(solution)/shard_map/dot_general | solution.py:65
  42.3 1.3 %fusion.19 = bf16[256,1024]{1,0:T(8,128)(2,1)S(1)} fusion(f32[256,1024]{1,0:T(8,128)S(1)} %fusion.218, bf16[256,2048]{1,0:T(8,128)(2,1)S(1)} %get-tuple-element.12, bf16[512,2048]{1,0:T(8,128)(2,1)S(1)} %copy-done.2, bf16[512,2048]{1,0:T(8,128)(2,1)S(1)} %copy-done.4), kind=kOutput, calls=%fused_computation.40 | convolution fusion | flops 1082654720 | bytes 6815744 | tf_op jit(solution)/shard_map/dot_general | solution.py:65
  44.7 1.6 %collective-permute-start.2 = (bf16[96,512]{1,0:T(8,128)(2,1)S(1)}, bf16[96,512]{1,0:T(8,128)(2,1)S(1)}, u32[]{:S(2)}, u32[]{:S(2)}) collective-permute-start(bf16[96,512]{1,0:T(8,128)(2,1)S(1)} %pad_maximum_fusion.16), channel_id=1, source_target_pairs={{0,1},{1,0},{2,3},{3,2},{4,5},{5,4},{6,7},{7,6},{8,9},{9,8},{10,11... | collective-permute-start | bytes 294920 | tf_op jit(solution)/shard_map/ppermute | solution.py:29
  46.3 0.8 %slice_convert_fusion.1 = f32[8,2048]{1,0:T(8,128)S(1)} fusion(bf16[72,2048]{1,0:T(8,128)(2,1)} %copy-done.5), kind=kLoop, calls=%fused_computation.216 | loop fusion | flops 16384 | bytes 98304 | tf_op jit(solution)/shard_map/convert_element_type | solution.py:117
  47.1 3.1 %collective-permute-done.2 = bf16[96,512]{1,0:T(8,128)(2,1)S(1)} collective-permute-done((bf16[96,512]{1,0:T(8,128)(2,1)S(1)}, bf16[96,512]{1,0:T(8,128)(2,1)S(1)}, u32[]{:S(2)}, u32[]{:S(2)}) %collective-permute-start.2) | collective-permute-done | bytes 98336 | tf_op jit(solution)/shard_map/ppermute | solution.py:29
  50.2 2.7 %collective-permute-start.3 = (bf16[96,512]{1,0:T(8,128)(2,1)S(1)}, bf16[96,512]{1,0:T(8,128)(2,1)S(1)}, u32[]{:S(2)}, u32[]{:S(2)}) collective-permute-start(bf16[96,512]{1,0:T(8,128)(2,1)S(1)} %add_convert_fusion.2), channel_id=1, source_target_pairs={{0,2},{1,3},{2,0},{3,1},{4,6},{5,7},{6,4},{7,5},{8,10},{9,11},{10,... | collective-permute-start | bytes 294920 | tf_op jit(solution)/shard_map/ppermute | solution.py:29
  52.9 5.0 %collective-permute-done.3 = bf16[96,512]{1,0:T(8,128)(2,1)S(1)} collective-permute-done((bf16[96,512]{1,0:T(8,128)(2,1)S(1)}, bf16[96,512]{1,0:T(8,128)(2,1)S(1)}, u32[]{:S(2)}, u32[]{:S(2)}) %collective-permute-start.3) | collective-permute-done | bytes 98336 | tf_op jit(solution)/shard_map/ppermute | solution.py:29
  58.4 1.4 %collective-permute-start.4 = (bf16[96,512]{1,0:T(8,128)(2,1)S(1)}, bf16[96,512]{1,0:T(8,128)(2,1)S(1)}, u32[]{:S(2)}, u32[]{:S(2)}) collective-permute-start(bf16[96,512]{1,0:T(8,128)(2,1)S(1)} %add_convert_fusion.1), channel_id=1, source_target_pairs={{0,8},{4,12},{8,0},{12,4},{1,9},{5,13},{9,1},{13,5},{2,10},{6,14},... | collective-permute-start | bytes 294920 | tf_op jit(solution)/shard_map/ppermute | solution.py:20
  60.2 0.6 collective-permute-done.6
  61.1 2.2 %collective-permute-done.5 = bf16[96,512]{1,0:T(8,128)(2,1)S(1)} collective-permute-done((bf16[96,512]{1,0:T(8,128)(2,1)S(1)}, bf16[96,512]{1,0:T(8,128)(2,1)S(1)}, u32[]{:S(2)}, u32[]{:S(2)}) %collective-permute-start.5) | collective-permute-done | bytes 98336 | tf_op jit(solution)/shard_map/ppermute | solution.py:20
  63.6 1.2 %collective-permute-done.4 = bf16[96,512]{1,0:T(8,128)(2,1)S(1)} collective-permute-done((bf16[96,512]{1,0:T(8,128)(2,1)S(1)}, bf16[96,512]{1,0:T(8,128)(2,1)S(1)}, u32[]{:S(2)}, u32[]{:S(2)}) %collective-permute-start.4) | collective-permute-done | bytes 98336 | tf_op jit(solution)/shard_map/ppermute | solution.py:20
  65.2 1.0 %fusion.15 = f32[68,2048]{1,0:T(8,128)S(1)} fusion(f32[2,2048]{1,0:T(2,128)S(1)} %get-tuple-element.57, f32[64,2048]{1,0:T(8,128)S(1)} %copy-done.7, f32[2,2048]{1,0:T(2,128)S(1)} %get-tuple-element.58, pred[68]{0:T(512)(128)(4,1)S(1)} %copy-done.29, bf16[68,512]{1,0:T(8,128)(2,1)S(1)} %get-tuple-element.19, bf16[68,512]{1,0:T(8,128)(2,1)S(1)} %get-tuple-element.18, ...), kind=kOutput, calls=%fused_computation.33 | convolution fusion | flops 294993920 | bytes 5447748 | tf_op jit(solution)/shard_map/dot_general | solution.py:61
  66.2 1.2 %fusion.33 = f32[66,2048]{1,0:T(8,128)S(1)} fusion(f32[68,2048]{1,0:T(8,128)S(1)} %fusion.15, pred[66]{0:T(512)(128)(4,1)S(1)} %copy-done.27), kind=kLoop, calls=%fused_computation.62 | loop fusion | flops 3919872 | bytes 2900480 | tf_op jit(solution)/shard_map/jit(_where)/select_n | solution.py:208
  67.4 1.8 %multiply_add_fusion.1 = f32[64,2048]{1,0:T(8,128)} fusion(f32[66,2048]{1,0:T(8,128)S(1)} %fusion.33), kind=kLoop, calls=%fused_computation.85 | loop fusion | flops 3670016 | bytes 2686976 | tf_op jit(solution)/shard_map/add | solution.py:86
  (104 shorter events, 6.4 us)
Async XLA Ops:
  0.0 11.8 %copy-start.22 = (s32[512]{0:T(512)S(1)}, s32[512]{0:T(512)}, u32[]{:S(2)}) copy-start(s32[512]{0:T(512)} %param.13) | copy-start | bytes 6148
  2.1 23.2 %collective-permute-start.1 = (bf16[72,2048]{1,0:T(8,128)(2,1)S(1)}, bf16[72,2048]{1,0:T(8,128)(2,1)S(1)}, u32[]{:S(2)}, u32[]{:S(2)}) collective-permute-start(bf16[72,2048]{1,0:T(8,128)(2,1)S(1)} %pad_maximum_fusion.13), channel_id=1, source_target_pairs={{0,12},{4,0},{8,4},{12,8},{1,13},{5,1},{9,5},{13,9},{2,14},{6,2},{... | collective-permute-start | bytes 884744 | tf_op jit(solution)/shard_map/ppermute | solution.py:20
  4.6 20.8 %collective-permute-start = (bf16[72,2048]{1,0:T(8,128)(2,1)S(1)}, bf16[72,2048]{1,0:T(8,128)(2,1)S(1)}, u32[]{:S(2)}, u32[]{:S(2)}) collective-permute-start(bf16[72,2048]{1,0:T(8,128)(2,1)S(1)} %pad_maximum_fusion.13), channel_id=1, source_target_pairs={{0,4},{4,8},{8,12},{12,0},{1,5},{5,9},{9,13},{13,1},{2,6},{6,10},{... | collective-permute-start | bytes 884744 | tf_op jit(solution)/shard_map/ppermute | solution.py:20
  11.8 8.7 %copy-start.23 = (s32[48]{0:T(128)S(1)}, s32[48]{0:T(128)}, u32[]{:S(2)}) copy-start(s32[48]{0:T(128)} %param.12) | copy-start | bytes 580
  19.7 6.5 %copy-start.1 = (bf16[512,2048]{1,0:T(8,128)(2,1)S(1)}, bf16[512,2048]{1,0:T(8,128)(2,1)}, u32[]{:S(2)}) copy-start(bf16[512,2048]{1,0:T(8,128)(2,1)} %get-tuple-element.23) | copy-start | bytes 6291460
  19.7 3.2 %copy-start.28 = (pred[68]{0:T(512)(128)(4,1)}, pred[68]{0:T(512)(128)(4,1)S(1)}, u32[]{:S(2)}) copy-start(pred[68]{0:T(512)(128)(4,1)S(1)} %compare_and_fusion) | copy-start | bytes 208
  26.2 2.1 %copy-start.8 = (f32[48,512]{1,0:T(8,128)S(1)}, f32[48,512]{1,0:T(8,128)}, u32[]{:S(2)}) copy-start(f32[48,512]{1,0:T(8,128)} %param.11) | copy-start | bytes 294916
  31.5 3.2 %copy-start = (f32[256,2048]{1,0:T(8,128)}, f32[256,2048]{1,0:T(8,128)S(1)}, u32[]{:S(2)}) copy-start(f32[256,2048]{1,0:T(8,128)S(1)} %convolution_multiply_fusion.1) | copy-start | bytes 6291460
  37.7 2.9 %copy-start.2 = (bf16[512,2048]{1,0:T(8,128)(2,1)S(1)}, bf16[512,2048]{1,0:T(8,128)(2,1)}, u32[]{:S(2)}) copy-start(bf16[512,2048]{1,0:T(8,128)(2,1)} %get-tuple-element.23) | copy-start | bytes 6291460
  43.9 16.0 %copy-start.15 = (bf16[48,68]{1,0:T(8,128)(2,1)S(1)}, bf16[48,68]{1,0:T(8,128)(2,1)}, u32[]{:S(2)}) copy-start(bf16[48,68]{1,0:T(8,128)(2,1)} %get-tuple-element.45) | copy-start | bytes 19588
  43.9 16.0 %copy-start.20 = (bf16[48,68]{1,0:T(8,128)(2,1)S(1)}, bf16[48,68]{1,0:T(8,128)(2,1)}, u32[]{:S(2)}) copy-start(bf16[48,68]{1,0:T(8,128)(2,1)} %get-tuple-element.36) | copy-start | bytes 19588
  43.9 16.0 %copy-start.21 = (bf16[48,68]{1,0:T(8,128)(2,1)S(1)}, bf16[48,68]{1,0:T(8,128)(2,1)}, u32[]{:S(2)}) copy-start(bf16[48,68]{1,0:T(8,128)(2,1)} %get-tuple-element.37) | copy-start | bytes 19588
  43.9 16.0 %copy-start.26 = (f32[1,136]{1,0:T(1,128)S(1)}, f32[1,136]{1,0:T(1,128)}, u32[]{:S(2)}) copy-start(f32[1,136]{1,0:T(1,128)} %add_convert_fusion.8) | copy-start | bytes 1636
  44.2 16.6 %copy-start.14 = (bf16[48,68]{1,0:T(8,128)(2,1)S(1)}, bf16[48,68]{1,0:T(8,128)(2,1)}, u32[]{:S(2)}) copy-start(bf16[48,68]{1,0:T(8,128)(2,1)} %get-tuple-element.46) | copy-start | bytes 19588
  44.2 16.6 %copy-start.18 = (bf16[48,68]{1,0:T(8,128)(2,1)S(1)}, bf16[48,68]{1,0:T(8,128)(2,1)}, u32[]{:S(2)}) copy-start(bf16[48,68]{1,0:T(8,128)(2,1)} %get-tuple-element.38) | copy-start | bytes 19588
  44.2 16.6 %copy-start.19 = (bf16[48,68]{1,0:T(8,128)(2,1)S(1)}, bf16[48,68]{1,0:T(8,128)(2,1)}, u32[]{:S(2)}) copy-start(bf16[48,68]{1,0:T(8,128)(2,1)} %get-tuple-element.39) | copy-start | bytes 19588
  44.2 19.1 %copy-start.13 = (bf16[48,68]{1,0:T(8,128)(2,1)S(1)}, bf16[48,68]{1,0:T(8,128)(2,1)}, u32[]{:S(2)}) copy-start(bf16[48,68]{1,0:T(8,128)(2,1)} %get-tuple-element.44) | copy-start | bytes 19588
  44.2 19.1 %copy-start.16 = (bf16[48,68]{1,0:T(8,128)(2,1)S(1)}, bf16[48,68]{1,0:T(8,128)(2,1)}, u32[]{:S(2)}) copy-start(bf16[48,68]{1,0:T(8,128)(2,1)} %get-tuple-element.34) | copy-start | bytes 19588
  44.3 19.1 %copy-start.17 = (bf16[48,68]{1,0:T(8,128)(2,1)S(1)}, bf16[48,68]{1,0:T(8,128)(2,1)}, u32[]{:S(2)}) copy-start(bf16[48,68]{1,0:T(8,128)(2,1)} %get-tuple-element.35) | copy-start | bytes 19588
  44.3 19.1 %copy-start.24 = (f32[1,136]{1,0:T(1,128)S(1)}, f32[1,136]{1,0:T(1,128)}, u32[]{:S(2)}) copy-start(f32[1,136]{1,0:T(1,128)} %add_convert_fusion.7) | copy-start | bytes 1636
  44.3 20.5 %copy-start.9 = (bf16[48,68]{1,0:T(8,128)(2,1)S(1)}, bf16[48,68]{1,0:T(8,128)(2,1)}, u32[]{:S(2)}) copy-start(bf16[48,68]{1,0:T(8,128)(2,1)} %get-tuple-element.24) | copy-start | bytes 19588
  44.3 20.5 %copy-start.10 = (bf16[48,68]{1,0:T(8,128)(2,1)S(1)}, bf16[48,68]{1,0:T(8,128)(2,1)}, u32[]{:S(2)}) copy-start(bf16[48,68]{1,0:T(8,128)(2,1)} %get-tuple-element.25) | copy-start | bytes 19588
  44.3 20.5 %copy-start.11 = (bf16[48,68]{1,0:T(8,128)(2,1)S(1)}, bf16[48,68]{1,0:T(8,128)(2,1)}, u32[]{:S(2)}) copy-start(bf16[48,68]{1,0:T(8,128)(2,1)} %get-tuple-element.40) | copy-start | bytes 19588
  44.3 20.5 %copy-start.12 = (bf16[48,68]{1,0:T(8,128)(2,1)S(1)}, bf16[48,68]{1,0:T(8,128)(2,1)}, u32[]{:S(2)}) copy-start(bf16[48,68]{1,0:T(8,128)(2,1)} %get-tuple-element.41) | copy-start | bytes 19588
  44.3 20.5 %copy-start.25 = (f32[1,136]{1,0:T(1,128)S(1)}, f32[1,136]{1,0:T(1,128)}, u32[]{:S(2)}) copy-start(f32[1,136]{1,0:T(1,128)} %add_convert_fusion.5) | copy-start | bytes 1636
  44.6 20.5 %copy-start.7 = (f32[64,2048]{1,0:T(8,128)S(1)}, f32[64,2048]{1,0:T(8,128)}, u32[]{:S(2)}) copy-start(f32[64,2048]{1,0:T(8,128)} %param.7) | copy-start | bytes 1572868
  44.6 20.5 %copy-start.29 = (pred[68]{0:T(512)(128)(4,1)S(1)}, pred[68]{0:T(512)(128)(4,1)}, u32[]{:S(2)}) copy-start(pred[68]{0:T(512)(128)(4,1)} %copy-done.28) | copy-start | bytes 208
  44.7 5.5 %collective-permute-start.2 = (bf16[96,512]{1,0:T(8,128)(2,1)S(1)}, bf16[96,512]{1,0:T(8,128)(2,1)S(1)}, u32[]{:S(2)}, u32[]{:S(2)}) collective-permute-start(bf16[96,512]{1,0:T(8,128)(2,1)S(1)} %pad_maximum_fusion.16), channel_id=1, source_target_pairs={{0,1},{1,0},{2,3},{3,2},{4,5},{5,4},{6,7},{7,6},{8,9},{9,8},{10,11... | collective-permute-start | bytes 294920 | tf_op jit(solution)/shard_map/ppermute | solution.py:29
  50.2 7.7 %collective-permute-start.3 = (bf16[96,512]{1,0:T(8,128)(2,1)S(1)}, bf16[96,512]{1,0:T(8,128)(2,1)S(1)}, u32[]{:S(2)}, u32[]{:S(2)}) collective-permute-start(bf16[96,512]{1,0:T(8,128)(2,1)S(1)} %add_convert_fusion.2), channel_id=1, source_target_pairs={{0,2},{1,3},{2,0},{3,1},{4,6},{5,7},{6,4},{7,5},{8,10},{9,11},{10,... | collective-permute-start | bytes 294920 | tf_op jit(solution)/shard_map/ppermute | solution.py:29
  57.9 2.9 %collective-permute-start.6 = (bf16[96,512]{1,0:T(8,128)(2,1)S(1)}, bf16[96,512]{1,0:T(8,128)(2,1)S(1)}, u32[]{:S(2)}, u32[]{:S(2)}) collective-permute-start(bf16[96,512]{1,0:T(8,128)(2,1)S(1)} %add_convert_fusion.1), channel_id=1, source_target_pairs={{0,12},{4,0},{8,4},{12,8},{1,13},{5,1},{9,5},{13,9},{2,14},{6,2},{... | collective-permute-start | bytes 294920 | tf_op jit(solution)/shard_map/ppermute | solution.py:20
  58.2 5.1 %collective-permute-start.5 = (bf16[96,512]{1,0:T(8,128)(2,1)S(1)}, bf16[96,512]{1,0:T(8,128)(2,1)S(1)}, u32[]{:S(2)}, u32[]{:S(2)}) collective-permute-start(bf16[96,512]{1,0:T(8,128)(2,1)S(1)} %add_convert_fusion.1), channel_id=1, source_target_pairs={{0,4},{4,8},{8,12},{12,0},{1,5},{5,9},{9,13},{13,1},{2,6},{6,10},{... | collective-permute-start | bytes 294920 | tf_op jit(solution)/shard_map/ppermute | solution.py:20
  58.4 6.4 %collective-permute-start.4 = (bf16[96,512]{1,0:T(8,128)(2,1)S(1)}, bf16[96,512]{1,0:T(8,128)(2,1)S(1)}, u32[]{:S(2)}, u32[]{:S(2)}) collective-permute-start(bf16[96,512]{1,0:T(8,128)(2,1)S(1)} %add_convert_fusion.1), channel_id=1, source_target_pairs={{0,8},{4,12},{8,0},{12,4},{1,9},{5,13},{9,1},{13,5},{2,10},{6,14},... | collective-permute-start | bytes 294920 | tf_op jit(solution)/shard_map/ppermute | solution.py:20
  (5 other events, 6.1 us)

commit v2 on v1

v2 whole, which is shorter than its diff:
```python
import functools

import jax
import jax.numpy as jnp
from jax import lax
from jax.experimental import pallas as pl
from jax.experimental.pallas import tpu as pltpu
from jax.sharding import PartitionSpec as P

MARGIN = 64
LEVELS = 31
SWEEPS = 2
HALO = SWEEPS
LANES = 128
PAD = 8
CHUNK = 256

slope_resist = 4.0
level_resist = 0.5
step_size = 1.0
flow_rate = 0.2

SIN_TERMS = (1.0, -1.0 / 6, 1.0 / 120, -1.0 / 5040, 1.0 / 362880, -1.0 / 39916800)
COS_TERMS = (1.0, -0.5, 1.0 / 24, -1.0 / 720, 1.0 / 40320, -1.0 / 3628800, 1.0 / 479001600)


def cos_sin(angle):
    half = 0.5 * angle
    square = half * half
    s = jnp.full_like(half, SIN_TERMS[-1])
    for term in SIN_TERMS[-2::-1]:
        s = s * square + term
    s = s * half
    c = jnp.full_like(half, COS_TERMS[-1])
    for term in COS_TERMS[-2::-1]:
        c = c * square + term
    return 1.0 - 2.0 * s * s, 2.0 * s * c


def turn(product, period):
    rest = product - jnp.round(product * (1.0 / period)) * period
    return cos_sin(rest * (2.0 * jnp.pi / period))


def mirrored(block):
    spots = (LANES - 1) - lax.broadcasted_iota(jnp.int32, block.shape, 1)
    return jnp.take_along_axis(block, spots, axis=1, mode="promise_in_bounds")


def dot(lhs_mat, rhs_mat):
    return jnp.dot(lhs_mat, rhs_mat, preferred_element_type=jnp.float32)


def dot_t(lhs_mat, rhs_mat):
    return lax.dot_general(
        lhs_mat, rhs_mat, (((1,), (1,)), ((), ())), preferred_element_type=jnp.float32
    )


def packet_kernel(phi_ref, out_ref):
    rows, cols = phi_ref.shape
    half = cols // 2
    for b in range(half // LANES):
        left = jnp.tanh(phi_ref[:, b * LANES : (b + 1) * LANES])
        right = mirrored(jnp.tanh(phi_ref[:, cols - (b + 1) * LANES : cols - b * LANES]))
        out_ref[:rows, b * LANES : (b + 1) * LANES] = (left + right).astype(jnp.bfloat16)
        out_ref[:rows, half + b * LANES : half + (b + 1) * LANES] = (left - right).astype(
            jnp.bfloat16
        )
    first = phi_ref[:HALO]
    last = phi_ref[rows - HALO :]
    first_high = first.astype(jnp.bfloat16).astype(jnp.float32)
    last_high = last.astype(jnp.bfloat16).astype(jnp.float32)
    filler = jnp.zeros((2 * PAD - 4 * HALO, cols), jnp.float32)
    edges = jnp.concatenate(
        [first_high, first - first_high, last_high, last - last_high, filler], axis=0
    )
    out_ref[rows:] = edges.astype(jnp.bfloat16)


def offset_groups(rows, strips):
    reach = (MARGIN + HALO + rows - 1) // rows
    groups = {}
    for offset in range(-reach, reach + 1):
        groups.setdefault(offset % strips, []).append(offset)
    return groups


def tables_kernel(
    rows,
    strips,
    groups,
    defocus_ref,
    row_freqs_ref,
    col_freqs_ref,
    kernels_ref,
    psi_ref,
    cos_ref,
    sin_ref,
    window_ref,
    inner_ref,
    inner_t_ref,
    tall_ref,
    k_re_ref,
    k_im_ref,
    freq_lanes,
):
    place = lax.axis_index("strip")
    fr = psi_ref.shape[0]
    fc, half = cos_ref.shape
    cols = 2 * half
    window = rows + 2 * MARGIN

    freqs = jnp.broadcast_to(col_freqs_ref[...].astype(jnp.float32), (8, fc)).T[:, :1]
    lane = lax.broadcasted_iota(jnp.int32, (fc, LANES), 1).astype(jnp.float32)
    c, s = turn(freqs * (2.0 * lane + 1.0), 2.0 * cols)
    step_c, step_s = turn(freqs * float(LANES), float(cols))
    step_c = jnp.broadcast_to(step_c, (fc, LANES))
    step_s = jnp.broadcast_to(step_s, (fc, LANES))
    for b in range(half // LANES):
        if b:
            c, s = c * step_c - s * step_s, s * step_c + c * step_s
        cos_ref[:, b * LANES : (b + 1) * LANES] = c.astype(jnp.bfloat16)
        sin_ref[:, b * LANES : (b + 1) * LANES] = s.astype(jnp.bfloat16)

    freq_lanes[...] = jnp.zeros_like(freq_lanes)
    freq_lanes[0:1, 0:fr] = row_freqs_ref[...].astype(jnp.float32)
    freq_lanes[0:1, fr : 2 * fr] = row_freqs_ref[...].astype(jnp.float32)
    across = freq_lanes[0:1, :]
    down = jnp.broadcast_to(across, (8, LANES)).T[: 2 * fr, :1]

    def rotation(length, first, down_first):
        shape = (2 * fr, 2 * length) if down_first else (2 * length, LANES)
        freq_dim, spot_dim = (0, 1) if down_first else (1, 0)
        spot = lax.broadcasted_iota(jnp.int32, shape, spot_dim)
        second = spot >= length
        spot = jnp.where(second, spot - length, spot) + first
        imag = lax.broadcasted_iota(jnp.int32, shape, freq_dim) >= fr
        c, s = turn((down if down_first else across) * spot.astype(jnp.float32), float(window))
        plain = second == imag
        return jnp.where(plain, c, jnp.where(second, s, -s)), spot

    table, spot = rotation(window, 0, True)
    keep = ((spot >= MARGIN) | (place > 0)) & ((spot < MARGIN + rows) | (place < strips - 1))
    window_ref[...] = jnp.where(keep, table, 0.0).astype(jnp.bfloat16)
    inner_ref[...] = rotation(rows, MARGIN, True)[0].astype(jnp.bfloat16)
    inner_t_ref[...] = rotation(rows, MARGIN, False)[0][:, : 2 * fr].astype(jnp.bfloat16)
    for index, offsets in enumerate(groups.values()):
        total = 0.0
        for offset in offsets:
            table, spot = rotation(rows + 2 * PAD, MARGIN - PAD - offset * rows, False)
            keep = (spot >= 0) & (spot < window)
            keep = keep & (place + offset >= 0) & (place + offset < strips)
            total = total + jnp.where(keep, table, 0.0)
        tall_ref[index] = total[:, : 2 * fr].astype(jnp.bfloat16)

    middle = (LEVELS - 1) / 2.0
    defocus = (defocus_ref[0].astype(jnp.float32) - middle) * (1.0 / middle)
    turn_c, turn_s = cos_sin(psi_ref[...] * defocus)
    for k in range(kernels_ref.shape[1]):
        k_re_ref[k] = kernels_ref[0, k] * turn_c - kernels_ref[1, k] * turn_s
        k_im_ref[k] = kernels_ref[0, k] * turn_s + kernels_ref[1, k] * turn_c


def main_kernel(
    own_ref,
    above_ref,
    below_ref,
    target_ref,
    cos_ref,
    sin_ref,
    window_ref,
    inner_ref,
    inner_t_ref,
    k_re_ref,
    k_im_ref,
    out_ref,
    q_ref,
    u_ref,
):
    rows, cols = target_ref.shape
    half = cols // 2
    count, fr, fc = k_re_ref.shape
    scale = 1.0 / float((rows + 2 * MARGIN) * cols) ** 0.5
    bf = jnp.bfloat16

    mask = jnp.concatenate(
        [above_ref[rows - MARGIN : rows], own_ref[:rows], below_ref[:MARGIN]], axis=0
    )
    p_re = dot_t(mask[:, :half], cos_ref[...])
    p_im = -dot_t(mask[:, half:], sin_ref[...])
    p = jnp.concatenate([p_re, p_im], axis=0).astype(bf)
    spec = scale * dot(window_ref[...], p)
    s_re, s_im = spec[:fr], spec[fr:]
    for k in range(count):
        k_re, k_im = k_re_ref[k], k_im_ref[k]
        g = jnp.concatenate([k_re * s_re - k_im * s_im, k_re * s_im + k_im * s_re], axis=0)
        q_ref[k * 2 * rows : (k + 1) * 2 * rows] = dot(inner_t_ref[...], g.astype(bf)).astype(bf)

    u_ref[...] = jnp.zeros_like(u_ref)
    gain = 4.0 * slope_resist / count * scale
    width = min(CHUNK, half)
    for start in range(0, half, width):
        cos_part = cos_ref[:, start : start + width]
        sin_part = sin_ref[:, start : start + width]
        af = dot(q_ref[...], cos_part)
        db = dot(q_ref[...], sin_part)
        even = 0.0
        cross = 0.0
        for k in range(count):
            a = af[2 * k * rows : (2 * k + 1) * rows]
            f = af[(2 * k + 1) * rows : (2 * k + 2) * rows]
            d = db[2 * k * rows : (2 * k + 1) * rows]
            b = db[(2 * k + 1) * rows : (2 * k + 2) * rows]
            even = even + ((a * a + f * f) + (d * d + b * b))
            cross = cross + (a * b - d * f)
        norm = scale * scale / count

        def weight(intensity, goal):
            resist = jax.nn.sigmoid(slope_resist * (norm * intensity - level_resist))
            return gain * (resist - goal) * resist * (1.0 - resist)

        goal_left = target_ref[:, start : start + width].astype(jnp.float32)
        goal_right = jnp.concatenate(
            [
                mirrored(
                    target_ref[:, cols - x - LANES : cols - x].astype(jnp.float32)
                )
                for x in range(start, start + width, LANES)
            ],
            axis=1,
        )
        w_left = weight(even - 2.0 * cross, goal_left)
        w_right = weight(even + 2.0 * cross, goal_right)
        p_w = w_left + w_right
        q_w = w_right - w_left
        x_cos = []
        x_sin = []
        for k in range(count):
            a = af[2 * k * rows : (2 * k + 1) * rows]
            f = af[(2 * k + 1) * rows : (2 * k + 2) * rows]
            d = db[2 * k * rows : (2 * k + 1) * rows]
            b = db[(2 * k + 1) * rows : (2 * k + 2) * rows]
            x_cos += [(p_w * a + q_w * b).astype(bf), (p_w * f - q_w * d).astype(bf)]
            x_sin += [(p_w * d - q_w * f).astype(bf), (q_w * a + p_w * b).astype(bf)]
        u_ref[...] += dot_t(jnp.concatenate(x_cos, axis=0), cos_part) + dot_t(
            jnp.concatenate(x_sin, axis=0), sin_part
        )

    y_re = 0.0
    y_im = 0.0
    for k in range(count):
        u = u_ref[k * 2 * rows : (k + 1) * 2 * rows].astype(bf)
        w = scale * dot(inner_ref[...], u)
        w_re, w_im = w[:fr], w[fr:]
        k_re, k_im = k_re_ref[k], k_im_ref[k]
        y_re = y_re + (k_re * w_re + k_im * w_im)
        y_im = y_im + (k_re * w_im - k_im * w_re)
    out_ref[:fr] = y_re.astype(bf)
    out_ref[fr:] = y_im.astype(bf)


def final_kernel(
    strips,
    count,
    phi_ref,
    above_ref,
    below_ref,
    cos_ref,
    sin_ref,
    tall_ref,
    *rest,
):
    spectra, (out_ref, level_ref, next_ref) = rest[:count], rest[count:]
    place = lax.axis_index("strip")
    rows, cols = phi_ref.shape
    half = cols // 2
    tall = rows + 2 * PAD
    bf = jnp.bfloat16
    scale = 1.0 / float((rows + 2 * MARGIN) * cols) ** 0.5

    z = 0.0
    for index in range(count):
        z = z + dot(tall_ref[index], spectra[index][...])
    z = z.astype(bf)
    even = dot(z[:tall], cos_ref[...])
    odd = dot(z[tall:], sin_ref[...])

    above = above_ref[rows:].astype(jnp.float32)
    below = below_ref[rows:].astype(jnp.float32)
    level_ref[:PAD] = jnp.zeros((PAD, cols), jnp.float32)
    level_ref[tall - PAD :] = jnp.zeros((PAD, cols), jnp.float32)
    level_ref[PAD - HALO : PAD] = above[2 * HALO : 3 * HALO] + above[3 * HALO : 4 * HALO]
    level_ref[PAD : PAD + rows] = phi_ref[...]
    level_ref[PAD + rows : PAD + rows + HALO] = below[:HALO] + below[HALO : 2 * HALO]
    down = lax.broadcasted_iota(jnp.int32, (tall, LANES), 0)
    inside = ((down >= PAD) | (place > 0)) & ((down < PAD + rows) | (place < strips - 1))

    def advance(start, grad):
        phi = level_ref[:, start : start + LANES]
        mask = jnp.tanh(phi)
        stepped = phi - step_size * (1.0 - mask * mask) * (scale * grad)
        level_ref[:, start : start + LANES] = jnp.where(inside, stepped, 0.0)

    for b in range(half // LANES):
        part = slice(b * LANES, (b + 1) * LANES)
        advance(b * LANES, even[:, part] - odd[:, part])
        advance(cols - (b + 1) * LANES, mirrored(even[:, part] + odd[:, part]))

    def sweep(source, first, number):
        center = source[first : first + number]
        upper = source[first + 1 : first + 1 + number]
        lower = source[first - 1 : first - 1 + number]
        lane = lax.broadcasted_iota(jnp.int32, (number, cols), 1)

        def beside(values):
            right = jnp.where(lane < cols - 1, pltpu.roll(values, cols - 1, 1), 0.0)
            left = jnp.where(lane > 0, pltpu.roll(values, 1, 1), 0.0)
            return right, left

        right, left = beside(center)
        slope = upper - lower
        slope_right, slope_left = beside(slope)
        grad_x = 0.5 * slope
        grad_y = 0.5 * (right - left)
        second_x = upper - 2.0 * center + lower
        second_y = right - 2.0 * center + left
        crossed = 0.25 * (slope_right - slope_left)
        flow = (
            second_x * grad_y * grad_y
            - 2.0 * grad_x * grad_y * crossed
            + second_y * grad_x * grad_x
        ) / (1.0 + grad_x * grad_x + grad_y * grad_y)
        return center + flow_rate * flow

    top_inside = place > 0
    low_inside = place < strips - 1
    for block in range(PAD - 1, PAD + rows + 1, 8):
        number = min(8, PAD + rows + 1 - block)
        swept = sweep(level_ref, block, number)
        spot = lax.broadcasted_iota(jnp.int32, (number, cols), 0) + block
        keep = ((spot >= PAD) | top_inside) & ((spot < PAD + rows) | low_inside)
        next_ref[block : block + number] = jnp.where(keep, swept, 0.0)
    for block in range(0, rows, 8):
        out_ref[block : block + 8] = sweep(next_ref, PAD + block, 8)


def vmem(count):
    return [pl.BlockSpec(memory_space=pltpu.VMEM)] * count


def call(kernel, out_shape, args, scratch=(), scalars=0, limit=24, flops=1000000):
    outs = out_shape if isinstance(out_shape, list) else [out_shape]
    single = not isinstance(out_shape, list)
    return pl.pallas_call(
        kernel,
        out_shape=out_shape,
        in_specs=[pl.BlockSpec(memory_space=pltpu.SMEM)] * scalars + vmem(len(args) - scalars),
        out_specs=vmem(1)[0] if single else vmem(len(outs)),
        scratch_shapes=list(scratch),
        compiler_params=pltpu.CompilerParams(vmem_limit_bytes=limit << 20),
        cost_estimate=pl.CostEstimate(flops=flops, bytes_accessed=4 << 20, transcendentals=0),
    )(*args)


def ring_shift(block, axis, step):
    count = lax.axis_size(axis)
    return lax.ppermute(block, axis, [(i, (i + step) % count) for i in range(count)])


def focus_sum(part):
    count = lax.axis_size("focus")
    step = 1
    while step < count:
        other = lax.ppermute(part, "focus", [(i, i ^ step) for i in range(count)])
        part = lax.optimization_barrier(
            (part.astype(jnp.float32) + other.astype(jnp.float32)).astype(jnp.bfloat16)
        )
        step *= 2
    return part


def on_device(phi, target, defocus_ids, kernels, psi, row_freqs, col_freqs):
    rows, cols = phi.shape
    half = cols // 2
    fr, fc = psi.shape
    count = kernels.shape[1]
    strips = lax.axis_size("strip")
    groups = offset_groups(rows, strips)
    tall = rows + 2 * PAD
    window = rows + 2 * MARGIN
    bf = jnp.bfloat16
    f32 = jnp.float32
    shape = jax.ShapeDtypeStruct

    packet = call(packet_kernel, shape((rows + 2 * PAD, cols), bf), (phi,))
    above = ring_shift(packet, "strip", 1)
    below = ring_shift(packet, "strip", -1)
    cos_t, sin_t, window_t, inner, inner_t, tall_t, k_re, k_im = call(
        functools.partial(tables_kernel, rows, strips, groups),
        [
            shape((fc, half), bf),
            shape((fc, half), bf),
            shape((2 * fr, 2 * window), bf),
            shape((2 * fr, 2 * rows), bf),
            shape((2 * rows, 2 * fr), bf),
            shape((len(groups), 2 * tall, 2 * fr), bf),
            shape((count, fr, fc), f32),
            shape((count, fr, fc), f32),
        ],
        (defocus_ids, row_freqs.reshape(1, fr), col_freqs.reshape(1, fc), kernels, psi),
        scratch=[pltpu.VMEM((8, LANES), f32)],
        scalars=1,
        flops=4000000000,
    )
    spectrum = call(
        main_kernel,
        shape((2 * fr, fc), bf),
        (packet, above, below, target, cos_t, sin_t, window_t, inner, inner_t, k_re, k_im),
        scratch=[
            pltpu.VMEM((count * 2 * rows, fc), bf),
            pltpu.VMEM((count * 2 * rows, fc), f32),
        ],
        limit=40,
        flops=4000000000,
    )
    own = focus_sum(spectrum)
    spectra = [own if turn_by == 0 else ring_shift(own, "strip", -turn_by) for turn_by in groups]
    return call(
        functools.partial(final_kernel, strips, len(spectra)),
        shape((rows, cols), f32),
        (phi, above, below, cos_t, sin_t, tall_t, *spectra),
        scratch=[pltpu.VMEM((tall, cols), f32), pltpu.VMEM((tall, cols), f32)],
        limit=24,
    )


def solution(mesh):
    return jax.shard_map(
        on_device,
        mesh=mesh,
        in_specs=(
            P(("tile", "strip"), None),
            P(("tile", "strip"), None),
            P(("tile", "focus")),
            P(),
            P(),
            P(),
            P(),
        ),
        out_specs=P(("tile", "strip"), None),
        check_vma=False,
    )
```

time: 69.6 us -> 39.9 us (0.57)
  other arithmetic: 31.1 us -> 0.05 us
  matrix products: 12.4 us -> 0 us
  Pallas kernels: 0 us -> 10.8 us
  waiting for transfers between devices: 12.1 us -> 15.3 us
  starting transfers between devices: 8.75 us -> 10.1 us
  local copies, waits for them, and re-layouts: 3.45 us -> 2.61 us
    convert_element_type x11 -> x2, other arithmetic: 13.7 us -> 0.05 us  [focus_sum(): (part.astype(jnp.float32) + other.astype(jnp.float32)).astype(jnp.bfloat16)]
    dot_general x16 -> x0, matrix products: 12.4 us -> none  [the longest x5 5.7 us: product(): return jnp.dot(lhs_mat, rhs_mat, preferred_element_type=jnp.float32)]
    pallas_call x0 -> x4, Pallas kernels: none -> 10.8 us  [call(): pl.pallas_call(kernel, out_shape=out_shape, in_specs=[pl.BlockSpec(memory...]
    neg x2 -> x0, other arithmetic: 8.12 us -> none  [the longest x1 7.23 us: on_device(): forward = jnp.concatenate([col_cos, -col_sin], axis=0)]
    mul x6 -> x0, other arithmetic: 3.39 us -> none  [the longest x5 2.12 us: on_device(): kept = kept + part * jnp.concatenate([weight_row, weight_row], axis=1)]
    ppermute x5, waiting for transfers between devices: 4.03 us -> 6.5 us  [ring_shift(): lax.ppermute(block, axis, [(i, (i + step) % count) for i in range(count)])]
    reduce_sum x2 -> x0, other arithmetic: 2.05 us -> none  [the longest x1 1.76 us: on_device(): intensity = jnp.mean(e_re * e_re + e_im * e_im, axis=0)]
    add x4 -> x0, other arithmetic: 1.8 us -> none  [the longest x1 1.77 us: curvature_step(): return center + flow_rate * flow_term]
  transfers between devices with their start and end apart: 7 -> 7, of which waited for: 5 -> 6; matrix products, arithmetic and copies ran while one was open for 31% -> 0% of each run, Pallas kernels for 0% -> 6%
where the time goes in v2:
time: 39.9 us; the launch traced here: 39.6 us
  waiting for transfers between devices  15.3 us (38%)
  Pallas kernels  10.8 us (27%)
  starting transfers between devices  10.1 us (25%)
  local copies, waits for them, and re-layouts  2.61 us (7%)
  between operations  0.73 us (2%)
    pallas_call x4, Pallas kernels, call(): pl.pallas_call(kernel, out_shape=out_shape, in_specs=[pl.BlockSpec(memory...  10.8 us
    ppermute x2, waiting for transfers between devices, focus_sum(): other = lax.ppermute(part, 'focus', [(i, i ^ step) for i in range(count)])  8.79 us
    ppermute x5, waiting for transfers between devices, ring_shift(): lax.ppermute(block, axis, [(i, (i + step) % count) for i in range(count)])  6.5 us
    ppermute x5, starting transfers between devices, ring_shift(): lax.ppermute(block, axis, [(i, (i + step) % count) for i in range(count)])  5.68 us
    ppermute x2, starting transfers between devices, focus_sum(): other = lax.ppermute(part, 'focus', [(i, i ^ step) for i in range(count)])  4.47 us
    unnamed x14, local copies, waits for them, and re-layouts  2.61 us
  transfers between devices with their start and end apart: 7, of which 6 were waited for; matrix products, arithmetic and copies ran while one was open for 0% of the time, Pallas kernels for 6%

profile of v2, /device:TPU:0, one launch (start us, length us, event | category | flops | bytes accessed | tf_op | source)
XLA Modules:
  0.0 39.6 jit_solution(4727430154073360884)
XLA Ops:
  0.0 0.0 copy-start
  0.0 1.0 %copy-done = f32[64,2048]{1,0:T(8,128)S(1)} copy-done((f32[64,2048]{1,0:T(8,128)S(1)}, f32[64,2048]{1,0:T(8,128)}, u32[]{:S(2)}) %copy-start) | copy-done | bytes 524312
  1.0 0.0 copy-start.2
  1.0 0.1 shard_map.73.own_ref
  1.2 0.5 %collective-permute-start = (bf16[80,2048]{1,0:T(8,128)(2,1)S(1)}, bf16[80,2048]{1,0:T(8,128)(2,1)S(1)}, u32[]{:S(2)}, u32[]{:S(2)}) collective-permute-start(bf16[80,2048]{1,0:T(8,128)(2,1)S(1)} %shard_map.73.own_ref), channel_id=1, source_target_pairs={{0,4},{4,8},{8,12},{12,0},{1,5},{5,9},{9,13},{13,1},{2,6},{6,10},{... | collective-permute-start | bytes 983048 | tf_op jit(solution)/shard_map/ppermute | solution.py:368
  1.7 2.0 %collective-permute-start.1 = (bf16[80,2048]{1,0:T(8,128)(2,1)S(1)}, bf16[80,2048]{1,0:T(8,128)(2,1)S(1)}, u32[]{:S(2)}, u32[]{:S(2)}) collective-permute-start(bf16[80,2048]{1,0:T(8,128)(2,1)S(1)} %shard_map.73.own_ref), channel_id=1, source_target_pairs={{0,12},{4,0},{8,4},{12,8},{1,13},{5,1},{9,5},{13,9},{2,14},{6,2},{... | collective-permute-start | bytes 983048 | tf_op jit(solution)/shard_map/ppermute | solution.py:368
  4.4 0.0 copy-start.5
  4.4 0.0 copy-start.6
  4.4 0.0 copy-done.2
  4.4 0.7 %copy-done.5 = s32[512]{0:T(512)S(1)} copy-done((s32[512]{0:T(512)S(1)}, s32[512]{0:T(512)}, u32[]{:S(2)}) %copy-start.5) | copy-done | bytes 2072
  5.1 0.0 copy-done.6
  5.1 0.0 copy-start.4
  5.1 0.9 %copy-done.4 = f32[48,512]{1,0:T(8,128)S(1)} copy-done((f32[48,512]{1,0:T(8,128)S(1)}, f32[48,512]{1,0:T(8,128)}, u32[]{:S(2)}) %copy-start.4) | copy-done | bytes 98328
  6.0 0.0 copy-start.3
  6.0 2.2 %shard_map.74 = (bf16[512,1024]{1,0:T(8,128)(2,1)S(1)}, bf16[512,1024]{1,0:T(8,128)(2,1)S(1)}, bf16[96,384]{1,0:T(8,128)(2,1)S(1)}, bf16[96,128]{1,0:T(8,128)(2,...) custom-call(s32[1]{0:T(128)S(6)} %copy.8.defocus_ref, ...), custom_call_target="tpu_custom_call" | custom-call | flops 4000000000 | bytes 4194304 | tf_op jit(solution)/shard_map/pallas_call | solution.py:355
  8.2 1.1 %collective-permute-done.above_ref = bf16[80,2048]{1,0:T(8,128)(2,1)S(1)} collective-permute-done((bf16[80,2048]{1,0:T(8,128)(2,1)S(1)}, bf16[80,2048]{1,0:T(8,128)(2,1)S(1)}, u32[]{:S(2)}, u32[]{:S(2)}) %collective-permute-start) | collective-permute-done | bytes 327712 | tf_op jit(solution)/shard_map/ppermute | solution.py:368
  9.3 2.4 %collective-permute-done.1.below_ref = bf16[80,2048]{1,0:T(8,128)(2,1)S(1)} collective-permute-done((bf16[80,2048]{1,0:T(8,128)(2,1)S(1)}, bf16[80,2048]{1,0:T(8,128)(2,1)S(1)}, u32[]{:S(2)}, u32[]{:S(2)}) %collective-permute-start.1) | collective-permute-done | bytes 327712 | tf_op jit(solution)/shard_map/ppermute | solution.py:368
  11.8 0.0 copy-done.3
  11.8 4.6 %shard_map.75 = bf16[96,512]{1,0:T(8,128)(2,1)S(1)} custom-call(bf16[80,2048]{1,0:T(8,128)(2,1)S(1)} %shard_map.73.own_ref, bf16[80,2048]{1,0:T(8,128)(2,1)S(1)} %collective-permute-done.above_ref, bf16[80,2048]{1,0:T(8,128)(2,1)S(1)} %collective-permute-done.1.below_ref, s32[64,2048]{1,0:T(8,128)S(1)} %copy-done.3, ...), custom_call_target="tpu_custom_call" | custom-call | flops 4000000000 | bytes 4194304 | tf_op jit(solution)/shard_map/pallas_call | solution.py:355
  16.4 0.0 copy-start.1
  16.4 1.7 %collective-permute-start.2 = (bf16[96,512]{1,0:T(8,128)(2,1)S(1)}, bf16[96,512]{1,0:T(8,128)(2,1)S(1)}, u32[]{:S(2)}, u32[]{:S(2)}) collective-permute-start(bf16[96,512]{1,0:T(8,128)(2,1)S(1)} %shard_map.75), channel_id=1, source_target_pairs={{0,1},{1,0},{2,3},{3,2},{4,5},{5,4},{6,7},{7,6},{8,9},{9,8},{10,11... | collective-permute-start | bytes 294920 | tf_op jit(solution)/shard_map/ppermute | solution.py:375
  18.0 3.8 %collective-permute-done.2 = bf16[96,512]{1,0:T(8,128)(2,1)S(1)} collective-permute-done((bf16[96,512]{1,0:T(8,128)(2,1)S(1)}, bf16[96,512]{1,0:T(8,128)(2,1)S(1)}, u32[]{:S(2)}, u32[]{:S(2)}) %collective-permute-start.2) | collective-permute-done | bytes 98336 | tf_op jit(solution)/shard_map/ppermute | solution.py:375
  21.8 2.8 %collective-permute-start.3 = (bf16[96,512]{1,0:T(8,128)(2,1)S(1)}, bf16[96,512]{1,0:T(8,128)(2,1)S(1)}, u32[]{:S(2)}, u32[]{:S(2)}) collective-permute-start(bf16[96,512]{1,0:T(8,128)(2,1)S(1)} %add_convert_fusion.1), channel_id=1, source_target_pairs={{0,2},{1,3},{2,0},{3,1},{4,6},{5,7},{6,4},{7,5},{8,10},{9,11},{10,... | collective-permute-start | bytes 294920 | tf_op jit(solution)/shard_map/ppermute | solution.py:375
  24.6 5.0 %collective-permute-done.3 = bf16[96,512]{1,0:T(8,128)(2,1)S(1)} collective-permute-done((bf16[96,512]{1,0:T(8,128)(2,1)S(1)}, bf16[96,512]{1,0:T(8,128)(2,1)S(1)}, u32[]{:S(2)}, u32[]{:S(2)}) %collective-permute-start.3) | collective-permute-done | bytes 98336 | tf_op jit(solution)/shard_map/ppermute | solution.py:375
  29.7 1.4 %collective-permute-start.4 = (bf16[96,512]{1,0:T(8,128)(2,1)S(1)}, bf16[96,512]{1,0:T(8,128)(2,1)S(1)}, u32[]{:S(2)}, u32[]{:S(2)}) collective-permute-start(bf16[96,512]{1,0:T(8,128)(2,1)S(1)} %add_convert_fusion.rest_2_), channel_id=1, source_target_pairs={{0,8},{4,12},{8,0},{12,4},{1,9},{5,13},{9,1},{13,5},{2,10},{6,14},... | collective-permute-start | bytes 294920 | tf_op jit(solution)/shard_map/ppermute | solution.py:368
  31.1 0.0 collective-permute-start.5
  31.1 1.7 %collective-permute-start.6 = (bf16[96,512]{1,0:T(8,128)(2,1)S(1)}, bf16[96,512]{1,0:T(8,128)(2,1)S(1)}, u32[]{:S(2)}, u32[]{:S(2)}) collective-permute-start(bf16[96,512]{1,0:T(8,128)(2,1)S(1)} %add_convert_fusion.rest_2_), channel_id=1, source_target_pairs={{0,12},{4,0},{8,4},{12,8},{1,13},{5,1},{9,5},{13,9},{2,14},{6,2},{... | collective-permute-start | bytes 294920 | tf_op jit(solution)/shard_map/ppermute | solution.py:368
  32.9 1.8 %collective-permute-done.4.rest_0_ = bf16[96,512]{1,0:T(8,128)(2,1)S(1)} collective-permute-done((bf16[96,512]{1,0:T(8,128)(2,1)S(1)}, bf16[96,512]{1,0:T(8,128)(2,1)S(1)}, u32[]{:S(2)}, u32[]{:S(2)}) %collective-permute-start.4) | collective-permute-done | bytes 98336 | tf_op jit(solution)/shard_map/ppermute | solution.py:368
  34.7 1.1 %collective-permute-done.5.rest_1_ = bf16[96,512]{1,0:T(8,128)(2,1)S(1)} collective-permute-done((bf16[96,512]{1,0:T(8,128)(2,1)S(1)}, bf16[96,512]{1,0:T(8,128)(2,1)S(1)}, u32[]{:S(2)}, u32[]{:S(2)}) %collective-permute-start.5) | collective-permute-done | bytes 98336 | tf_op jit(solution)/shard_map/ppermute | solution.py:368
  35.8 0.0 collective-permute-done.6.rest_3_
  35.8 0.0 copy-done.1
  35.8 3.9 %shard_map.76 = f32[64,2048]{1,0:T(8,128)} custom-call(f32[64,2048]{1,0:T(8,128)S(1)} %copy-done.1, bf16[80,2048]{1,0:T(8,128)(2,1)S(1)} %collective-permute-done.above_ref, bf16[80,2048]{1,0:T(8,128)(2,1)S(1)} %collective-permute-done.1.below_ref, bf16[512,1024]{1,0:T(8,128)(2,1)S(1)} %get-tuple-element.13.cos_ref, ...), custom_call_target="tpu_custom_call" | custom-call | flops 1000000 | bytes 4194304 | tf_op jit(solution)/shard_map/pallas_call | solution.py:355
  (2 shorter events, 0.1 us)
Async XLA Ops:
  0.0 1.0 %copy-start = (f32[64,2048]{1,0:T(8,128)S(1)}, f32[64,2048]{1,0:T(8,128)}, u32[]{:S(2)}) copy-start(f32[64,2048]{1,0:T(8,128)} %phi_ref.3) | copy-start | bytes 1572868
  1.0 3.4 %copy-start.2 = (f32[2,4,48,512]{3,2,1,0:T(8,128)S(1)}, f32[2,4,48,512]{3,2,1,0:T(8,128)}, u32[]{:S(2)}) copy-start(f32[2,4,48,512]{3,2,1,0:T(8,128)} %kernels_ref.1) | copy-start | bytes 2359300
  1.2 8.1 %collective-permute-start = (bf16[80,2048]{1,0:T(8,128)(2,1)S(1)}, bf16[80,2048]{1,0:T(8,128)(2,1)S(1)}, u32[]{:S(2)}, u32[]{:S(2)}) collective-permute-start(bf16[80,2048]{1,0:T(8,128)(2,1)S(1)} %shard_map.73.own_ref), channel_id=1, source_target_pairs={{0,4},{4,8},{8,12},{12,0},{1,5},{5,9},{9,13},{13,1},{2,6},{6,10},{... | collective-permute-start | bytes 983048 | tf_op jit(solution)/shard_map/ppermute | solution.py:368
  1.7 10.0 %collective-permute-start.1 = (bf16[80,2048]{1,0:T(8,128)(2,1)S(1)}, bf16[80,2048]{1,0:T(8,128)(2,1)S(1)}, u32[]{:S(2)}, u32[]{:S(2)}) collective-permute-start(bf16[80,2048]{1,0:T(8,128)(2,1)S(1)} %shard_map.73.own_ref), channel_id=1, source_target_pairs={{0,12},{4,0},{8,4},{12,8},{1,13},{5,1},{9,5},{13,9},{2,14},{6,2},{... | collective-permute-start | bytes 983048 | tf_op jit(solution)/shard_map/ppermute | solution.py:368
  4.4 0.7 %copy-start.5 = (s32[512]{0:T(512)S(1)}, s32[512]{0:T(512)}, u32[]{:S(2)}) copy-start(s32[512]{0:T(512)} %param.13) | copy-start | bytes 6148
  4.4 0.7 %copy-start.6 = (s32[48]{0:T(128)S(1)}, s32[48]{0:T(128)}, u32[]{:S(2)}) copy-start(s32[48]{0:T(128)} %param.12) | copy-start | bytes 580
  5.1 0.9 %copy-start.4 = (f32[48,512]{1,0:T(8,128)S(1)}, f32[48,512]{1,0:T(8,128)}, u32[]{:S(2)}) copy-start(f32[48,512]{1,0:T(8,128)} %psi_ref.1) | copy-start | bytes 294916
  6.0 5.8 %copy-start.3 = (s32[64,2048]{1,0:T(8,128)S(1)}, s32[64,2048]{1,0:T(8,128)}, u32[]{:S(2)}) copy-start(s32[64,2048]{1,0:T(8,128)} %target_ref.1) | copy-start | bytes 1572868
  16.4 19.4 %copy-start.1 = (f32[64,2048]{1,0:T(8,128)S(1)}, f32[64,2048]{1,0:T(8,128)}, u32[]{:S(2)}) copy-start(f32[64,2048]{1,0:T(8,128)} %phi_ref.3) | copy-start | bytes 1572868
  16.4 5.4 %collective-permute-start.2 = (bf16[96,512]{1,0:T(8,128)(2,1)S(1)}, bf16[96,512]{1,0:T(8,128)(2,1)S(1)}, u32[]{:S(2)}, u32[]{:S(2)}) collective-permute-start(bf16[96,512]{1,0:T(8,128)(2,1)S(1)} %shard_map.75), channel_id=1, source_target_pairs={{0,1},{1,0},{2,3},{3,2},{4,5},{5,4},{6,7},{7,6},{8,9},{9,8},{10,11... | collective-permute-start | bytes 294920 | tf_op jit(solution)/shard_map/ppermute | solution.py:375
  21.8 7.8 %collective-permute-start.3 = (bf16[96,512]{1,0:T(8,128)(2,1)S(1)}, bf16[96,512]{1,0:T(8,128)(2,1)S(1)}, u32[]{:S(2)}, u32[]{:S(2)}) collective-permute-start(bf16[96,512]{1,0:T(8,128)(2,1)S(1)} %add_convert_fusion.1), channel_id=1, source_target_pairs={{0,2},{1,3},{2,0},{3,1},{4,6},{5,7},{6,4},{7,5},{8,10},{9,11},{10,... | collective-permute-start | bytes 294920 | tf_op jit(solution)/shard_map/ppermute | solution.py:375
  29.7 5.0 %collective-permute-start.4 = (bf16[96,512]{1,0:T(8,128)(2,1)S(1)}, bf16[96,512]{1,0:T(8,128)(2,1)S(1)}, u32[]{:S(2)}, u32[]{:S(2)}) collective-permute-start(bf16[96,512]{1,0:T(8,128)(2,1)S(1)} %add_convert_fusion.rest_2_), channel_id=1, source_target_pairs={{0,8},{4,12},{8,0},{12,4},{1,9},{5,13},{9,1},{13,5},{2,10},{6,14},... | collective-permute-start | bytes 294920 | tf_op jit(solution)/shard_map/ppermute | solution.py:368
  31.1 4.7 %collective-permute-start.5 = (bf16[96,512]{1,0:T(8,128)(2,1)S(1)}, bf16[96,512]{1,0:T(8,128)(2,1)S(1)}, u32[]{:S(2)}, u32[]{:S(2)}) collective-permute-start(bf16[96,512]{1,0:T(8,128)(2,1)S(1)} %add_convert_fusion.rest_2_), channel_id=1, source_target_pairs={{0,4},{4,8},{8,12},{12,0},{1,5},{5,9},{9,13},{13,1},{2,6},{6,10},{... | collective-permute-start | bytes 294920 | tf_op jit(solution)/shard_map/ppermute | solution.py:368
  31.1 4.7 %collective-permute-start.6 = (bf16[96,512]{1,0:T(8,128)(2,1)S(1)}, bf16[96,512]{1,0:T(8,128)(2,1)S(1)}, u32[]{:S(2)}, u32[]{:S(2)}) collective-permute-start(bf16[96,512]{1,0:T(8,128)(2,1)S(1)} %add_convert_fusion.rest_2_), channel_id=1, source_target_pairs={{0,12},{4,0},{8,4},{12,8},{1,13},{5,1},{9,5},{13,9},{2,14},{6,2},{... | collective-permute-start | bytes 294920 | tf_op jit(solution)/shard_map/ppermute | solution.py:368

commit v3 on v2

v3 whole, which is shorter than its diff:
```python
import functools

import jax
import jax.numpy as jnp
from jax import lax
from jax.experimental import pallas as pl
from jax.experimental.pallas import tpu as pltpu
from jax.sharding import PartitionSpec as P

MARGIN = 64
LEVELS = 31
SWEEPS = 2
HALO = SWEEPS
LANES = 128
PAD = 8
CHUNK = 256

slope_resist = 4.0
level_resist = 0.5
step_size = 1.0
flow_rate = 0.2

SIN_TERMS = (1.0, -1.0 / 6, 1.0 / 120, -1.0 / 5040, 1.0 / 362880, -1.0 / 39916800)
COS_TERMS = (1.0, -0.5, 1.0 / 24, -1.0 / 720, 1.0 / 40320, -1.0 / 3628800, 1.0 / 479001600)


def cos_sin(angle):
    half = 0.5 * angle
    square = half * half
    s = jnp.full_like(half, SIN_TERMS[-1])
    for term in SIN_TERMS[-2::-1]:
        s = s * square + term
    s = s * half
    c = jnp.full_like(half, COS_TERMS[-1])
    for term in COS_TERMS[-2::-1]:
        c = c * square + term
    return 1.0 - 2.0 * s * s, 2.0 * s * c


def turn(product, period):
    rest = product - jnp.round(product * (1.0 / period)) * period
    return cos_sin(rest * (2.0 * jnp.pi / period))


def mirrored(block):
    spots = (LANES - 1) - lax.broadcasted_iota(jnp.int32, block.shape, 1)
    return jnp.take_along_axis(block, spots, axis=1, mode="promise_in_bounds")


def dot(lhs_mat, rhs_mat):
    return jnp.dot(lhs_mat, rhs_mat, preferred_element_type=jnp.float32)


def dot_t(lhs_mat, rhs_mat):
    return lax.dot_general(
        lhs_mat, rhs_mat, (((1,), (1,)), ((), ())), preferred_element_type=jnp.float32
    )


def offset_groups(rows, strips):
    reach = (MARGIN + HALO + rows - 1) // rows
    groups = {}
    for offset in range(-reach, reach + 1):
        if abs(offset) > 1:
            groups.setdefault(offset % strips, []).append(offset)
    return groups


def partners(strips):
    place = lax.axis_index("strip")
    first = jnp.where(place % 2 == 0, 1, -1)
    second = -first

    def inside(offset):
        return (place + offset >= 0) & (place + offset < strips)

    return place, first, second, inside(first), inside(second)


def rotation(freqs, shape, length, freq_dim, fr, start, period):
    spot = lax.broadcasted_iota(jnp.int32, shape, 1 - freq_dim)
    second = spot >= length
    spot = jnp.where(second, spot - length, spot) + start
    imag = lax.broadcasted_iota(jnp.int32, shape, freq_dim) >= fr
    c, s = turn(freqs * spot.astype(jnp.float32), float(period))
    return jnp.where(second == imag, c, jnp.where(second, s, -s)), spot


def row_freq_lanes(row_freqs_ref, freq_lanes):
    fr = row_freqs_ref.shape[1]
    freqs = row_freqs_ref[...].astype(jnp.float32)
    freq_lanes[...] = jnp.zeros_like(freq_lanes)
    freq_lanes[0:1, 0:fr] = freqs
    freq_lanes[0:1, fr : 2 * fr] = freqs
    across = freq_lanes[0:1, :]
    down = jnp.broadcast_to(across, (8, LANES)).T[: 2 * fr, :1]
    return across, down


def first_kernel(
    strips,
    phi_hbm,
    row_freqs_ref,
    col_freqs_ref,
    table_ref,
    own_ref,
    send_a_ref,
    send_b_ref,
    phi_ref,
    mask_ref,
    p_ref,
    freq_lanes,
    sem,
):
    rows, cols = phi_ref.shape
    half = cols // 2
    fr, fc = row_freqs_ref.shape[1], table_ref.shape[0]
    window = rows + 2 * MARGIN
    bf = jnp.bfloat16
    load = pltpu.make_async_copy(phi_hbm, phi_ref, sem)
    load.start()
    place, first, second, first_in, second_in = partners(strips)

    down = row_freq_lanes(row_freqs_ref, freq_lanes)[1]

    def rows_in(offset, keep):
        table, spot = rotation(
            down, (2 * fr, 2 * rows), rows, 0, fr, MARGIN - offset * rows, window
        )
        keep = keep & (spot >= 0) & (spot < window)
        return jnp.where(keep, table, 0.0).astype(bf)

    in_own = rows_in(0, True)
    in_a = rows_in(first, first_in)
    in_b = rows_in(second, second_in)

    freqs = jnp.broadcast_to(col_freqs_ref[...].astype(jnp.float32), (8, fc)).T[:, :1]

    def make_columns(start, number):
        f = freqs[start : start + number]
        spot = lax.broadcasted_iota(jnp.int32, (number, LANES), 1).astype(jnp.float32)
        c, s = turn(f * (2.0 * spot + 1.0), 2.0 * cols)
        step_c, step_s = turn(f * float(LANES), float(cols))
        step_c = jnp.broadcast_to(step_c, (number, LANES))
        step_s = jnp.broadcast_to(step_s, (number, LANES))
        for b in range(half // LANES):
            if b:
                c, s = c * step_c - s * step_s, s * step_c + c * step_s
            here = slice(start, start + number)
            table_ref[here, b * LANES : (b + 1) * LANES] = c.astype(bf)
            table_ref[here, half + b * LANES : half + (b + 1) * LANES] = s.astype(bf)

    def transform(start, number):
        here = slice(start, start + number)
        p_ref[:rows, here] = dot_t(mask_ref[:, :half], table_ref[here, :half]).astype(bf)
        p_ref[rows:, here] = (-dot_t(mask_ref[:, half:], table_ref[here, half:])).astype(bf)

    group = fc // 2
    piece = 64
    for start in range(0, group, piece):
        make_columns(start, piece)
    load.wait()
    for b in range(half // LANES):
        left = jnp.tanh(phi_ref[:, b * LANES : (b + 1) * LANES])
        right = mirrored(jnp.tanh(phi_ref[:, cols - (b + 1) * LANES : cols - b * LANES]))
        mask_ref[:, b * LANES : (b + 1) * LANES] = (left + right).astype(bf)
        mask_ref[:, half + b * LANES : half + (b + 1) * LANES] = (left - right).astype(bf)
    transform(0, group)
    for start in range(group, fc, piece):
        make_columns(start, piece)
    transform(group, fc - group)

    p = p_ref[...]
    send_b_ref[: 2 * fr] = dot(in_b, p).astype(bf)
    send_a_ref[: 2 * fr] = dot(in_a, p).astype(bf)
    own_ref[...] = dot(in_own, p)
    tops = [phi_ref[i : i + 1, q : q + fc] for i in range(HALO) for q in range(0, cols, fc)]
    lows = [
        phi_ref[rows - HALO + i : rows - HALO + i + 1, q : q + fc]
        for i in range(HALO)
        for q in range(0, cols, fc)
    ]
    tops = jnp.concatenate(tops, axis=0)
    lows = jnp.concatenate(lows, axis=0)
    send_a_ref[2 * fr :] = jnp.where(first > 0, lows, tops).astype(bf)
    send_b_ref[2 * fr :] = jnp.where(second > 0, lows, tops).astype(bf)


def second_kernel(
    strips,
    groups,
    defocus_ref,
    row_freqs_ref,
    kernels_ref,
    psi_ref,
    phi_ref,
    target_ref,
    inner_ref,
    inner_t_ref,
    tall_ref,
    far_ref,
    k_re_ref,
    k_im_ref,
    goal_ref,
    slope_ref,
    freq_lanes,
):
    rows, cols = phi_ref.shape
    half = cols // 2
    fr = psi_ref.shape[0]
    window = rows + 2 * MARGIN
    bf = jnp.bfloat16
    place, first, second, first_in, second_in = partners(strips)
    across, down = row_freq_lanes(row_freqs_ref, freq_lanes)

    inner_ref[...] = rotation(down, (2 * fr, 2 * rows), rows, 0, fr, MARGIN, window)[0].astype(bf)
    table = rotation(across, (2 * rows, LANES), rows, 1, fr, MARGIN, window)[0]
    inner_t_ref[...] = table[:, : 2 * fr].astype(bf)

    def rows_from(offset, keep, first_row, number):
        table, spot = rotation(
            across, (2 * number, LANES), number, 1, fr, first_row - offset * rows + MARGIN, window
        )
        keep = keep & (spot >= 0) & (spot < window)
        return jnp.where(keep, table, 0.0)

    tall = rows + 2 * PAD
    for index, (offset, keep) in enumerate(((0, True), (first, first_in), (second, second_in))):
        tall_ref[index] = rows_from(offset, keep, -PAD, tall)[:, : 2 * fr].astype(bf)
    for index, offsets in enumerate(groups.values()):
        total = jnp.zeros((4 * PAD, LANES), jnp.float32)
        for offset in offsets:
            keep = (place - offset >= 0) & (place - offset < strips)
            part = rows_from(offset, keep, -PAD if offset < 0 else rows, PAD)
            nothing = jnp.zeros((PAD, LANES), jnp.float32)
            if offset < 0:
                total = total + jnp.concatenate([part[:PAD], nothing, part[PAD:], nothing], axis=0)
            else:
                total = total + jnp.concatenate([nothing, part[:PAD], nothing, part[PAD:]], axis=0)
        far_ref[index] = total[:, : 2 * fr].astype(bf)

    middle = (LEVELS - 1) / 2.0
    defocus = (defocus_ref[0].astype(jnp.float32) - middle) * (1.0 / middle)
    turn_c, turn_s = cos_sin(psi_ref[...] * defocus)
    for k in range(kernels_ref.shape[1]):
        k_re_ref[k] = kernels_ref[0, k] * turn_c - kernels_ref[1, k] * turn_s
        k_im_ref[k] = kernels_ref[0, k] * turn_s + kernels_ref[1, k] * turn_c

    scale = 1.0 / float(window * cols) ** 0.5
    goal_ref[:, :half] = target_ref[:, :half].astype(jnp.float32)
    for b in range(half // LANES):
        goal_ref[:, half + b * LANES : half + (b + 1) * LANES] = mirrored(
            target_ref[:, cols - (b + 1) * LANES : cols - b * LANES].astype(jnp.float32)
        )
    mask = jnp.tanh(phi_ref[...])
    slope_ref[...] = (step_size * scale) * (1.0 - mask * mask)


def main_kernel(
    own_ref,
    from_a_ref,
    from_b_ref,
    goal_ref,
    table_ref,
    inner_ref,
    inner_t_ref,
    k_re_ref,
    k_im_ref,
    out_ref,
    q_ref,
    x_ref,
):
    rows, cols = goal_ref.shape
    half = cols // 2
    count, fr, fc = k_re_ref.shape
    scale = 1.0 / float((rows + 2 * MARGIN) * cols) ** 0.5
    bf = jnp.bfloat16
    f32 = jnp.float32

    spec = scale * (
        own_ref[...] + from_a_ref[: 2 * fr].astype(f32) + from_b_ref[: 2 * fr].astype(f32)
    )
    s_re, s_im = spec[:fr], spec[fr:]
    for k in range(count):
        k_re, k_im = k_re_ref[k], k_im_ref[k]
        g = jnp.concatenate([k_re * s_re - k_im * s_im, k_re * s_im + k_im * s_re], axis=0)
        q_ref[k * 2 * rows : (k + 1) * 2 * rows] = dot(inner_t_ref[...], g.astype(bf)).astype(bf)

    gain = 4.0 * slope_resist / count * scale
    norm = scale * scale / count

    def weight(intensity, goal):
        resist = jax.nn.sigmoid(slope_resist * (norm * intensity - level_resist))
        return gain * (resist - goal) * resist * (1.0 - resist)

    width = min(CHUNK, half)
    for start in range(0, half, width):
        left_half = slice(start, start + width)
        right_half = slice(half + start, half + start + width)
        af = dot(q_ref[...], table_ref[:, left_half])
        db = dot(q_ref[...], table_ref[:, right_half])

        def parts(k):
            re = slice(2 * k * rows, (2 * k + 1) * rows)
            im = slice((2 * k + 1) * rows, (2 * k + 2) * rows)
            return af[re], db[im], af[im], db[re], re, im

        even = 0.0
        cross = 0.0
        for k in range(count):
            a, b, f, d, _, _ = parts(k)
            even = even + ((a * a + f * f) + (d * d + b * b))
            cross = cross + (a * b - d * f)
        cross = 2.0 * cross
        w_left = weight(even - cross, goal_ref[:, left_half])
        w_right = weight(even + cross, goal_ref[:, right_half])
        p_w = w_left + w_right
        q_w = w_right - w_left
        for k in range(count):
            a, b, f, d, re, im = parts(k)
            x_ref[re, left_half] = (p_w * a + q_w * b).astype(bf)
            x_ref[im, left_half] = (p_w * f - q_w * d).astype(bf)
            x_ref[re, right_half] = (p_w * d - q_w * f).astype(bf)
            x_ref[im, right_half] = (q_w * a + p_w * b).astype(bf)

    y_re = 0.0
    y_im = 0.0
    for k in range(count):
        u = dot_t(x_ref[k * 2 * rows : (k + 1) * 2 * rows], table_ref[...]).astype(bf)
        w = scale * dot(inner_ref[...], u)
        w_re, w_im = w[:fr], w[fr:]
        k_re, k_im = k_re_ref[k], k_im_ref[k]
        y_re = y_re + (k_re * w_re + k_im * w_im)
        y_im = y_im + (k_re * w_im - k_im * w_re)
    out_ref[:fr] = y_re.astype(bf)
    out_ref[fr:] = y_im.astype(bf)


def sum_kernel(part_ref, other_ref, far_ref, total_ref, *payload_refs):
    total = part_ref[...].astype(jnp.float32) + other_ref[...].astype(jnp.float32)
    total = total.astype(jnp.bfloat16)
    total_ref[...] = total
    for index, payload_ref in enumerate(payload_refs):
        payload_ref[...] = dot(far_ref[index], total).astype(jnp.bfloat16)


def final_kernel(
    strips,
    phi_ref,
    slope_ref,
    from_a_ref,
    from_b_ref,
    table_ref,
    tall_ref,
    y_own_ref,
    y_a_ref,
    y_b_ref,
    *rest,
):
    payload_refs = rest[:-6]
    out_hbm, level_ref, next_ref, halo_ref, out_ref, sems = rest[-6:]
    place, first, second, _, _ = partners(strips)
    rows, cols = phi_ref.shape
    half = cols // 2
    blocks = cols // LANES
    tall = rows + 2 * PAD
    fc = y_own_ref.shape[1]
    lead = y_own_ref.shape[0]
    bf = jnp.bfloat16
    f32 = jnp.float32
    scale = 1.0 / float((rows + 2 * MARGIN) * cols) ** 0.5

    z = dot(tall_ref[0], y_own_ref[...])
    z = z + dot(tall_ref[1], y_a_ref[...]) + dot(tall_ref[2], y_b_ref[...])
    for payload_ref in payload_refs:
        far = payload_ref[...].astype(f32)
        nothing = jnp.zeros((rows, fc), f32)
        z = z + jnp.concatenate(
            [
                far[:PAD],
                nothing,
                far[PAD : 2 * PAD],
                far[2 * PAD : 3 * PAD],
                nothing,
                far[3 * PAD :],
            ],
            axis=0,
        )
    z = z.astype(bf)
    even = dot(z[:tall], table_ref[:, :half])
    odd = dot(z[tall:], table_ref[:, half:])

    halo_ref[...] = jnp.zeros_like(halo_ref)
    edges_a = from_a_ref[lead:].astype(f32)
    edges_b = from_b_ref[lead:].astype(f32)
    above = jnp.where(first < 0, edges_a, edges_b)
    below = jnp.where(first < 0, edges_b, edges_a)
    per_row = cols // fc
    for i in range(HALO):
        for q in range(per_row):
            here = slice(q * fc, (q + 1) * fc)
            spot = i * per_row + q
            halo_ref[PAD - HALO + i : PAD - HALO + i + 1, here] = above[spot : spot + 1]
            halo_ref[PAD + i : PAD + i + 1, here] = below[spot : spot + 1]
    top_in = place > 0
    low_in = place < strips - 1

    def advance(b, grad):
        here = slice(b * LANES, (b + 1) * LANES)
        level_ref[b, PAD : PAD + rows] = phi_ref[:, here] - slope_ref[:, here] * grad[
            PAD : PAD + rows
        ]
        for inside, edge, to in ((top_in, 0, 0), (low_in, PAD, PAD + rows)):
            phi = halo_ref[edge : edge + PAD, here]
            mask = jnp.tanh(phi)
            slope = (step_size * scale) * (1.0 - mask * mask)
            level_ref[b, to : to + PAD] = jnp.where(
                inside, phi - slope * grad[to : to + PAD], 0.0
            )

    for b in range(half // LANES):
        part = slice(b * LANES, (b + 1) * LANES)
        advance(b, even[:, part] - odd[:, part])
        advance(blocks - 1 - b, mirrored(even[:, part] + odd[:, part]))

    lane = lax.broadcasted_iota(jnp.int32, (8, LANES), 1)

    def sweep(source, first_row, store):
        center, rise, turned = [], [], []
        nothing = jnp.zeros((8, LANES), f32)
        for b in range(blocks):
            c = source[b, first_row : first_row + 8]
            u = source[b, first_row + 1 : first_row + 9]
            d = source[b, first_row - 1 : first_row + 7]
            x = u - d
            center.append(c)
            rise.append((x, (u + d) - 2.0 * c))
            turned.append(
                (
                    pltpu.roll(c, LANES - 1, 1),
                    pltpu.roll(c, 1, 1),
                    pltpu.roll(x, LANES - 1, 1),
                    pltpu.roll(x, 1, 1),
                )
            )
        for b in range(blocks):
            after = turned[b + 1] if b + 1 < blocks else (nothing,) * 4
            before = turned[b - 1] if b else (nothing,) * 4
            right = jnp.where(lane == LANES - 1, after[0], turned[b][0])
            left = jnp.where(lane == 0, before[1], turned[b][1])
            x_right = jnp.where(lane == LANES - 1, after[2], turned[b][2])
            x_left = jnp.where(lane == 0, before[3], turned[b][3])
            c = center[b]
            x, second_x = rise[b]
            y = right - left
            second_y = (right + left) - 2.0 * c
            x_x = x * x
            y_y = y * y
            numer = second_x * y_y + second_y * x_x - (0.5 * x) * y * (x_right - x_left)
            store(b, c + flow_rate * (numer / (4.0 + x_x + y_y)))

    starts = list(range(PAD - 1, PAD + rows - 7, 8))
    if starts[-1] + 8 < PAD + rows + 1:
        starts.append(PAD + rows - 7)
    for at in starts:
        spot = lax.broadcasted_iota(jnp.int32, (8, LANES), 0) + at
        keep = ((spot >= PAD) | top_in) & ((spot < PAD + rows) | low_in)
        edge = at < PAD or at + 8 > PAD + rows

        def store_next(b, value):
            next_ref[b, at : at + 8] = jnp.where(keep, value, 0.0) if edge else value

        sweep(level_ref, at, store_next)

    copies = []
    for index in range(rows // 8):

        def store_out(b, value):
            out_ref[8 * index : 8 * index + 8, b * LANES : (b + 1) * LANES] = value

        sweep(next_ref, PAD + 8 * index, store_out)
        here = pl.ds(8 * index, 8)
        copies.append(pltpu.make_async_copy(out_ref.at[here], out_hbm.at[here], sems.at[index]))
        copies[-1].start()
    for copy in copies:
        copy.wait()


def spec(kind):
    return pl.BlockSpec(memory_space={"v": pltpu.VMEM, "s": pltpu.SMEM, "h": pltpu.HBM}[kind])


def call(kernel, outs, args, kinds=None, out_kinds=None, scratch=(), limit=24, flops=1000000):
    kinds = kinds or "v" * len(args)
    out_kinds = out_kinds or "v" * len(outs)
    return pl.pallas_call(
        kernel,
        out_shape=outs,
        in_specs=[spec(kind) for kind in kinds],
        out_specs=[spec(kind) for kind in out_kinds],
        scratch_shapes=list(scratch),
        compiler_params=pltpu.CompilerParams(vmem_limit_bytes=limit << 20),
        cost_estimate=pl.CostEstimate(flops=flops, bytes_accessed=4 << 20, transcendentals=0),
    )(*args)


def pair_up(block, first):
    count = lax.axis_size("strip")
    low = range(0 if first else 1, count, 2)
    pairs = [(i, (i + 1) % count) for i in low]
    return lax.ppermute(block, "strip", pairs + [(b, a) for a, b in pairs])


def on_device(phi, target, defocus_ids, kernels, psi, row_freqs, col_freqs):
    rows, cols = phi.shape
    half = cols // 2
    fr, fc = psi.shape
    count = kernels.shape[1]
    strips = lax.axis_size("strip")
    planes = lax.axis_size("focus")
    groups = offset_groups(rows, strips)
    tall = rows + 2 * PAD
    bf = jnp.bfloat16
    f32 = jnp.float32
    shape = jax.ShapeDtypeStruct
    lanes = pltpu.VMEM((8, LANES), f32)
    packet = shape((2 * fr + HALO * (cols // fc), fc), bf)
    row_freqs = row_freqs.reshape(1, fr)

    table, s_own, send_a, send_b = call(
        functools.partial(first_kernel, strips),
        [shape((fc, cols), bf), shape((2 * fr, fc), f32), packet, packet],
        (phi, row_freqs, col_freqs.reshape(1, fc)),
        kinds="hvv",
        scratch=[
            pltpu.VMEM((rows, cols), f32),
            pltpu.VMEM((rows, cols), bf),
            pltpu.VMEM((2 * rows, fc), bf),
            lanes,
            pltpu.SemaphoreType.DMA(()),
        ],
    )
    from_b = pair_up(send_b, False)
    from_a = pair_up(send_a, True)
    inner, inner_t, tall_t, far_t, k_re, k_im, goal, slope = call(
        functools.partial(second_kernel, strips, groups),
        [
            shape((2 * fr, 2 * rows), bf),
            shape((2 * rows, 2 * fr), bf),
            shape((3, 2 * tall, 2 * fr), bf),
            shape((max(1, len(groups)), 4 * PAD, 2 * fr), bf),
            shape((count, fr, fc), f32),
            shape((count, fr, fc), f32),
            shape((rows, cols), f32),
            shape((rows, cols), f32),
        ],
        (defocus_ids, row_freqs, kernels, psi, phi, target),
        kinds="svvvvv",
        scratch=[lanes],
        flops=4000000000,
    )
    (part,) = call(
        main_kernel,
        [shape((2 * fr, fc), bf)],
        (s_own, from_a, from_b, goal, table, inner, inner_t, k_re, k_im),
        scratch=[
            pltpu.VMEM((count * 2 * rows, fc), bf),
            pltpu.VMEM((count * 2 * rows, cols), bf),
        ],
        flops=4000000000,
    )
    step = 1
    other = jnp.zeros_like(part)
    while step < planes:
        if step > 1:
            part = lax.optimization_barrier(
                (part.astype(f32) + other.astype(f32)).astype(bf)
            )
        other = lax.ppermute(part, "focus", [(i, i ^ step) for i in range(planes)])
        step *= 2
    total, *payloads = call(
        sum_kernel,
        [shape((2 * fr, fc), bf)] + [shape((4 * PAD, fc), bf)] * len(groups),
        (part, other, far_t),
    )
    far = [
        lax.ppermute(payload, "strip", [(i, (i - turn_by) % strips) for i in range(strips)])
        for turn_by, payload in zip(groups, payloads)
    ]
    y_b = pair_up(total, False)
    y_a = pair_up(total, True)
    return call(
        functools.partial(final_kernel, strips),
        [shape((rows, cols), f32)],
        (phi, slope, from_a, from_b, table, tall_t, total, y_a, y_b, *far),
        out_kinds="h",
        scratch=[
            pltpu.VMEM((cols // LANES, tall, LANES), f32),
            pltpu.VMEM((cols // LANES, tall, LANES), f32),
            pltpu.VMEM((2 * PAD, cols), f32),
            pltpu.VMEM((rows, cols), f32),
            pltpu.SemaphoreType.DMA((rows // 8,)),
        ],
    )[0]


def solution(mesh):
    return jax.shard_map(
        on_device,
        mesh=mesh,
        in_specs=(
            P(("tile", "strip"), None),
            P(("tile", "strip"), None),
            P(("tile", "focus")),
            P(),
            P(),
            P(),
            P(),
        ),
        out_specs=P(("tile", "strip"), None),
        check_vma=False,
    )
```

time: 39.9 us -> 38.8 us (0.972)
  waiting for transfers between devices: 15.3 us -> 10.4 us
  local copies, waits for them, and re-layouts: 2.61 us -> 6.49 us
  starting transfers between devices: 10.1 us -> 9.58 us
  Pallas kernels: 10.8 us -> 11.2 us
    ppermute x7, waiting for transfers between devices: 15.3 us -> 10.4 us  [the longest x2 7.54 us: on_device(): other = lax.ppermute(part, 'focus', [(i, i ^ step) for i in range(planes)])]
    unnamed x14 -> x16, local copies, waits for them, and re-layouts: 2.61 us -> 6.49 us
    ppermute x7, starting transfers between devices: 10.1 us -> 9.58 us  [the longest x2 4.3 us: on_device(): other = lax.ppermute(part, 'focus', [(i, i ^ step) for i in range(planes)])]
    pallas_call x4 -> x5, Pallas kernels: 10.8 us -> 11.2 us  [call(): pl.pallas_call(kernel, out_shape=outs, in_specs=[spec(kind) for kind in k...]
  transfers between devices with their start and end apart: 7 -> 7, of which waited for: 6 -> 3; matrix products, arithmetic and copies ran while one was open for 0% -> 0% of each run, Pallas kernels for 6% -> 2%
where the time goes in v3:
time: 38.8 us; the launch traced here: 38.5 us
  Pallas kernels  11.2 us (29%)
  waiting for transfers between devices  10.4 us (27%)
  starting transfers between devices  9.58 us (25%)
  local copies, waits for them, and re-layouts  6.49 us (17%)
  between operations  0.74 us (2%)
    pallas_call x5, Pallas kernels, call(): pl.pallas_call(kernel, out_shape=outs, in_specs=[spec(kind) for kind in k...  11.2 us
    ppermute x2, waiting for transfers between devices, on_device(): other = lax.ppermute(part, 'focus', [(i, i ^ step) for i in range(planes)])  7.54 us
    unnamed x16, local copies, waits for them, and re-layouts  6.49 us
    ppermute x2, starting transfers between devices, on_device(): other = lax.ppermute(part, 'focus', [(i, i ^ step) for i in range(planes)])  4.3 us
    ppermute x4, starting transfers between devices, pair_up(): return lax.ppermute(block, 'strip', pairs + [(b, a) for a, b in pairs])  3.9 us
    ppermute x1, waiting for transfers between devices, on_device(): lax.ppermute(payload, 'strip', [(i, (i - turn_by) % strips) for i in rang...  2.85 us
    ppermute x1, starting transfers between devices, on_device(): lax.ppermute(payload, 'strip', [(i, (i - turn_by) % strips) for i in rang...  1.39 us
  transfers between devices with their start and end apart: 7, of which 3 were waited for; matrix products, arithmetic and copies ran while one was open for 0% of the time, Pallas kernels for 2%

profile of v3, /device:TPU:0, one launch (start us, length us, event | category | flops | bytes accessed | tf_op | source)
XLA Modules:
  0.0 38.5 jit_solution(5472443962506843706)
XLA Ops:
  0.0 0.0 copy-start
  0.0 1.0 %copy-done = f32[64,2048]{1,0:T(8,128)S(1)} copy-done((f32[64,2048]{1,0:T(8,128)S(1)}, f32[64,2048]{1,0:T(8,128)}, u32[]{:S(2)}) %copy-start) | copy-done | bytes 524312
  1.0 0.0 copy-start.3
  1.0 0.7 %copy-done.3 = s32[512]{0:T(512)S(1)} copy-done((s32[512]{0:T(512)S(1)}, s32[512]{0:T(512)}, u32[]{:S(2)}) %copy-start.3) | copy-done | bytes 2072
  1.7 0.0 copy-start.4
  1.7 0.7 %copy-done.4 = s32[48]{0:T(128)S(1)} copy-done((s32[48]{0:T(128)S(1)}, s32[48]{0:T(128)}, u32[]{:S(2)}) %copy-start.4) | copy-done | bytes 216
  2.4 2.2 %shard_map.74 = (bf16[512,2048]{1,0:T(8,128)(2,1)S(1)}, f32[96,512]{1,0:T(8,128)S(1)}, bf16[104,512]{1,0:T(8,128)(2,1)S(1)}, bf16[104,512]{1,0:T(8,128)(2,1)S(1)}) custom-call(f32[64,2048]{1,0:T(8,128)S(1)} %copy-done, s32[1,48]{1,0:T(1,128)S(1)} %bitcast.3, s32[1,512]{1,0:T(1,128)S(1)} %bitcast.2), custom_call_target="tpu_custom_call" | custom-call | flops 1000000 | bytes 4194304 | tf_op jit(solution)/shard_map/pallas_call | solution.py:496
  4.6 0.6 %collective-permute-start = (bf16[104,512]{1,0:T(8,128)(2,1)S(1)}, bf16[104,512]{1,0:T(8,128)(2,1)S(1)}, u32[]{:S(2)}, u32[]{:S(2)}) collective-permute-start(bf16[104,512]{1,0:T(8,128)(2,1)S(1)} %get-tuple-element.20), channel_id=1, source_target_pairs={{0,4},{8,12},{4,0},{12,8},{1,5},{9,13},{5,1},{13,9},{2,6},{10,14},... | collective-permute-start | bytes 319496 | tf_op jit(solution)/shard_map/ppermute | solution.py:511
  5.2 2.6 %collective-permute-start.1 = (bf16[104,512]{1,0:T(8,128)(2,1)S(1)}, bf16[104,512]{1,0:T(8,128)(2,1)S(1)}, u32[]{:S(2)}, u32[]{:S(2)}) collective-permute-start(bf16[104,512]{1,0:T(8,128)(2,1)S(1)} %get-tuple-element.21), channel_id=1, source_target_pairs={{4,8},{12,0},{8,4},{0,12},{5,9},{13,1},{9,5},{1,13},{6,10},{14,2},... | collective-permute-start | bytes 319496 | tf_op jit(solution)/shard_map/ppermute | solution.py:511
  8.4 0.0 copy-start.1
  8.4 1.0 %copy-done.1 = f32[64,2048]{1,0:T(8,128)S(1)} copy-done((f32[64,2048]{1,0:T(8,128)S(1)}, f32[64,2048]{1,0:T(8,128)}, u32[]{:S(2)}) %copy-start.1) | copy-done | bytes 524312
  9.4 1.1 %copy-done.5 = f32[2,4,48,512]{3,2,1,0:T(8,128)S(1)} copy-done((f32[2,4,48,512]{3,2,1,0:T(8,128)S(1)}, f32[2,4,48,512]{3,2,1,0:T(8,128)}, u32[]{:S(2)}) %copy-start.5) | copy-done | bytes 786456
  10.6 1.0 %copy-done.6 = s32[64,2048]{1,0:T(8,128)S(1)} copy-done((s32[64,2048]{1,0:T(8,128)S(1)}, s32[64,2048]{1,0:T(8,128)}, u32[]{:S(2)}) %copy-start.6) | copy-done | bytes 524312
  11.6 0.9 %copy-done.7 = f32[48,512]{1,0:T(8,128)S(1)} copy-done((f32[48,512]{1,0:T(8,128)S(1)}, f32[48,512]{1,0:T(8,128)}, u32[]{:S(2)}) %copy-start.7) | copy-done | bytes 98328
  12.5 0.9 %shard_map.73 = (bf16[96,128]{1,0:T(8,128)(2,1)S(1)}, bf16[128,96]{1,0:T(8,128)(2,1)S(1)}, bf16[3,160,96]{2,1,0:T(8,128)(2,1)S(1)}, bf16[1,32,96]{2,1,0:T(8,128)...) custom-call(s32[1]{0:T(128)S(6)} %copy.8.defocus_ref, ...), custom_call_target="tpu_custom_call" | custom-call | flops 4000000000 | bytes 4194304 | tf_op jit(solution)/shard_map/pallas_call | solution.py:496
  13.4 0.0 collective-permute-done.from_a_ref
  13.5 0.0 collective-permute-done.1.from_b_ref
  13.5 0.0 copy-start.2
  13.5 5.3 %shard_map.75 = bf16[96,512]{1,0:T(8,128)(2,1)S(1)} custom-call(f32[96,512]{1,0:T(8,128)S(1)} %get-tuple-element.24.own_ref, bf16[104,512]{1,0:T(8,128)(2,1)S(1)} %collective-permute-done.from_a_ref, bf16[104,512]{1,0:T(8,128)(2,1)S(1)} %collective-permute-done.1.from_b_ref, f32[64,2048]{1,0:T(8,128)S(1)} %get-tuple-element.25.goal_ref, ...), custom_call_target="tpu_custom_call" | custom-call | flops 4000000000 | bytes 4194304 | tf_op jit(solution)/shard_map/pallas_call | solution.py:496
  18.8 1.6 %collective-permute-start.2 = (bf16[96,512]{1,0:T(8,128)(2,1)S(1)}, bf16[96,512]{1,0:T(8,128)(2,1)S(1)}, u32[]{:S(2)}, u32[]{:S(2)}) collective-permute-start(bf16[96,512]{1,0:T(8,128)(2,1)S(1)} %shard_map.75), channel_id=1, source_target_pairs={{0,1},{1,0},{2,3},{3,2},{4,5},{5,4},{6,7},{7,6},{8,9},{9,8},{10,11... | collective-permute-start | bytes 294920 | tf_op jit(solution)/shard_map/ppermute | solution.py:579
  20.4 3.2 %collective-permute-done.2 = bf16[96,512]{1,0:T(8,128)(2,1)S(1)} collective-permute-done((bf16[96,512]{1,0:T(8,128)(2,1)S(1)}, bf16[96,512]{1,0:T(8,128)(2,1)S(1)}, u32[]{:S(2)}, u32[]{:S(2)}) %collective-permute-start.2) | collective-permute-done | bytes 98336 | tf_op jit(solution)/shard_map/ppermute | solution.py:579
  23.6 2.7 %collective-permute-start.3 = (bf16[96,512]{1,0:T(8,128)(2,1)S(1)}, bf16[96,512]{1,0:T(8,128)(2,1)S(1)}, u32[]{:S(2)}, u32[]{:S(2)}) collective-permute-start(bf16[96,512]{1,0:T(8,128)(2,1)S(1)} %add_convert_fusion.part_ref), channel_id=1, source_target_pairs={{0,2},{1,3},{2,0},{3,1},{4,6},{5,7},{6,4},{7,5},{8,10},{9,11},{10,... | collective-permute-start | bytes 294920 | tf_op jit(solution)/shard_map/ppermute | solution.py:579
  26.3 4.3 %collective-permute-done.3.other_ref = bf16[96,512]{1,0:T(8,128)(2,1)S(1)} collective-permute-done((bf16[96,512]{1,0:T(8,128)(2,1)S(1)}, bf16[96,512]{1,0:T(8,128)(2,1)S(1)}, u32[]{:S(2)}, u32[]{:S(2)}) %collective-permute-start.3) | collective-permute-done | bytes 98336 | tf_op jit(solution)/shard_map/ppermute | solution.py:579
  30.6 0.1 shard_map.76
  30.8 0.0 collective-permute-start.5
  30.8 0.7 %collective-permute-start.4 = (bf16[96,512]{1,0:T(8,128)(2,1)S(1)}, bf16[96,512]{1,0:T(8,128)(2,1)S(1)}, u32[]{:S(2)}, u32[]{:S(2)}) collective-permute-start(bf16[96,512]{1,0:T(8,128)(2,1)S(1)} %get-tuple-element.31.y_own_ref), channel_id=1, source_target_pairs={{0,4},{8,12},{4,0},{12,8},{1,5},{9,13},{5,1},{13,9},{2,6},{10,14},... | collective-permute-start | bytes 294920 | tf_op jit(solution)/shard_map/ppermute | solution.py:511
  31.5 1.4 %collective-permute-start.6 = (bf16[32,512]{1,0:T(8,128)(2,1)S(1)}, bf16[32,512]{1,0:T(8,128)(2,1)S(1)}, u32[]{:S(2)}, u32[]{:S(2)}) collective-permute-start(bf16[32,512]{1,0:T(8,128)(2,1)S(1)} %get-tuple-element.32), channel_id=1, source_target_pairs={{0,8},{4,12},{8,0},{12,4},{1,9},{5,13},{9,1},{13,5},{2,10},{6,14},... | collective-permute-start | bytes 98312 | tf_op jit(solution)/shard_map/ppermute | solution.py:587
  32.9 2.8 %collective-permute-done.6.rest_0_ = bf16[32,512]{1,0:T(8,128)(2,1)S(1)} collective-permute-done((bf16[32,512]{1,0:T(8,128)(2,1)S(1)}, bf16[32,512]{1,0:T(8,128)(2,1)S(1)}, u32[]{:S(2)}, u32[]{:S(2)}) %collective-permute-start.6) | collective-permute-done | bytes 32800 | tf_op jit(solution)/shard_map/ppermute | solution.py:587
  35.8 0.0 collective-permute-done.5.y_b_ref
  35.8 0.0 collective-permute-done.4.y_a_ref
  35.8 0.0 copy-done.2
  35.8 2.7 %shard_map.77 = f32[64,2048]{1,0:T(8,128)} custom-call(f32[64,2048]{1,0:T(8,128)S(1)} %copy-done.2, f32[64,2048]{1,0:T(8,128)S(1)} %get-tuple-element.19.slope_ref, bf16[104,512]{1,0:T(8,128)(2,1)S(1)} %collective-permute-done.from_a_ref, bf16[104,512]{1,0:T(8,128)(2,1)S(1)} %collective-permute-done.1.from_b_ref, ...), custom_call_target="tpu_custom_call" | custom-call | flops 1000000 | bytes 4194304 | tf_op jit(solution)/shard_map/pallas_call | solution.py:496
  (4 shorter events, 0.0 us)
Async XLA Ops:
  0.0 1.0 %copy-start = (f32[64,2048]{1,0:T(8,128)S(1)}, f32[64,2048]{1,0:T(8,128)}, u32[]{:S(2)}) copy-start(f32[64,2048]{1,0:T(8,128)} %phi_ref.3) | copy-start | bytes 1572868
  1.0 0.7 %copy-start.3 = (s32[512]{0:T(512)S(1)}, s32[512]{0:T(512)}, u32[]{:S(2)}) copy-start(s32[512]{0:T(512)} %param.13) | copy-start | bytes 6148
  1.7 0.7 %copy-start.4 = (s32[48]{0:T(128)S(1)}, s32[48]{0:T(128)}, u32[]{:S(2)}) copy-start(s32[48]{0:T(128)} %param.12) | copy-start | bytes 580
  4.6 8.9 %collective-permute-start = (bf16[104,512]{1,0:T(8,128)(2,1)S(1)}, bf16[104,512]{1,0:T(8,128)(2,1)S(1)}, u32[]{:S(2)}, u32[]{:S(2)}) collective-permute-start(bf16[104,512]{1,0:T(8,128)(2,1)S(1)} %get-tuple-element.20), channel_id=1, source_target_pairs={{0,4},{8,12},{4,0},{12,8},{1,5},{9,13},{5,1},{13,9},{2,6},{10,14},... | collective-permute-start | bytes 319496 | tf_op jit(solution)/shard_map/ppermute | solution.py:511
  5.2 8.3 %collective-permute-start.1 = (bf16[104,512]{1,0:T(8,128)(2,1)S(1)}, bf16[104,512]{1,0:T(8,128)(2,1)S(1)}, u32[]{:S(2)}, u32[]{:S(2)}) collective-permute-start(bf16[104,512]{1,0:T(8,128)(2,1)S(1)} %get-tuple-element.21), channel_id=1, source_target_pairs={{4,8},{12,0},{8,4},{0,12},{5,9},{13,1},{9,5},{1,13},{6,10},{14,2},... | collective-permute-start | bytes 319496 | tf_op jit(solution)/shard_map/ppermute | solution.py:511
  8.4 1.0 %copy-start.1 = (f32[64,2048]{1,0:T(8,128)S(1)}, f32[64,2048]{1,0:T(8,128)}, u32[]{:S(2)}) copy-start(f32[64,2048]{1,0:T(8,128)} %phi_ref.3) | copy-start | bytes 1572868
  9.4 1.1 %copy-start.5 = (f32[2,4,48,512]{3,2,1,0:T(8,128)S(1)}, f32[2,4,48,512]{3,2,1,0:T(8,128)}, u32[]{:S(2)}) copy-start(f32[2,4,48,512]{3,2,1,0:T(8,128)} %kernels_ref.1) | copy-start | bytes 2359300
  10.6 1.0 %copy-start.6 = (s32[64,2048]{1,0:T(8,128)S(1)}, s32[64,2048]{1,0:T(8,128)}, u32[]{:S(2)}) copy-start(s32[64,2048]{1,0:T(8,128)} %target_ref.1) | copy-start | bytes 1572868
  11.6 0.9 %copy-start.7 = (f32[48,512]{1,0:T(8,128)S(1)}, f32[48,512]{1,0:T(8,128)}, u32[]{:S(2)}) copy-start(f32[48,512]{1,0:T(8,128)} %psi_ref.1) | copy-start | bytes 294916
  13.5 22.3 %copy-start.2 = (f32[64,2048]{1,0:T(8,128)S(1)}, f32[64,2048]{1,0:T(8,128)}, u32[]{:S(2)}) copy-start(f32[64,2048]{1,0:T(8,128)} %phi_ref.3) | copy-start | bytes 1572868
  18.8 4.8 %collective-permute-start.2 = (bf16[96,512]{1,0:T(8,128)(2,1)S(1)}, bf16[96,512]{1,0:T(8,128)(2,1)S(1)}, u32[]{:S(2)}, u32[]{:S(2)}) collective-permute-start(bf16[96,512]{1,0:T(8,128)(2,1)S(1)} %shard_map.75), channel_id=1, source_target_pairs={{0,1},{1,0},{2,3},{3,2},{4,5},{5,4},{6,7},{7,6},{8,9},{9,8},{10,11... | collective-permute-start | bytes 294920 | tf_op jit(solution)/shard_map/ppermute | solution.py:579
  23.6 7.0 %collective-permute-start.3 = (bf16[96,512]{1,0:T(8,128)(2,1)S(1)}, bf16[96,512]{1,0:T(8,128)(2,1)S(1)}, u32[]{:S(2)}, u32[]{:S(2)}) collective-permute-start(bf16[96,512]{1,0:T(8,128)(2,1)S(1)} %add_convert_fusion.part_ref), channel_id=1, source_target_pairs={{0,2},{1,3},{2,0},{3,1},{4,6},{5,7},{6,4},{7,5},{8,10},{9,11},{10,... | collective-permute-start | bytes 294920 | tf_op jit(solution)/shard_map/ppermute | solution.py:579
  30.8 5.0 %collective-permute-start.5 = (bf16[96,512]{1,0:T(8,128)(2,1)S(1)}, bf16[96,512]{1,0:T(8,128)(2,1)S(1)}, u32[]{:S(2)}, u32[]{:S(2)}) collective-permute-start(bf16[96,512]{1,0:T(8,128)(2,1)S(1)} %get-tuple-element.31.y_own_ref), channel_id=1, source_target_pairs={{4,8},{12,0},{8,4},{0,12},{5,9},{13,1},{9,5},{1,13},{6,10},{14,2},... | collective-permute-start | bytes 294920 | tf_op jit(solution)/shard_map/ppermute | solution.py:511
  30.8 5.0 %collective-permute-start.4 = (bf16[96,512]{1,0:T(8,128)(2,1)S(1)}, bf16[96,512]{1,0:T(8,128)(2,1)S(1)}, u32[]{:S(2)}, u32[]{:S(2)}) collective-permute-start(bf16[96,512]{1,0:T(8,128)(2,1)S(1)} %get-tuple-element.31.y_own_ref), channel_id=1, source_target_pairs={{0,4},{8,12},{4,0},{12,8},{1,5},{9,13},{5,1},{13,9},{2,6},{10,14},... | collective-permute-start | bytes 294920 | tf_op jit(solution)/shard_map/ppermute | solution.py:511
  31.5 4.2 %collective-permute-start.6 = (bf16[32,512]{1,0:T(8,128)(2,1)S(1)}, bf16[32,512]{1,0:T(8,128)(2,1)S(1)}, u32[]{:S(2)}, u32[]{:S(2)}) collective-permute-start(bf16[32,512]{1,0:T(8,128)(2,1)S(1)} %get-tuple-element.32), channel_id=1, source_target_pairs={{0,8},{4,12},{8,0},{12,4},{1,9},{5,13},{9,1},{13,5},{2,10},{6,14},... | collective-permute-start | bytes 98312 | tf_op jit(solution)/shard_map/ppermute | solution.py:587

commit v4 on v3

--- a/solution.py
+++ b/solution.py
@@ -77,63 +77,67 @@
     return place, first, second, inside(first), inside(second)
 
 
+def quarter(second, imag, c, s):
+    return jnp.where(second == imag, c, jnp.where(second, s, -s))
+
+
 def rotation(freqs, shape, length, freq_dim, fr, start, period):
     spot = lax.broadcasted_iota(jnp.int32, shape, 1 - freq_dim)
     second = spot >= length
     spot = jnp.where(second, spot - length, spot) + start
     imag = lax.broadcasted_iota(jnp.int32, shape, freq_dim) >= fr
     c, s = turn(freqs * spot.astype(jnp.float32), float(period))
-    return jnp.where(second == imag, c, jnp.where(second, s, -s)), spot
-
-
-def row_freq_lanes(row_freqs_ref, freq_lanes):
+    return quarter(second, imag, c, s), spot
+
+
+def interleaved(freqs, shape, freq_dim, fr, start, period):
+    index = lax.broadcasted_iota(jnp.int32, shape, 1 - freq_dim)
+    spot = ((index >> 4) << 3) + (index & 7) + start
+    second = (index & 8) > 0
+    imag = lax.broadcasted_iota(jnp.int32, shape, freq_dim) >= fr
+    c, s = turn(freqs * spot.astype(jnp.float32), float(period))
+    return quarter(second, imag, c, s)
+
+
+def row_freq_lanes(row_freqs_ref, freq_ref):
     fr = row_freqs_ref.shape[1]
-    freqs = row_freqs_ref[...].astype(jnp.float32)
-    freq_lanes[...] = jnp.zeros_like(freq_lanes)
-    freq_lanes[0:1, 0:fr] = freqs
-    freq_lanes[0:1, fr : 2 * fr] = freqs
-    across = freq_lanes[0:1, :]
-    down = jnp.broadcast_to(across, (8, LANES)).T[: 2 * fr, :1]
-    return across, down
+    freqs = jnp.broadcast_to(row_freqs_ref[...].astype(jnp.float32), (8, fr))
+    freq_ref[...] = jnp.zeros_like(freq_ref)
+    freq_ref[:, 0:fr] = freqs
+    freq_ref[:, fr : 2 * fr] = freqs
 
 
 def first_kernel(
     strips,
     phi_hbm,
-    row_freqs_ref,
-    col_freqs_ref,
+    row_freqs_hbm,
+    col_freqs_hbm,
     table_ref,
     own_ref,
     send_a_ref,
     send_b_ref,
     phi_ref,
+    freq_ref,
     mask_ref,
     p_ref,
-    freq_lanes,
-    sem,
+    row_freqs_ref,
+    col_freqs_ref,
+    sems,
 ):
     rows, cols = phi_ref.shape
     half = cols // 2
     fr, fc = row_freqs_ref.shape[1], table_ref.shape[0]
     window = rows + 2 * MARGIN
     bf = jnp.bfloat16
-    load = pltpu.make_async_copy(phi_hbm, phi_ref, sem)
-    load.start()
+    load_cols = pltpu.make_async_copy(col_freqs_hbm, col_freqs_ref, sems.at[0])
+    load_rows = pltpu.make_async_copy(row_freqs_hbm, row_freqs_ref, sems.at[1])
+    load_phi = pltpu.make_async_copy(phi_hbm, phi_ref, sems.at[2])
+    load_cols.start()
+    load_rows.start()
+    load_phi.start()
     place, first, second, first_in, second_in = partners(strips)
 
-    down = row_freq_lanes(row_freqs_ref, freq_lanes)[1]
-
-    def rows_in(offset, keep):
-        table, spot = rotation(
-            down, (2 * fr, 2 * rows), rows, 0, fr, MARGIN - offset * rows, window
-        )
-        keep = keep & (spot >= 0) & (spot < window)
-        return jnp.where(keep, table, 0.0).astype(bf)
-
-    in_own = rows_in(0, True)
-    in_a = rows_in(first, first_in)
-    in_b = rows_in(second, second_in)
-
+    load_cols.wait()
     freqs = jnp.broadcast_to(col_freqs_ref[...].astype(jnp.float32), (8, fc)).T[:, :1]
 
     def make_columns(start, number):
@@ -143,10 +147,14 @@
         step_c, step_s = turn(f * float(LANES), float(cols))
         step_c = jnp.broadcast_to(step_c, (number, LANES))
         step_s = jnp.broadcast_to(step_s, (number, LANES))
+        twice = 2.0 * step_c
+        c_old, s_old = c, s
+        here = slice(start, start + number)
         for b in range(half // LANES):
-            if b:
+            if b == 1:
                 c, s = c * step_c - s * step_s, s * step_c + c * step_s
-            here = slice(start, start + number)
+            elif b:
+                c, s, c_old, s_old = twice * c - c_old, twice * s - s_old, c, s
             table_ref[here, b * LANES : (b + 1) * LANES] = c.astype(bf)
             table_ref[here, half + b * LANES : half + (b + 1) * LANES] = s.astype(bf)
 
@@ -159,7 +167,8 @@
     piece = 64
     for start in range(0, group, piece):
         make_columns(start, piece)
-    load.wait()
+    load_rows.wait()
+    load_phi.wait()
     for b in range(half // LANES):
         left = jnp.tanh(phi_ref[:, b * LANES : (b + 1) * LANES])
         right = mirrored(jnp.tanh(phi_ref[:, cols - (b + 1) * LANES : cols - b * LANES]))
@@ -169,6 +178,30 @@
     for start in range(group, fc, piece):
         make_columns(start, piece)
     transform(group, fc - group)
+
+    row_freq_lanes(row_freqs_ref, freq_ref)
+    down = freq_ref[...].T[:fr, :1]
+    spot = lax.broadcasted_iota(jnp.int32, (fr, 2 * rows), 1)
+    later = spot >= rows
+    spot = jnp.where(later, spot - rows, spot)
+    c, s = turn(down * (spot + MARGIN).astype(jnp.float32), float(window))
+    turn_c, turn_s = turn(down * float(rows), float(window))
+    turn_c = jnp.broadcast_to(turn_c, c.shape)
+    turn_s = jnp.broadcast_to(turn_s, c.shape)
+
+    def rows_in(c, s, offset, keep):
+        at = spot + MARGIN - offset * rows
+        keep = keep & (at >= 0) & (at < window)
+        c = jnp.where(keep, c, 0.0)
+        s = jnp.where(keep, s, 0.0)
+        return jnp.concatenate([jnp.where(later, s, c), jnp.where(later, c, -s)], axis=0).astype(bf)
+
+    in_own = rows_in(c, s, 0, True)
+    sign = -first.astype(jnp.float32)
+    in_a = rows_in(c * turn_c - s * (sign * turn_s), s * turn_c + c * (sign * turn_s), first, first_in)
+    in_b = rows_in(
+        c * turn_c + s * (sign * turn_s), s * turn_c - c * (sign * turn_s), second, second_in
+    )
 
     p = p_ref[...]
     send_b_ref[: 2 * fr] = dot(in_b, p).astype(bf)
@@ -190,11 +223,11 @@
     strips,
     groups,
     defocus_ref,
-    row_freqs_ref,
-    kernels_ref,
-    psi_ref,
+    freq_ref,
     phi_ref,
-    target_ref,
+    kernels_hbm,
+    psi_hbm,
+    target_hbm,
     inner_ref,
     inner_t_ref,
     tall_ref,
@@ -203,18 +236,28 @@
     k_im_ref,
     goal_ref,
     slope_ref,
-    freq_lanes,
+    kernels_ref,
+    psi_ref,
+    target_ref,
+    sems,
 ):
     rows, cols = phi_ref.shape
     half = cols // 2
     fr = psi_ref.shape[0]
+    load_psi = pltpu.make_async_copy(psi_hbm, psi_ref, sems.at[0])
+    load_kernels = pltpu.make_async_copy(kernels_hbm, kernels_ref, sems.at[1])
+    load_target = pltpu.make_async_copy(target_hbm, target_ref, sems.at[2])
+    load_psi.start()
+    load_kernels.start()
+    load_target.start()
     window = rows + 2 * MARGIN
     bf = jnp.bfloat16
     place, first, second, first_in, second_in = partners(strips)
-    across, down = row_freq_lanes(row_freqs_ref, freq_lanes)
-
-    inner_ref[...] = rotation(down, (2 * fr, 2 * rows), rows, 0, fr, MARGIN, window)[0].astype(bf)
-    table = rotation(across, (2 * rows, LANES), rows, 1, fr, MARGIN, window)[0]
+    across = freq_ref[0:1, :]
+    down = freq_ref[...].T[: 2 * fr, :1]
+
+    inner_ref[...] = interleaved(down, (2 * fr, 2 * rows), 0, fr, MARGIN, window).astype(bf)
+    table = interleaved(across, (2 * rows, LANES), 1, fr, MARGIN, window)
     inner_t_ref[...] = table[:, : 2 * fr].astype(bf)
 
     def rows_from(offset, keep, first_row, number):
@@ -239,6 +282,12 @@
                 total = total + jnp.concatenate([nothing, part[:PAD], nothing, part[PAD:]], axis=0)
         far_ref[index] = total[:, : 2 * fr].astype(bf)
 
+    scale = 1.0 / float(window * cols) ** 0.5
+    mask = jnp.tanh(phi_ref[...])
+    slope_ref[...] = (step_size * scale) * (1.0 - mask * mask)
+
+    load_psi.wait()
+    load_kernels.wait()
     middle = (LEVELS - 1) / 2.0
     defocus = (defocus_ref[0].astype(jnp.float32) - middle) * (1.0 / middle)
     turn_c, turn_s = cos_sin(psi_ref[...] * defocus)
@@ -246,14 +295,12 @@
         k_re_ref[k] = kernels_ref[0, k] * turn_c - kernels_ref[1, k] * turn_s
         k_im_ref[k] = kernels_ref[0, k] * turn_s + kernels_ref[1, k] * turn_c
 
-    scale = 1.0 / float(window * cols) ** 0.5
+    load_target.wait()
     goal_ref[:, :half] = target_ref[:, :half].astype(jnp.float32)
     for b in range(half // LANES):
         goal_ref[:, half + b * LANES : half + (b + 1) * LANES] = mirrored(
             target_ref[:, cols - (b + 1) * LANES : cols - b * LANES].astype(jnp.float32)
         )
-    mask = jnp.tanh(phi_ref[...])
-    slope_ref[...] = (step_size * scale) * (1.0 - mask * mask)
 
 
 def main_kernel(
@@ -281,10 +328,13 @@
         own_ref[...] + from_a_ref[: 2 * fr].astype(f32) + from_b_ref[: 2 * fr].astype(f32)
     )
     s_re, s_im = spec[:fr], spec[fr:]
+    unit = 16 * count
     for k in range(count):
         k_re, k_im = k_re_ref[k], k_im_ref[k]
         g = jnp.concatenate([k_re * s_re - k_im * s_im, k_re * s_im + k_im * s_re], axis=0)
-        q_ref[k * 2 * rows : (k + 1) * 2 * rows] = dot(inner_t_ref[...], g.astype(bf)).astype(bf)
+        q = dot(inner_t_ref[...], g.astype(bf)).astype(bf)
+        for r in range(rows // 8):
+            q_ref[r * unit + 16 * k : r * unit + 16 * k + 16] = q[16 * r : 16 * r + 16]
 
     gain = 4.0 * slope_resist / count * scale
     norm = scale * scale / count
@@ -299,34 +349,41 @@
         right_half = slice(half + start, half + start + width)
         af = dot(q_ref[...], table_ref[:, left_half])
         db = dot(q_ref[...], table_ref[:, right_half])
-
-        def parts(k):
-            re = slice(2 * k * rows, (2 * k + 1) * rows)
-            im = slice((2 * k + 1) * rows, (2 * k + 2) * rows)
-            return af[re], db[im], af[im], db[re], re, im
-
-        even = 0.0
-        cross = 0.0
-        for k in range(count):
-            a, b, f, d, _, _ = parts(k)
-            even = even + ((a * a + f * f) + (d * d + b * b))
-            cross = cross + (a * b - d * f)
-        cross = 2.0 * cross
-        w_left = weight(even - cross, goal_ref[:, left_half])
-        w_right = weight(even + cross, goal_ref[:, right_half])
-        p_w = w_left + w_right
-        q_w = w_right - w_left
-        for k in range(count):
-            a, b, f, d, re, im = parts(k)
-            x_ref[re, left_half] = (p_w * a + q_w * b).astype(bf)
-            x_ref[im, left_half] = (p_w * f - q_w * d).astype(bf)
-            x_ref[re, right_half] = (p_w * d - q_w * f).astype(bf)
-            x_ref[im, right_half] = (q_w * a + p_w * b).astype(bf)
-
+        for r in range(rows // 8):
+
+            def parts(k):
+                at = r * unit + 16 * k
+                return af[at : at + 8], db[at + 8 : at + 16], af[at + 8 : at + 16], db[at : at + 8]
+
+            even = 0.0
+            cross = 0.0
+            for k in range(count):
+                a, b, f, d = parts(k)
+                even = even + ((a * a + f * f) + (d * d + b * b))
+                cross = cross + (a * b - d * f)
+            cross = 2.0 * cross
+            here = slice(8 * r, 8 * r + 8)
+            w_left = weight(even - cross, goal_ref[here, left_half])
+            w_right = weight(even + cross, goal_ref[here, right_half])
+            p_w = w_left + w_right
+            q_w = w_right - w_left
+            for k in range(count):
+                a, b, f, d = parts(k)
+                at = slice(r * unit + 16 * k, r * unit + 16 * k + 16)
+                x_ref[at, left_half] = jnp.concatenate(
+                    [p_w * a + q_w * b, p_w * f - q_w * d], axis=0
+                ).astype(bf)
+                x_ref[at, right_half] = jnp.concatenate(
+                    [p_w * d - q_w * f, q_w * a + p_w * b], axis=0
+                ).astype(bf)
+
+    q_ref[...] = dot_t(x_ref[...], table_ref[...]).astype(bf)
     y_re = 0.0
     y_im = 0.0
     for k in range(count):
-        u = dot_t(x_ref[k * 2 * rows : (k + 1) * 2 * rows], table_ref[...]).astype(bf)
+        u = jnp.concatenate(
+            [q_ref[r * unit + 16 * k : r * unit + 16 * k + 16] for r in range(rows // 8)], axis=0
+        )
         w = scale * dot(inner_ref[...], u)
         w_re, w_im = w[:fr], w[fr:]
         k_re, k_im = k_re_ref[k], k_im_ref[k]
@@ -523,21 +580,27 @@
     bf = jnp.bfloat16
     f32 = jnp.float32
     shape = jax.ShapeDtypeStruct
-    lanes = pltpu.VMEM((8, LANES), f32)
     packet = shape((2 * fr + HALO * (cols // fc), fc), bf)
     row_freqs = row_freqs.reshape(1, fr)
 
-    table, s_own, send_a, send_b = call(
+    table, s_own, send_a, send_b, phi, freqs = call(
         functools.partial(first_kernel, strips),
-        [shape((fc, cols), bf), shape((2 * fr, fc), f32), packet, packet],
+        [
+            shape((fc, cols), bf),
+            shape((2 * fr, fc), f32),
+            packet,
+            packet,
+            shape((rows, cols), f32),
+            shape((8, LANES), f32),
+        ],
         (phi, row_freqs, col_freqs.reshape(1, fc)),
-        kinds="hvv",
+        kinds="hhh",
         scratch=[
-            pltpu.VMEM((rows, cols), f32),
             pltpu.VMEM((rows, cols), bf),
             pltpu.VMEM((2 * rows, fc), bf),
-            lanes,
-            pltpu.SemaphoreType.DMA(()),
+            pltpu.VMEM((1, fr), jnp.int32),
+            pltpu.VMEM((1, fc), jnp.int32),
+            pltpu.SemaphoreType.DMA((3,)),
         ],
     )
     from_b = pair_up(send_b, False)
@@ -554,9 +617,14 @@
             shape((rows, cols), f32),
             shape((rows, cols), f32),
         ],
-        (defocus_ids, row_freqs, kernels, psi, phi, target),
-        kinds="svvvvv",
-        scratch=[lanes],
+        (defocus_ids, freqs, phi, kernels, psi, target),
+        kinds="svvhhh",
+        scratch=[
+            pltpu.VMEM(kernels.shape, f32),
+            pltpu.VMEM(psi.shape, f32),
+            pltpu.VMEM(target.shape, jnp.int32),
+            pltpu.SemaphoreType.DMA((3,)),
+        ],
         flops=4000000000,
     )
     (part,) = call(

time: 38.8 us -> 36 us (0.928)
  Pallas kernels: 11.2 us -> 9.46 us
  local copies, waits for them, and re-layouts: 6.49 us -> 5.44 us
    pallas_call x5, Pallas kernels: 11.2 us -> 9.46 us  [call(): pl.pallas_call(kernel, out_shape=outs, in_specs=[spec(kind) for kind in k...]
    unnamed x16 -> x12, local copies, waits for them, and re-layouts: 6.49 us -> 5.44 us
  transfers between devices with their start and end apart: 7 -> 7, of which waited for: 3 -> 3; matrix products, arithmetic and copies ran while one was open for 0% -> 0% of each run, Pallas kernels for 2% -> 4%
where the time goes in v4:
time: 36 us; the launch traced here: 35.6 us
  waiting for transfers between devices  10.4 us (29%)
  starting transfers between devices  9.58 us (27%)
  Pallas kernels  9.46 us (26%)
  local copies, waits for them, and re-layouts  5.44 us (15%)
  between operations  0.72 us (2%)
    pallas_call x5, Pallas kernels, call(): pl.pallas_call(kernel, out_shape=outs, in_specs=[spec(kind) for kind in k...  9.46 us
    ppermute x2, waiting for transfers between devices, on_device(): other = lax.ppermute(part, 'focus', [(i, i ^ step) for i in range(planes)])  7.52 us
    unnamed x12, local copies, waits for them, and re-layouts  5.44 us
    ppermute x2, starting transfers between devices, on_device(): other = lax.ppermute(part, 'focus', [(i, i ^ step) for i in range(planes)])  4.29 us
    ppermute x4, starting transfers between devices, pair_up(): return lax.ppermute(block, 'strip', pairs + [(b, a) for a, b in pairs])  3.93 us
    ppermute x1, waiting for transfers between devices, on_device(): lax.ppermute(payload, 'strip', [(i, (i - turn_by) % strips) for i in rang...  2.88 us
    ppermute x1, starting transfers between devices, on_device(): lax.ppermute(payload, 'strip', [(i, (i - turn_by) % strips) for i in rang...  1.35 us
  transfers between devices with their start and end apart: 7, of which 3 were waited for; matrix products, arithmetic and copies ran while one was open for 0% of the time, Pallas kernels for 4%

profile of v4, /device:TPU:0, one launch (start us, length us, event | category | flops | bytes accessed | tf_op | source)
XLA Modules:
  0.0 35.6 jit_solution(12890780874019541422)
XLA Ops:
  0.0 0.0 copy-start
  0.0 1.0 %copy-done = f32[64,2048]{1,0:T(8,128)S(1)} copy-done((f32[64,2048]{1,0:T(8,128)S(1)}, f32[64,2048]{1,0:T(8,128)}, u32[]{:S(2)}) %copy-start) | copy-done | bytes 524312
  1.0 0.0 copy-start.1
  1.0 0.7 %copy-done.1 = s32[512]{0:T(512)S(1)} copy-done((s32[512]{0:T(512)S(1)}, s32[512]{0:T(512)}, u32[]{:S(2)}) %copy-start.1) | copy-done | bytes 2072
  1.7 0.0 copy-start.2
  1.7 0.7 %copy-done.2 = s32[48]{0:T(128)S(1)} copy-done((s32[48]{0:T(128)S(1)}, s32[48]{0:T(128)}, u32[]{:S(2)}) %copy-start.2) | copy-done | bytes 216
  2.4 2.1 %shard_map.73 = (bf16[512,2048]{1,0:T(8,128)(2,1)S(1)}, f32[96,512]{1,0:T(8,128)S(1)}, bf16[104,512]{1,0:T(8,128)(2,1)S(1)}, bf16[104,512]{1,0:T(8,128)(2,1)S(1)...) custom-call(f32[64,2048]{1,0:T(8,128)S(1)} %copy-done, s32[1,48]{1,0:T(1,128)S(1)} %bitcast.3, s32[1,512]{1,0:T(1,128)S(1)} %bitcast.2), custom_call_target="tpu_custom_call" | custom-call | flops 1000000 | bytes 4194304 | tf_op jit(solution)/shard_map/pallas_call | solution.py:553
  4.5 0.6 %collective-permute-start = (bf16[104,512]{1,0:T(8,128)(2,1)S(1)}, bf16[104,512]{1,0:T(8,128)(2,1)S(1)}, u32[]{:S(2)}, u32[]{:S(2)}) collective-permute-start(bf16[104,512]{1,0:T(8,128)(2,1)S(1)} %get-tuple-element.24), channel_id=1, source_target_pairs={{0,4},{8,12},{4,0},{12,8},{1,5},{9,13},{5,1},{13,9},{2,6},{10,14},... | collective-permute-start | bytes 319496 | tf_op jit(solution)/shard_map/ppermute | solution.py:568
  5.0 2.6 %collective-permute-start.1 = (bf16[104,512]{1,0:T(8,128)(2,1)S(1)}, bf16[104,512]{1,0:T(8,128)(2,1)S(1)}, u32[]{:S(2)}, u32[]{:S(2)}) collective-permute-start(bf16[104,512]{1,0:T(8,128)(2,1)S(1)} %get-tuple-element.25), channel_id=1, source_target_pairs={{4,8},{12,0},{8,4},{0,12},{5,9},{13,1},{9,5},{1,13},{6,10},{14,2},... | collective-permute-start | bytes 319496 | tf_op jit(solution)/shard_map/ppermute | solution.py:568
  8.3 0.0 copy-start.3
  8.3 1.1 %copy-done.3 = f32[2,4,48,512]{3,2,1,0:T(8,128)S(1)} copy-done((f32[2,4,48,512]{3,2,1,0:T(8,128)S(1)}, f32[2,4,48,512]{3,2,1,0:T(8,128)}, u32[]{:S(2)}) %copy-start.3) | copy-done | bytes 786456
  9.4 0.0 copy-start.4
  9.4 1.0 %copy-done.4 = s32[64,2048]{1,0:T(8,128)S(1)} copy-done((s32[64,2048]{1,0:T(8,128)S(1)}, s32[64,2048]{1,0:T(8,128)}, u32[]{:S(2)}) %copy-start.4) | copy-done | bytes 524312
  10.4 0.0 copy-start.5
  10.4 0.9 %copy-done.5 = f32[48,512]{1,0:T(8,128)S(1)} copy-done((f32[48,512]{1,0:T(8,128)S(1)}, f32[48,512]{1,0:T(8,128)}, u32[]{:S(2)}) %copy-start.5) | copy-done | bytes 98328
  11.3 1.3 %shard_map.74 = (bf16[96,128]{1,0:T(8,128)(2,1)S(1)}, bf16[128,96]{1,0:T(8,128)(2,1)S(1)}, bf16[3,160,96]{2,1,0:T(8,128)(2,1)S(1)}, bf16[1,32,96]{2,1,0:T(8,128)...) custom-call(s32[1]{0:T(128)S(6)} %copy.8.defocus_ref, ...), custom_call_target="tpu_custom_call" | custom-call | flops 4000000000 | bytes 4194304 | tf_op jit(solution)/shard_map/pallas_call | solution.py:553
  12.6 0.0 collective-permute-done.from_a_ref
  12.6 0.0 collective-permute-done.1.from_b_ref
  12.7 3.3 %shard_map.75 = bf16[96,512]{1,0:T(8,128)(2,1)S(1)} custom-call(f32[96,512]{1,0:T(8,128)S(1)} %get-tuple-element.28.own_ref, bf16[104,512]{1,0:T(8,128)(2,1)S(1)} %collective-permute-done.from_a_ref, bf16[104,512]{1,0:T(8,128)(2,1)S(1)} %collective-permute-done.1.from_b_ref, f32[64,2048]{1,0:T(8,128)S(1)} %get-tuple-element.29.goal_ref, ...), custom_call_target="tpu_custom_call" | custom-call | flops 4000000000 | bytes 4194304 | tf_op jit(solution)/shard_map/pallas_call | solution.py:553
  15.9 1.6 %collective-permute-start.2 = (bf16[96,512]{1,0:T(8,128)(2,1)S(1)}, bf16[96,512]{1,0:T(8,128)(2,1)S(1)}, u32[]{:S(2)}, u32[]{:S(2)}) collective-permute-start(bf16[96,512]{1,0:T(8,128)(2,1)S(1)} %shard_map.75), channel_id=1, source_target_pairs={{0,1},{1,0},{2,3},{3,2},{4,5},{5,4},{6,7},{7,6},{8,9},{9,8},{10,11... | collective-permute-start | bytes 294920 | tf_op jit(solution)/shard_map/ppermute | solution.py:647
  17.5 3.2 %collective-permute-done.2 = bf16[96,512]{1,0:T(8,128)(2,1)S(1)} collective-permute-done((bf16[96,512]{1,0:T(8,128)(2,1)S(1)}, bf16[96,512]{1,0:T(8,128)(2,1)S(1)}, u32[]{:S(2)}, u32[]{:S(2)}) %collective-permute-start.2) | collective-permute-done | bytes 98336 | tf_op jit(solution)/shard_map/ppermute | solution.py:647
  20.8 2.7 %collective-permute-start.3 = (bf16[96,512]{1,0:T(8,128)(2,1)S(1)}, bf16[96,512]{1,0:T(8,128)(2,1)S(1)}, u32[]{:S(2)}, u32[]{:S(2)}) collective-permute-start(bf16[96,512]{1,0:T(8,128)(2,1)S(1)} %add_convert_fusion.part_ref), channel_id=1, source_target_pairs={{0,2},{1,3},{2,0},{3,1},{4,6},{5,7},{6,4},{7,5},{8,10},{9,11},{10,... | collective-permute-start | bytes 294920 | tf_op jit(solution)/shard_map/ppermute | solution.py:647
  23.5 4.3 %collective-permute-done.3.other_ref = bf16[96,512]{1,0:T(8,128)(2,1)S(1)} collective-permute-done((bf16[96,512]{1,0:T(8,128)(2,1)S(1)}, bf16[96,512]{1,0:T(8,128)(2,1)S(1)}, u32[]{:S(2)}, u32[]{:S(2)}) %collective-permute-start.3) | collective-permute-done | bytes 98336 | tf_op jit(solution)/shard_map/ppermute | solution.py:647
  27.8 0.1 shard_map.76
  27.9 0.0 collective-permute-start.5
  27.9 0.8 %collective-permute-start.4 = (bf16[96,512]{1,0:T(8,128)(2,1)S(1)}, bf16[96,512]{1,0:T(8,128)(2,1)S(1)}, u32[]{:S(2)}, u32[]{:S(2)}) collective-permute-start(bf16[96,512]{1,0:T(8,128)(2,1)S(1)} %get-tuple-element.35.y_own_ref), channel_id=1, source_target_pairs={{0,4},{8,12},{4,0},{12,8},{1,5},{9,13},{5,1},{13,9},{2,6},{10,14},... | collective-permute-start | bytes 294920 | tf_op jit(solution)/shard_map/ppermute | solution.py:568
  28.7 1.4 %collective-permute-start.6 = (bf16[32,512]{1,0:T(8,128)(2,1)S(1)}, bf16[32,512]{1,0:T(8,128)(2,1)S(1)}, u32[]{:S(2)}, u32[]{:S(2)}) collective-permute-start(bf16[32,512]{1,0:T(8,128)(2,1)S(1)} %get-tuple-element.36), channel_id=1, source_target_pairs={{0,8},{4,12},{8,0},{12,4},{1,9},{5,13},{9,1},{13,5},{2,10},{6,14},... | collective-permute-start | bytes 98312 | tf_op jit(solution)/shard_map/ppermute | solution.py:655
  30.1 2.9 %collective-permute-done.6.rest_0_ = bf16[32,512]{1,0:T(8,128)(2,1)S(1)} collective-permute-done((bf16[32,512]{1,0:T(8,128)(2,1)S(1)}, bf16[32,512]{1,0:T(8,128)(2,1)S(1)}, u32[]{:S(2)}, u32[]{:S(2)}) %collective-permute-start.6) | collective-permute-done | bytes 32800 | tf_op jit(solution)/shard_map/ppermute | solution.py:655
  32.9 0.0 collective-permute-done.5.y_b_ref
  32.9 0.0 collective-permute-done.4.y_a_ref
  33.0 2.7 %shard_map.77 = f32[64,2048]{1,0:T(8,128)} custom-call(f32[64,2048]{1,0:T(8,128)S(1)} %get-tuple-element.21.phi_ref, f32[64,2048]{1,0:T(8,128)S(1)} %get-tuple-element.23.slope_ref, bf16[104,512]{1,0:T(8,128)(2,1)S(1)} %collective-permute-done.from_a_ref, bf16[104,512]{1,0:T(8,128)(2,1)S(1)} %collective-permute-done.1.from_b_ref, ...), custom_call_target="tpu_custom_call" | custom-call | flops 1000000 | bytes 4194304 | tf_op jit(solution)/shard_map/pallas_call | solution.py:553
  (1 shorter events, 0.0 us)
Async XLA Ops:
  0.0 1.0 %copy-start = (f32[64,2048]{1,0:T(8,128)S(1)}, f32[64,2048]{1,0:T(8,128)}, u32[]{:S(2)}) copy-start(f32[64,2048]{1,0:T(8,128)} %phi_hbm.1) | copy-start | bytes 1572868
  1.0 0.7 %copy-start.1 = (s32[512]{0:T(512)S(1)}, s32[512]{0:T(512)}, u32[]{:S(2)}) copy-start(s32[512]{0:T(512)} %param.13) | copy-start | bytes 6148
  1.7 0.7 %copy-start.2 = (s32[48]{0:T(128)S(1)}, s32[48]{0:T(128)}, u32[]{:S(2)}) copy-start(s32[48]{0:T(128)} %param.12) | copy-start | bytes 580
  4.5 8.2 %collective-permute-start = (bf16[104,512]{1,0:T(8,128)(2,1)S(1)}, bf16[104,512]{1,0:T(8,128)(2,1)S(1)}, u32[]{:S(2)}, u32[]{:S(2)}) collective-permute-start(bf16[104,512]{1,0:T(8,128)(2,1)S(1)} %get-tuple-element.24), channel_id=1, source_target_pairs={{0,4},{8,12},{4,0},{12,8},{1,5},{9,13},{5,1},{13,9},{2,6},{10,14},... | collective-permute-start | bytes 319496 | tf_op jit(solution)/shard_map/ppermute | solution.py:568
  5.0 7.6 %collective-permute-start.1 = (bf16[104,512]{1,0:T(8,128)(2,1)S(1)}, bf16[104,512]{1,0:T(8,128)(2,1)S(1)}, u32[]{:S(2)}, u32[]{:S(2)}) collective-permute-start(bf16[104,512]{1,0:T(8,128)(2,1)S(1)} %get-tuple-element.25), channel_id=1, source_target_pairs={{4,8},{12,0},{8,4},{0,12},{5,9},{13,1},{9,5},{1,13},{6,10},{14,2},... | collective-permute-start | bytes 319496 | tf_op jit(solution)/shard_map/ppermute | solution.py:568
  8.3 1.1 %copy-start.3 = (f32[2,4,48,512]{3,2,1,0:T(8,128)S(1)}, f32[2,4,48,512]{3,2,1,0:T(8,128)}, u32[]{:S(2)}) copy-start(f32[2,4,48,512]{3,2,1,0:T(8,128)} %kernels_hbm.1) | copy-start | bytes 2359300
  9.4 1.0 %copy-start.4 = (s32[64,2048]{1,0:T(8,128)S(1)}, s32[64,2048]{1,0:T(8,128)}, u32[]{:S(2)}) copy-start(s32[64,2048]{1,0:T(8,128)} %target_hbm.1) | copy-start | bytes 1572868
  10.4 0.9 %copy-start.5 = (f32[48,512]{1,0:T(8,128)S(1)}, f32[48,512]{1,0:T(8,128)}, u32[]{:S(2)}) copy-start(f32[48,512]{1,0:T(8,128)} %psi_hbm.1) | copy-start | bytes 294916
  15.9 4.8 %collective-permute-start.2 = (bf16[96,512]{1,0:T(8,128)(2,1)S(1)}, bf16[96,512]{1,0:T(8,128)(2,1)S(1)}, u32[]{:S(2)}, u32[]{:S(2)}) collective-permute-start(bf16[96,512]{1,0:T(8,128)(2,1)S(1)} %shard_map.75), channel_id=1, source_target_pairs={{0,1},{1,0},{2,3},{3,2},{4,5},{5,4},{6,7},{7,6},{8,9},{9,8},{10,11... | collective-permute-start | bytes 294920 | tf_op jit(solution)/shard_map/ppermute | solution.py:647
  20.8 7.0 %collective-permute-start.3 = (bf16[96,512]{1,0:T(8,128)(2,1)S(1)}, bf16[96,512]{1,0:T(8,128)(2,1)S(1)}, u32[]{:S(2)}, u32[]{:S(2)}) collective-permute-start(bf16[96,512]{1,0:T(8,128)(2,1)S(1)} %add_convert_fusion.part_ref), channel_id=1, source_target_pairs={{0,2},{1,3},{2,0},{3,1},{4,6},{5,7},{6,4},{7,5},{8,10},{9,11},{10,... | collective-permute-start | bytes 294920 | tf_op jit(solution)/shard_map/ppermute | solution.py:647
  27.9 5.0 %collective-permute-start.5 = (bf16[96,512]{1,0:T(8,128)(2,1)S(1)}, bf16[96,512]{1,0:T(8,128)(2,1)S(1)}, u32[]{:S(2)}, u32[]{:S(2)}) collective-permute-start(bf16[96,512]{1,0:T(8,128)(2,1)S(1)} %get-tuple-element.35.y_own_ref), channel_id=1, source_target_pairs={{4,8},{12,0},{8,4},{0,12},{5,9},{13,1},{9,5},{1,13},{6,10},{14,2},... | collective-permute-start | bytes 294920 | tf_op jit(solution)/shard_map/ppermute | solution.py:568
  27.9 5.0 %collective-permute-start.4 = (bf16[96,512]{1,0:T(8,128)(2,1)S(1)}, bf16[96,512]{1,0:T(8,128)(2,1)S(1)}, u32[]{:S(2)}, u32[]{:S(2)}) collective-permute-start(bf16[96,512]{1,0:T(8,128)(2,1)S(1)} %get-tuple-element.35.y_own_ref), channel_id=1, source_target_pairs={{0,4},{8,12},{4,0},{12,8},{1,5},{9,13},{5,1},{13,9},{2,6},{10,14},... | collective-permute-start | bytes 294920 | tf_op jit(solution)/shard_map/ppermute | solution.py:568
  28.7 4.2 %collective-permute-start.6 = (bf16[32,512]{1,0:T(8,128)(2,1)S(1)}, bf16[32,512]{1,0:T(8,128)(2,1)S(1)}, u32[]{:S(2)}, u32[]{:S(2)}) collective-permute-start(bf16[32,512]{1,0:T(8,128)(2,1)S(1)} %get-tuple-element.36), channel_id=1, source_target_pairs={{0,8},{4,12},{8,0},{12,4},{1,9},{5,13},{9,1},{13,5},{2,10},{6,14},... | collective-permute-start | bytes 98312 | tf_op jit(solution)/shard_map/ppermute | solution.py:655

commit v5 on v4

--- a/solution.py
+++ b/solution.py
@@ -550,6 +550,10 @@
 def call(kernel, outs, args, kinds=None, out_kinds=None, scratch=(), limit=24, flops=1000000):
     kinds = kinds or "v" * len(args)
     out_kinds = out_kinds or "v" * len(outs)
+    args = [
+        pltpu.with_memory_space_constraint(arg, pltpu.HBM) if kind == "h" else arg
+        for kind, arg in zip(kinds, args)
+    ]
     return pl.pallas_call(
         kernel,
         out_shape=outs,

time: 36 us -> 33.6 us (0.933)
  local copies, waits for them, and re-layouts: 5.44 us -> 0 us
  waiting for transfers between devices: 10.4 us -> 12.7 us
  Pallas kernels: 9.46 us -> 10.4 us
    unnamed x12 -> x0, local copies, waits for them, and re-layouts: 5.44 us -> none
    ppermute x4, waiting for transfers between devices: 0.01 us -> 1.03 us  [pair_up(): return lax.ppermute(block, 'strip', pairs + [(b, a) for a, b in pairs])]
    pallas_call x5, Pallas kernels: 9.46 us -> 10.4 us  [call(): pl.pallas_call(kernel, out_shape=outs, in_specs=[spec(kind) for kind in k...]
    ppermute x1, starting transfers between devices: 1.35 us -> 0.49 us  [on_device(): lax.ppermute(payload, 'strip', [(i, (i - turn_by) % strips) for i in rang...]
    ppermute x4, starting transfers between devices: 3.93 us -> 4.79 us  [pair_up(): return lax.ppermute(block, 'strip', pairs + [(b, a) for a, b in pairs])]
    ppermute x1, waiting for transfers between devices: 2.88 us -> 3.65 us  [on_device(): lax.ppermute(payload, 'strip', [(i, (i - turn_by) % strips) for i in rang...]
    ppermute x2, waiting for transfers between devices: 7.52 us -> 8.05 us  [on_device(): other = lax.ppermute(part, 'focus', [(i, i ^ step) for i in range(planes)])]
  transfers between devices with their start and end apart: 7 -> 7, of which waited for: 3 -> 4; matrix products, arithmetic and copies ran while one was open for 0% -> 0% of each run, Pallas kernels for 4% -> 5%
where the time goes in v5:
time: 33.6 us; the launch traced here: 33.4 us
  waiting for transfers between devices  12.7 us (38%)
  Pallas kernels  10.4 us (31%)
  starting transfers between devices  9.59 us (29%)
  between operations  0.7 us (2%)
    pallas_call x5, Pallas kernels, call(): pl.pallas_call(kernel, out_shape=outs, in_specs=[spec(kind) for kind in k...  10.4 us
    ppermute x2, waiting for transfers between devices, on_device(): other = lax.ppermute(part, 'focus', [(i, i ^ step) for i in range(planes)])  8.05 us
    ppermute x4, starting transfers between devices, pair_up(): return lax.ppermute(block, 'strip', pairs + [(b, a) for a, b in pairs])  4.79 us
    ppermute x2, starting transfers between devices, on_device(): other = lax.ppermute(part, 'focus', [(i, i ^ step) for i in range(planes)])  4.31 us
    ppermute x1, waiting for transfers between devices, on_device(): lax.ppermute(payload, 'strip', [(i, (i - turn_by) % strips) for i in rang...  3.65 us
    ppermute x4, waiting for transfers between devices, pair_up(): return lax.ppermute(block, 'strip', pairs + [(b, a) for a, b in pairs])  1.03 us
  transfers between devices with their start and end apart: 7, of which 4 were waited for; matrix products, arithmetic and copies ran while one was open for 0% of the time, Pallas kernels for 5%

profile of v5, /device:TPU:0, one launch (start us, length us, event | category | flops | bytes accessed | tf_op | source)
XLA Modules:
  0.0 33.4 jit_solution(8715993800365417918)
XLA Ops:
  0.0 2.7 %shard_map.73 = (bf16[512,2048]{1,0:T(8,128)(2,1)S(1)}, f32[96,512]{1,0:T(8,128)S(1)}, bf16[104,512]{1,0:T(8,128)(2,1)S(1)}, bf16[104,512]{1,0:T(8,128)(2,1)S(1)...) custom-call(f32[64,2048]{1,0:T(8,128)} %phi_hbm.1, s32[1,48]{1,0:T(1,128)} %bitcast.3, s32[1,512]{1,0:T(1,128)} %bitcast.2), custom_call_target="tpu_custom_call" | custom-call | flops 1000000 | bytes 4194304 | tf_op jit(solution)/shard_map/pallas_call | solution.py:557
  2.7 0.6 %collective-permute-start = (bf16[104,512]{1,0:T(8,128)(2,1)S(1)}, bf16[104,512]{1,0:T(8,128)(2,1)S(1)}, u32[]{:S(2)}, u32[]{:S(2)}) collective-permute-start(bf16[104,512]{1,0:T(8,128)(2,1)S(1)} %get-tuple-element.24), channel_id=1, source_target_pairs={{0,4},{8,12},{4,0},{12,8},{1,5},{9,13},{5,1},{13,9},{2,6},{10,14},... | collective-permute-start | bytes 319496 | tf_op jit(solution)/shard_map/ppermute | solution.py:572
  3.3 2.6 %collective-permute-start.1 = (bf16[104,512]{1,0:T(8,128)(2,1)S(1)}, bf16[104,512]{1,0:T(8,128)(2,1)S(1)}, u32[]{:S(2)}, u32[]{:S(2)}) collective-permute-start(bf16[104,512]{1,0:T(8,128)(2,1)S(1)} %get-tuple-element.25), channel_id=1, source_target_pairs={{4,8},{12,0},{8,4},{0,12},{5,9},{13,1},{9,5},{1,13},{6,10},{14,2},... | collective-permute-start | bytes 319496 | tf_op jit(solution)/shard_map/ppermute | solution.py:572
  6.5 1.6 %shard_map.74 = (bf16[96,128]{1,0:T(8,128)(2,1)S(1)}, bf16[128,96]{1,0:T(8,128)(2,1)S(1)}, bf16[3,160,96]{2,1,0:T(8,128)(2,1)S(1)}, bf16[1,32,96]{2,1,0:T(8,128)...) custom-call(s32[1]{0:T(128)S(6)} %copy.8.defocus_ref, ...), custom_call_target="tpu_custom_call" | custom-call | flops 4000000000 | bytes 4194304 | tf_op jit(solution)/shard_map/pallas_call | solution.py:557
  8.1 0.0 collective-permute-done.from_a_ref
  8.1 1.0 %collective-permute-done.1.from_b_ref = bf16[104,512]{1,0:T(8,128)(2,1)S(1)} collective-permute-done((bf16[104,512]{1,0:T(8,128)(2,1)S(1)}, bf16[104,512]{1,0:T(8,128)(2,1)S(1)}, u32[]{:S(2)}, u32[]{:S(2)}) %collective-permute-start.1) | collective-permute-done | bytes 106528 | tf_op jit(solution)/shard_map/ppermute | solution.py:572
  9.1 3.3 %shard_map.75 = bf16[96,512]{1,0:T(8,128)(2,1)S(1)} custom-call(f32[96,512]{1,0:T(8,128)S(1)} %get-tuple-element.28.own_ref, bf16[104,512]{1,0:T(8,128)(2,1)S(1)} %collective-permute-done.from_a_ref, bf16[104,512]{1,0:T(8,128)(2,1)S(1)} %collective-permute-done.1.from_b_ref, f32[64,2048]{1,0:T(8,128)S(1)} %get-tuple-element.29.goal_ref, ...), custom_call_target="tpu_custom_call" | custom-call | flops 4000000000 | bytes 4194304 | tf_op jit(solution)/shard_map/pallas_call | solution.py:557
  12.4 1.5 %collective-permute-start.2 = (bf16[96,512]{1,0:T(8,128)(2,1)S(1)}, bf16[96,512]{1,0:T(8,128)(2,1)S(1)}, u32[]{:S(2)}, u32[]{:S(2)}) collective-permute-start(bf16[96,512]{1,0:T(8,128)(2,1)S(1)} %shard_map.75), channel_id=1, source_target_pairs={{0,1},{1,0},{2,3},{3,2},{4,5},{5,4},{6,7},{7,6},{8,9},{9,8},{10,11... | collective-permute-start | bytes 294920 | tf_op jit(solution)/shard_map/ppermute | solution.py:651
  13.9 3.4 %collective-permute-done.2 = bf16[96,512]{1,0:T(8,128)(2,1)S(1)} collective-permute-done((bf16[96,512]{1,0:T(8,128)(2,1)S(1)}, bf16[96,512]{1,0:T(8,128)(2,1)S(1)}, u32[]{:S(2)}, u32[]{:S(2)}) %collective-permute-start.2) | collective-permute-done | bytes 98336 | tf_op jit(solution)/shard_map/ppermute | solution.py:651
  17.3 2.8 %collective-permute-start.3 = (bf16[96,512]{1,0:T(8,128)(2,1)S(1)}, bf16[96,512]{1,0:T(8,128)(2,1)S(1)}, u32[]{:S(2)}, u32[]{:S(2)}) collective-permute-start(bf16[96,512]{1,0:T(8,128)(2,1)S(1)} %add_convert_fusion.part_ref), channel_id=1, source_target_pairs={{0,2},{1,3},{2,0},{3,1},{4,6},{5,7},{6,4},{7,5},{8,10},{9,11},{10,... | collective-permute-start | bytes 294920 | tf_op jit(solution)/shard_map/ppermute | solution.py:651
  20.1 4.7 %collective-permute-done.3.other_ref = bf16[96,512]{1,0:T(8,128)(2,1)S(1)} collective-permute-done((bf16[96,512]{1,0:T(8,128)(2,1)S(1)}, bf16[96,512]{1,0:T(8,128)(2,1)S(1)}, u32[]{:S(2)}, u32[]{:S(2)}) %collective-permute-start.3) | collective-permute-done | bytes 98336 | tf_op jit(solution)/shard_map/ppermute | solution.py:651
  24.8 0.1 shard_map.76
  24.9 0.0 collective-permute-start.5
  24.9 1.6 %collective-permute-start.4 = (bf16[96,512]{1,0:T(8,128)(2,1)S(1)}, bf16[96,512]{1,0:T(8,128)(2,1)S(1)}, u32[]{:S(2)}, u32[]{:S(2)}) collective-permute-start(bf16[96,512]{1,0:T(8,128)(2,1)S(1)} %get-tuple-element.35.y_own_ref), channel_id=1, source_target_pairs={{0,4},{8,12},{4,0},{12,8},{1,5},{9,13},{5,1},{13,9},{2,6},{10,14},... | collective-permute-start | bytes 294920 | tf_op jit(solution)/shard_map/ppermute | solution.py:572
  26.6 0.5 %collective-permute-start.6 = (bf16[32,512]{1,0:T(8,128)(2,1)S(1)}, bf16[32,512]{1,0:T(8,128)(2,1)S(1)}, u32[]{:S(2)}, u32[]{:S(2)}) collective-permute-start(bf16[32,512]{1,0:T(8,128)(2,1)S(1)} %get-tuple-element.36), channel_id=1, source_target_pairs={{0,8},{4,12},{8,0},{12,4},{1,9},{5,13},{9,1},{13,5},{2,10},{6,14},... | collective-permute-start | bytes 98312 | tf_op jit(solution)/shard_map/ppermute | solution.py:659
  27.1 3.7 %collective-permute-done.6.rest_0_ = bf16[32,512]{1,0:T(8,128)(2,1)S(1)} collective-permute-done((bf16[32,512]{1,0:T(8,128)(2,1)S(1)}, bf16[32,512]{1,0:T(8,128)(2,1)S(1)}, u32[]{:S(2)}, u32[]{:S(2)}) %collective-permute-start.6) | collective-permute-done | bytes 32800 | tf_op jit(solution)/shard_map/ppermute | solution.py:659
  30.7 0.0 collective-permute-done.5.y_b_ref
  30.7 0.0 collective-permute-done.4.y_a_ref
  30.7 2.7 %shard_map.77 = f32[64,2048]{1,0:T(8,128)} custom-call(f32[64,2048]{1,0:T(8,128)S(1)} %get-tuple-element.21.phi_ref, f32[64,2048]{1,0:T(8,128)S(1)} %get-tuple-element.23.slope_ref, bf16[104,512]{1,0:T(8,128)(2,1)S(1)} %collective-permute-done.from_a_ref, bf16[104,512]{1,0:T(8,128)(2,1)S(1)} %collective-permute-done.1.from_b_ref, ...), custom_call_target="tpu_custom_call" | custom-call | flops 1000000 | bytes 4194304 | tf_op jit(solution)/shard_map/pallas_call | solution.py:557
  (1 shorter events, 0.0 us)
Async XLA Ops:
  2.7 5.4 %collective-permute-start = (bf16[104,512]{1,0:T(8,128)(2,1)S(1)}, bf16[104,512]{1,0:T(8,128)(2,1)S(1)}, u32[]{:S(2)}, u32[]{:S(2)}) collective-permute-start(bf16[104,512]{1,0:T(8,128)(2,1)S(1)} %get-tuple-element.24), channel_id=1, source_target_pairs={{0,4},{8,12},{4,0},{12,8},{1,5},{9,13},{5,1},{13,9},{2,6},{10,14},... | collective-permute-start | bytes 319496 | tf_op jit(solution)/shard_map/ppermute | solution.py:572
  3.3 5.9 %collective-permute-start.1 = (bf16[104,512]{1,0:T(8,128)(2,1)S(1)}, bf16[104,512]{1,0:T(8,128)(2,1)S(1)}, u32[]{:S(2)}, u32[]{:S(2)}) collective-permute-start(bf16[104,512]{1,0:T(8,128)(2,1)S(1)} %get-tuple-element.25), channel_id=1, source_target_pairs={{4,8},{12,0},{8,4},{0,12},{5,9},{13,1},{9,5},{1,13},{6,10},{14,2},... | collective-permute-start | bytes 319496 | tf_op jit(solution)/shard_map/ppermute | solution.py:572
  12.4 4.9 %collective-permute-start.2 = (bf16[96,512]{1,0:T(8,128)(2,1)S(1)}, bf16[96,512]{1,0:T(8,128)(2,1)S(1)}, u32[]{:S(2)}, u32[]{:S(2)}) collective-permute-start(bf16[96,512]{1,0:T(8,128)(2,1)S(1)} %shard_map.75), channel_id=1, source_target_pairs={{0,1},{1,0},{2,3},{3,2},{4,5},{5,4},{6,7},{7,6},{8,9},{9,8},{10,11... | collective-permute-start | bytes 294920 | tf_op jit(solution)/shard_map/ppermute | solution.py:651
  17.3 7.5 %collective-permute-start.3 = (bf16[96,512]{1,0:T(8,128)(2,1)S(1)}, bf16[96,512]{1,0:T(8,128)(2,1)S(1)}, u32[]{:S(2)}, u32[]{:S(2)}) collective-permute-start(bf16[96,512]{1,0:T(8,128)(2,1)S(1)} %add_convert_fusion.part_ref), channel_id=1, source_target_pairs={{0,2},{1,3},{2,0},{3,1},{4,6},{5,7},{6,4},{7,5},{8,10},{9,11},{10,... | collective-permute-start | bytes 294920 | tf_op jit(solution)/shard_map/ppermute | solution.py:651
  24.9 5.8 %collective-permute-start.5 = (bf16[96,512]{1,0:T(8,128)(2,1)S(1)}, bf16[96,512]{1,0:T(8,128)(2,1)S(1)}, u32[]{:S(2)}, u32[]{:S(2)}) collective-permute-start(bf16[96,512]{1,0:T(8,128)(2,1)S(1)} %get-tuple-element.35.y_own_ref), channel_id=1, source_target_pairs={{4,8},{12,0},{8,4},{0,12},{5,9},{13,1},{9,5},{1,13},{6,10},{14,2},... | collective-permute-start | bytes 294920 | tf_op jit(solution)/shard_map/ppermute | solution.py:572
  24.9 5.8 %collective-permute-start.4 = (bf16[96,512]{1,0:T(8,128)(2,1)S(1)}, bf16[96,512]{1,0:T(8,128)(2,1)S(1)}, u32[]{:S(2)}, u32[]{:S(2)}) collective-permute-start(bf16[96,512]{1,0:T(8,128)(2,1)S(1)} %get-tuple-element.35.y_own_ref), channel_id=1, source_target_pairs={{0,4},{8,12},{4,0},{12,8},{1,5},{9,13},{5,1},{13,9},{2,6},{10,14},... | collective-permute-start | bytes 294920 | tf_op jit(solution)/shard_map/ppermute | solution.py:572
  26.6 4.1 %collective-permute-start.6 = (bf16[32,512]{1,0:T(8,128)(2,1)S(1)}, bf16[32,512]{1,0:T(8,128)(2,1)S(1)}, u32[]{:S(2)}, u32[]{:S(2)}) collective-permute-start(bf16[32,512]{1,0:T(8,128)(2,1)S(1)} %get-tuple-element.36), channel_id=1, source_target_pairs={{0,8},{4,12},{8,0},{12,4},{1,9},{5,13},{9,1},{13,5},{2,10},{6,14},... | collective-permute-start | bytes 98312 | tf_op jit(solution)/shard_map/ppermute | solution.py:659

commit v6 on v5

--- a/solution.py
+++ b/solution.py
@@ -135,18 +135,19 @@
     load_cols.start()
     load_rows.start()
     load_phi.start()
-    place, first, second, first_in, second_in = partners(strips)
+    _, first, second, first_in, second_in = partners(strips)
 
     load_cols.wait()
-    freqs = jnp.broadcast_to(col_freqs_ref[...].astype(jnp.float32), (8, fc)).T[:, :1]
+    freq_row = jnp.broadcast_to(col_freqs_ref[...].astype(jnp.float32), (8, fc))
+    step_row_c, step_row_s = turn(freq_row * float(LANES), float(cols))
+    freqs, steps_c, steps_s = freq_row.T[:, :1], step_row_c.T[:, :1], step_row_s.T[:, :1]
 
     def make_columns(start, number):
         f = freqs[start : start + number]
         spot = lax.broadcasted_iota(jnp.int32, (number, LANES), 1).astype(jnp.float32)
         c, s = turn(f * (2.0 * spot + 1.0), 2.0 * cols)
-        step_c, step_s = turn(f * float(LANES), float(cols))
-        step_c = jnp.broadcast_to(step_c, (number, LANES))
-        step_s = jnp.broadcast_to(step_s, (number, LANES))
+        step_c = jnp.broadcast_to(steps_c[start : start + number], (number, LANES))
+        step_s = jnp.broadcast_to(steps_s[start : start + number], (number, LANES))
         twice = 2.0 * step_c
         c_old, s_old = c, s
         here = slice(start, start + number)
@@ -270,17 +271,22 @@
     tall = rows + 2 * PAD
     for index, (offset, keep) in enumerate(((0, True), (first, first_in), (second, second_in))):
         tall_ref[index] = rows_from(offset, keep, -PAD, tall)[:, : 2 * fr].astype(bf)
-    for index, offsets in enumerate(groups.values()):
-        total = jnp.zeros((4 * PAD, LANES), jnp.float32)
+    shape = (4 * HALO, LANES)
+    index = lax.broadcasted_iota(jnp.int32, shape, 0)
+    imag_row = index >= 2 * HALO
+    index = jnp.where(imag_row, index - 2 * HALO, index)
+    low = index >= HALO
+    row = jnp.where(low, index + (rows - HALO), index - HALO)
+    imag = lax.broadcasted_iota(jnp.int32, shape, 1) >= fr
+    for group, offsets in enumerate(groups.values()):
+        total = jnp.zeros(shape, jnp.float32)
         for offset in offsets:
-            keep = (place - offset >= 0) & (place - offset < strips)
-            part = rows_from(offset, keep, -PAD if offset < 0 else rows, PAD)
-            nothing = jnp.zeros((PAD, LANES), jnp.float32)
-            if offset < 0:
-                total = total + jnp.concatenate([part[:PAD], nothing, part[PAD:], nothing], axis=0)
-            else:
-                total = total + jnp.concatenate([nothing, part[:PAD], nothing, part[PAD:]], axis=0)
-        far_ref[index] = total[:, : 2 * fr].astype(bf)
+            spot = row - offset * rows + MARGIN
+            keep = (spot >= 0) & (spot < window) & (low if offset > 0 else ~low)
+            keep = keep & (place - offset >= 0) & (place - offset < strips)
+            c, s = turn(across * spot.astype(jnp.float32), float(window))
+            total = total + jnp.where(keep, quarter(imag_row, imag, c, s), 0.0)
+        far_ref[group] = total[:, : 2 * fr].astype(bf)
 
     scale = 1.0 / float(window * cols) ** 0.5
     mask = jnp.tanh(phi_ref[...])
@@ -319,7 +325,7 @@
 ):
     rows, cols = goal_ref.shape
     half = cols // 2
-    count, fr, fc = k_re_ref.shape
+    count, fr, _ = k_re_ref.shape
     scale = 1.0 / float((rows + 2 * MARGIN) * cols) ** 0.5
     bf = jnp.bfloat16
     f32 = jnp.float32
@@ -414,9 +420,10 @@
     y_b_ref,
     *rest,
 ):
-    payload_refs = rest[:-6]
-    out_hbm, level_ref, next_ref, halo_ref, out_ref, sems = rest[-6:]
-    place, first, second, _, _ = partners(strips)
+    payload_refs = rest[:-10]
+    out_hbm, halo_ref, out_ref, sems = rest[-10:-6]
+    level_ref, level_across, level_both, next_ref, next_across, next_both = rest[-6:]
+    place, first, _, _, _ = partners(strips)
     rows, cols = phi_ref.shape
     half = cols // 2
     blocks = cols // LANES
@@ -429,20 +436,16 @@
 
     z = dot(tall_ref[0], y_own_ref[...])
     z = z + dot(tall_ref[1], y_a_ref[...]) + dot(tall_ref[2], y_b_ref[...])
-    for payload_ref in payload_refs:
-        far = payload_ref[...].astype(f32)
-        nothing = jnp.zeros((rows, fc), f32)
-        z = z + jnp.concatenate(
-            [
-                far[:PAD],
-                nothing,
-                far[PAD : 2 * PAD],
-                far[2 * PAD : 3 * PAD],
-                nothing,
-                far[3 * PAD :],
-            ],
-            axis=0,
-        )
+    if payload_refs:
+        down = lax.broadcasted_iota(jnp.int32, (2 * tall, 4 * HALO), 0)
+        index = lax.broadcasted_iota(jnp.int32, (2 * tall, 4 * HALO), 1)
+        imag = index >= 2 * HALO
+        index = jnp.where(imag, index - 2 * HALO, index)
+        goes = jnp.where(index < HALO, index + (PAD - HALO), index + (PAD + rows - HALO))
+        goes = jnp.where(imag, goes + tall, goes)
+        place_rows = jnp.where(down == goes, 1.0, 0.0).astype(bf)
+        for payload_ref in payload_refs:
+            z = z + dot(place_rows, payload_ref[...])
     z = z.astype(bf)
     even = dot(z[:tall], table_ref[:, :half])
     odd = dot(z[tall:], table_ref[:, half:])
@@ -481,61 +484,59 @@
         advance(blocks - 1 - b, mirrored(even[:, part] + odd[:, part]))
 
     lane = lax.broadcasted_iota(jnp.int32, (8, LANES), 1)
-
-    def sweep(source, first_row, store):
-        center, rise, turned = [], [], []
-        nothing = jnp.zeros((8, LANES), f32)
-        for b in range(blocks):
-            c = source[b, first_row : first_row + 8]
-            u = source[b, first_row + 1 : first_row + 9]
-            d = source[b, first_row - 1 : first_row + 7]
-            x = u - d
-            center.append(c)
-            rise.append((x, (u + d) - 2.0 * c))
-            turned.append(
-                (
-                    pltpu.roll(c, LANES - 1, 1),
-                    pltpu.roll(c, 1, 1),
-                    pltpu.roll(x, LANES - 1, 1),
-                    pltpu.roll(x, 1, 1),
-                )
-            )
-        for b in range(blocks):
-            after = turned[b + 1] if b + 1 < blocks else (nothing,) * 4
-            before = turned[b - 1] if b else (nothing,) * 4
-            right = jnp.where(lane == LANES - 1, after[0], turned[b][0])
-            left = jnp.where(lane == 0, before[1], turned[b][1])
-            x_right = jnp.where(lane == LANES - 1, after[2], turned[b][2])
-            x_left = jnp.where(lane == 0, before[3], turned[b][3])
-            c = center[b]
-            x, second_x = rise[b]
-            y = right - left
-            second_y = (right + left) - 2.0 * c
-            x_x = x * x
-            y_y = y * y
-            numer = second_x * y_y + second_y * x_x - (0.5 * x) * y * (x_right - x_left)
-            store(b, c + flow_rate * (numer / (4.0 + x_x + y_y)))
-
+    nothing = jnp.zeros((8, LANES), f32)
+
+    def beside(values):
+        ahead = [pltpu.roll(value, LANES - 1, 1) for value in values] + [nothing]
+        behind = [nothing] + [pltpu.roll(value, 1, 1) for value in values]
+        for b in range(len(values)):
+            right = jnp.where(lane == LANES - 1, ahead[b + 1], ahead[b])
+            left = jnp.where(lane == 0, behind[b], behind[b + 1])
+            yield right - left, right + left
+
+    def sweep(refs, at, b):
+        source, across_ref, both_ref = refs
+        here = slice(at, at + 8)
+        c = source[b, here]
+        up, down = source[b, at + 1 : at + 9], source[b, at - 1 : at + 7]
+        y = across_ref[b, here]
+        crossed = across_ref[b, at + 1 : at + 9] - across_ref[b, at - 1 : at + 7]
+        twice = c + c
+        x = up - down
+        second_x = (up + down) - twice
+        second_y = both_ref[b, here] - twice
+        x_x = x * x
+        y_y = y * y
+        numer = second_x * y_y + second_y * x_x - (0.5 * x) * y * crossed
+        return c + flow_rate * (numer / (4.0 + x_x + y_y))
+
+    levels = (level_ref, level_across, level_both)
+    nexts = (next_ref, next_across, next_both)
+
+    def fill(refs, at, values):
+        for b, (difference, total) in enumerate(beside(values)):
+            refs[1][b, at : at + 8] = difference
+            refs[2][b, at : at + 8] = total
+
+    for at in range(0, tall, 8):
+        fill(levels, at, [level_ref[b, at : at + 8] for b in range(blocks)])
     starts = list(range(PAD - 1, PAD + rows - 7, 8))
     if starts[-1] + 8 < PAD + rows + 1:
         starts.append(PAD + rows - 7)
     for at in starts:
-        spot = lax.broadcasted_iota(jnp.int32, (8, LANES), 0) + at
-        keep = ((spot >= PAD) | top_in) & ((spot < PAD + rows) | low_in)
-        edge = at < PAD or at + 8 > PAD + rows
-
-        def store_next(b, value):
-            next_ref[b, at : at + 8] = jnp.where(keep, value, 0.0) if edge else value
-
-        sweep(level_ref, at, store_next)
-
+        values = [sweep(levels, at, b) for b in range(blocks)]
+        if at < PAD or at + 8 > PAD + rows:
+            spot = lax.broadcasted_iota(jnp.int32, (8, LANES), 0) + at
+            keep = ((spot >= PAD) | top_in) & ((spot < PAD + rows) | low_in)
+            values = [jnp.where(keep, value, 0.0) for value in values]
+        for b in range(blocks):
+            next_ref[b, at : at + 8] = values[b]
+        fill(nexts, at, values)
     copies = []
     for index in range(rows // 8):
-
-        def store_out(b, value):
-            out_ref[8 * index : 8 * index + 8, b * LANES : (b + 1) * LANES] = value
-
-        sweep(next_ref, PAD + 8 * index, store_out)
+        here = slice(8 * index, 8 * index + 8)
+        for b in range(blocks):
+            out_ref[here, b * LANES : (b + 1) * LANES] = sweep(nexts, PAD + 8 * index, b)
         here = pl.ds(8 * index, 8)
         copies.append(pltpu.make_async_copy(out_ref.at[here], out_hbm.at[here], sems.at[index]))
         copies[-1].start()
@@ -574,7 +575,6 @@
 
 def on_device(phi, target, defocus_ids, kernels, psi, row_freqs, col_freqs):
     rows, cols = phi.shape
-    half = cols // 2
     fr, fc = psi.shape
     count = kernels.shape[1]
     strips = lax.axis_size("strip")
@@ -615,7 +615,7 @@
             shape((2 * fr, 2 * rows), bf),
             shape((2 * rows, 2 * fr), bf),
             shape((3, 2 * tall, 2 * fr), bf),
-            shape((max(1, len(groups)), 4 * PAD, 2 * fr), bf),
+            shape((max(1, len(groups)), 4 * HALO, 2 * fr), bf),
             shape((count, fr, fc), f32),
             shape((count, fr, fc), f32),
             shape((rows, cols), f32),
@@ -652,7 +652,7 @@
         step *= 2
     total, *payloads = call(
         sum_kernel,
-        [shape((2 * fr, fc), bf)] + [shape((4 * PAD, fc), bf)] * len(groups),
+        [shape((2 * fr, fc), bf)] + [shape((4 * HALO, fc), bf)] * len(groups),
         (part, other, far_t),
     )
     far = [
@@ -667,12 +667,11 @@
         (phi, slope, from_a, from_b, table, tall_t, total, y_a, y_b, *far),
         out_kinds="h",
         scratch=[
-            pltpu.VMEM((cols // LANES, tall, LANES), f32),
-            pltpu.VMEM((cols // LANES, tall, LANES), f32),
             pltpu.VMEM((2 * PAD, cols), f32),
             pltpu.VMEM((rows, cols), f32),
             pltpu.SemaphoreType.DMA((rows // 8,)),
-        ],
+        ]
+        + [pltpu.VMEM((cols // LANES, tall, LANES), f32)] * 6,
     )[0]
 
 

time: 33.6 us -> 33.1 us (0.985)
  waiting for transfers between devices: 12.7 us -> 12.2 us
    ppermute x1, waiting for transfers between devices: 3.65 us -> 3.15 us  [on_device(): lax.ppermute(payload, 'strip', [(i, (i - turn_by) % strips) for i in rang...]
where the time goes in v6:
time: 33.1 us; the launch traced here: 32.9 us
  waiting for transfers between devices  12.2 us (37%)
  Pallas kernels  10.3 us (31%)
  starting transfers between devices  9.64 us (29%)
  between operations  0.69 us (2%)
    pallas_call x5, Pallas kernels, call(): pl.pallas_call(kernel, out_shape=outs, in_specs=[spec(kind) for kind in k...  10.3 us
    ppermute x2, waiting for transfers between devices, on_device(): other = lax.ppermute(part, 'focus', [(i, i ^ step) for i in range(planes)])  8.05 us
    ppermute x4, starting transfers between devices, pair_up(): return lax.ppermute(block, 'strip', pairs + [(b, a) for a, b in pairs])  4.78 us
    ppermute x2, starting transfers between devices, on_device(): other = lax.ppermute(part, 'focus', [(i, i ^ step) for i in range(planes)])  4.35 us
    ppermute x1, waiting for transfers between devices, on_device(): lax.ppermute(payload, 'strip', [(i, (i - turn_by) % strips) for i in rang...  3.15 us
    ppermute x4, waiting for transfers between devices, pair_up(): return lax.ppermute(block, 'strip', pairs + [(b, a) for a, b in pairs])  1.03 us
  transfers between devices with their start and end apart: 7, of which 4 were waited for; matrix products, arithmetic and copies ran while one was open for 0% of the time, Pallas kernels for 5%

profile of v6, /device:TPU:0, one launch (start us, length us, event | category | flops | bytes accessed | tf_op | source)
XLA Modules:
  0.0 32.9 jit_solution(5737769247993790429)
XLA Ops:
  0.0 2.7 %shard_map.73 = (bf16[512,2048]{1,0:T(8,128)(2,1)S(1)}, f32[96,512]{1,0:T(8,128)S(1)}, bf16[104,512]{1,0:T(8,128)(2,1)S(1)}, bf16[104,512]{1,0:T(8,128)(2,1)S(1)...) custom-call(f32[64,2048]{1,0:T(8,128)} %phi_hbm.1, s32[1,48]{1,0:T(1,128)} %bitcast.3, s32[1,512]{1,0:T(1,128)} %bitcast.2), custom_call_target="tpu_custom_call" | custom-call | flops 1000000 | bytes 4194304 | tf_op jit(solution)/shard_map/pallas_call | solution.py:558
  2.7 0.6 %collective-permute-start = (bf16[104,512]{1,0:T(8,128)(2,1)S(1)}, bf16[104,512]{1,0:T(8,128)(2,1)S(1)}, u32[]{:S(2)}, u32[]{:S(2)}) collective-permute-start(bf16[104,512]{1,0:T(8,128)(2,1)S(1)} %get-tuple-element.24), channel_id=1, source_target_pairs={{0,4},{8,12},{4,0},{12,8},{1,5},{9,13},{5,1},{13,9},{2,6},{10,14},... | collective-permute-start | bytes 319496 | tf_op jit(solution)/shard_map/ppermute | solution.py:573
  3.3 2.6 %collective-permute-start.1 = (bf16[104,512]{1,0:T(8,128)(2,1)S(1)}, bf16[104,512]{1,0:T(8,128)(2,1)S(1)}, u32[]{:S(2)}, u32[]{:S(2)}) collective-permute-start(bf16[104,512]{1,0:T(8,128)(2,1)S(1)} %get-tuple-element.25), channel_id=1, source_target_pairs={{4,8},{12,0},{8,4},{0,12},{5,9},{13,1},{9,5},{1,13},{6,10},{14,2},... | collective-permute-start | bytes 319496 | tf_op jit(solution)/shard_map/ppermute | solution.py:573
  6.5 1.6 %shard_map.74 = (bf16[96,128]{1,0:T(8,128)(2,1)S(1)}, bf16[128,96]{1,0:T(8,128)(2,1)S(1)}, bf16[3,160,96]{2,1,0:T(8,128)(2,1)S(1)}, bf16[1,8,96]{2,1,0:T(8,128)(...) custom-call(s32[1]{0:T(128)S(6)} %copy.8.defocus_ref, ...), custom_call_target="tpu_custom_call" | custom-call | flops 4000000000 | bytes 4194304 | tf_op jit(solution)/shard_map/pallas_call | solution.py:558
  8.1 0.0 collective-permute-done.from_a_ref
  8.1 1.0 %collective-permute-done.1.from_b_ref = bf16[104,512]{1,0:T(8,128)(2,1)S(1)} collective-permute-done((bf16[104,512]{1,0:T(8,128)(2,1)S(1)}, bf16[104,512]{1,0:T(8,128)(2,1)S(1)}, u32[]{:S(2)}, u32[]{:S(2)}) %collective-permute-start.1) | collective-permute-done | bytes 106528 | tf_op jit(solution)/shard_map/ppermute | solution.py:573
  9.1 3.2 %shard_map.75 = bf16[96,512]{1,0:T(8,128)(2,1)S(1)} custom-call(f32[96,512]{1,0:T(8,128)S(1)} %get-tuple-element.28.own_ref, bf16[104,512]{1,0:T(8,128)(2,1)S(1)} %collective-permute-done.from_a_ref, bf16[104,512]{1,0:T(8,128)(2,1)S(1)} %collective-permute-done.1.from_b_ref, f32[64,2048]{1,0:T(8,128)S(1)} %get-tuple-element.29.goal_ref, ...), custom_call_target="tpu_custom_call" | custom-call | flops 4000000000 | bytes 4194304 | tf_op jit(solution)/shard_map/pallas_call | solution.py:558
  12.4 1.5 %collective-permute-start.2 = (bf16[96,512]{1,0:T(8,128)(2,1)S(1)}, bf16[96,512]{1,0:T(8,128)(2,1)S(1)}, u32[]{:S(2)}, u32[]{:S(2)}) collective-permute-start(bf16[96,512]{1,0:T(8,128)(2,1)S(1)} %shard_map.75), channel_id=1, source_target_pairs={{0,1},{1,0},{2,3},{3,2},{4,5},{5,4},{6,7},{7,6},{8,9},{9,8},{10,11... | collective-permute-start | bytes 294920 | tf_op jit(solution)/shard_map/ppermute | solution.py:651
  13.9 3.4 %collective-permute-done.2 = bf16[96,512]{1,0:T(8,128)(2,1)S(1)} collective-permute-done((bf16[96,512]{1,0:T(8,128)(2,1)S(1)}, bf16[96,512]{1,0:T(8,128)(2,1)S(1)}, u32[]{:S(2)}, u32[]{:S(2)}) %collective-permute-start.2) | collective-permute-done | bytes 98336 | tf_op jit(solution)/shard_map/ppermute | solution.py:651
  17.3 2.8 %collective-permute-start.3 = (bf16[96,512]{1,0:T(8,128)(2,1)S(1)}, bf16[96,512]{1,0:T(8,128)(2,1)S(1)}, u32[]{:S(2)}, u32[]{:S(2)}) collective-permute-start(bf16[96,512]{1,0:T(8,128)(2,1)S(1)} %add_convert_fusion.part_ref), channel_id=1, source_target_pairs={{0,2},{1,3},{2,0},{3,1},{4,6},{5,7},{6,4},{7,5},{8,10},{9,11},{10,... | collective-permute-start | bytes 294920 | tf_op jit(solution)/shard_map/ppermute | solution.py:651
  20.1 4.7 %collective-permute-done.3.other_ref = bf16[96,512]{1,0:T(8,128)(2,1)S(1)} collective-permute-done((bf16[96,512]{1,0:T(8,128)(2,1)S(1)}, bf16[96,512]{1,0:T(8,128)(2,1)S(1)}, u32[]{:S(2)}, u32[]{:S(2)}) %collective-permute-start.3) | collective-permute-done | bytes 98336 | tf_op jit(solution)/shard_map/ppermute | solution.py:651
  24.8 0.1 shard_map.76
  24.9 0.0 collective-permute-start.5
  24.9 1.6 %collective-permute-start.4 = (bf16[96,512]{1,0:T(8,128)(2,1)S(1)}, bf16[96,512]{1,0:T(8,128)(2,1)S(1)}, u32[]{:S(2)}, u32[]{:S(2)}) collective-permute-start(bf16[96,512]{1,0:T(8,128)(2,1)S(1)} %get-tuple-element.35.y_own_ref), channel_id=1, source_target_pairs={{0,4},{8,12},{4,0},{12,8},{1,5},{9,13},{5,1},{13,9},{2,6},{10,14},... | collective-permute-start | bytes 294920 | tf_op jit(solution)/shard_map/ppermute | solution.py:573
  26.6 0.5 %collective-permute-start.6 = (bf16[8,512]{1,0:T(8,128)(2,1)S(1)}, bf16[8,512]{1,0:T(8,128)(2,1)S(1)}, u32[]{:S(2)}, u32[]{:S(2)}) collective-permute-start(bf16[8,512]{1,0:T(8,128)(2,1)S(1)} %get-tuple-element.36), channel_id=1, source_target_pairs={{0,8},{4,12},{8,0},{12,4},{1,9},{5,13},{9,1},{13,5},{2,10},{6,14},... | collective-permute-start | bytes 24584 | tf_op jit(solution)/shard_map/ppermute | solution.py:659
  27.1 3.1 %collective-permute-done.6.rest_0_ = bf16[8,512]{1,0:T(8,128)(2,1)S(1)} collective-permute-done((bf16[8,512]{1,0:T(8,128)(2,1)S(1)}, bf16[8,512]{1,0:T(8,128)(2,1)S(1)}, u32[]{:S(2)}, u32[]{:S(2)}) %collective-permute-start.6) | collective-permute-done | bytes 8224 | tf_op jit(solution)/shard_map/ppermute | solution.py:659
  30.2 0.0 collective-permute-done.5.y_b_ref
  30.2 0.0 collective-permute-done.4.y_a_ref
  30.2 2.7 %shard_map.77 = f32[64,2048]{1,0:T(8,128)} custom-call(f32[64,2048]{1,0:T(8,128)S(1)} %get-tuple-element.21.phi_ref, f32[64,2048]{1,0:T(8,128)S(1)} %get-tuple-element.23.slope_ref, bf16[104,512]{1,0:T(8,128)(2,1)S(1)} %collective-permute-done.from_a_ref, bf16[104,512]{1,0:T(8,128)(2,1)S(1)} %collective-permute-done.1.from_b_ref, ...), custom_call_target="tpu_custom_call" | custom-call | flops 1000000 | bytes 4194304 | tf_op jit(solution)/shard_map/pallas_call | solution.py:558
  (1 shorter events, 0.0 us)
Async XLA Ops:
  2.7 5.4 %collective-permute-start = (bf16[104,512]{1,0:T(8,128)(2,1)S(1)}, bf16[104,512]{1,0:T(8,128)(2,1)S(1)}, u32[]{:S(2)}, u32[]{:S(2)}) collective-permute-start(bf16[104,512]{1,0:T(8,128)(2,1)S(1)} %get-tuple-element.24), channel_id=1, source_target_pairs={{0,4},{8,12},{4,0},{12,8},{1,5},{9,13},{5,1},{13,9},{2,6},{10,14},... | collective-permute-start | bytes 319496 | tf_op jit(solution)/shard_map/ppermute | solution.py:573
  3.3 5.9 %collective-permute-start.1 = (bf16[104,512]{1,0:T(8,128)(2,1)S(1)}, bf16[104,512]{1,0:T(8,128)(2,1)S(1)}, u32[]{:S(2)}, u32[]{:S(2)}) collective-permute-start(bf16[104,512]{1,0:T(8,128)(2,1)S(1)} %get-tuple-element.25), channel_id=1, source_target_pairs={{4,8},{12,0},{8,4},{0,12},{5,9},{13,1},{9,5},{1,13},{6,10},{14,2},... | collective-permute-start | bytes 319496 | tf_op jit(solution)/shard_map/ppermute | solution.py:573
  12.4 4.9 %collective-permute-start.2 = (bf16[96,512]{1,0:T(8,128)(2,1)S(1)}, bf16[96,512]{1,0:T(8,128)(2,1)S(1)}, u32[]{:S(2)}, u32[]{:S(2)}) collective-permute-start(bf16[96,512]{1,0:T(8,128)(2,1)S(1)} %shard_map.75), channel_id=1, source_target_pairs={{0,1},{1,0},{2,3},{3,2},{4,5},{5,4},{6,7},{7,6},{8,9},{9,8},{10,11... | collective-permute-start | bytes 294920 | tf_op jit(solution)/shard_map/ppermute | solution.py:651
  17.3 7.5 %collective-permute-start.3 = (bf16[96,512]{1,0:T(8,128)(2,1)S(1)}, bf16[96,512]{1,0:T(8,128)(2,1)S(1)}, u32[]{:S(2)}, u32[]{:S(2)}) collective-permute-start(bf16[96,512]{1,0:T(8,128)(2,1)S(1)} %add_convert_fusion.part_ref), channel_id=1, source_target_pairs={{0,2},{1,3},{2,0},{3,1},{4,6},{5,7},{6,4},{7,5},{8,10},{9,11},{10,... | collective-permute-start | bytes 294920 | tf_op jit(solution)/shard_map/ppermute | solution.py:651
  24.9 5.3 %collective-permute-start.5 = (bf16[96,512]{1,0:T(8,128)(2,1)S(1)}, bf16[96,512]{1,0:T(8,128)(2,1)S(1)}, u32[]{:S(2)}, u32[]{:S(2)}) collective-permute-start(bf16[96,512]{1,0:T(8,128)(2,1)S(1)} %get-tuple-element.35.y_own_ref), channel_id=1, source_target_pairs={{4,8},{12,0},{8,4},{0,12},{5,9},{13,1},{9,5},{1,13},{6,10},{14,2},... | collective-permute-start | bytes 294920 | tf_op jit(solution)/shard_map/ppermute | solution.py:573
  24.9 5.3 %collective-permute-start.4 = (bf16[96,512]{1,0:T(8,128)(2,1)S(1)}, bf16[96,512]{1,0:T(8,128)(2,1)S(1)}, u32[]{:S(2)}, u32[]{:S(2)}) collective-permute-start(bf16[96,512]{1,0:T(8,128)(2,1)S(1)} %get-tuple-element.35.y_own_ref), channel_id=1, source_target_pairs={{0,4},{8,12},{4,0},{12,8},{1,5},{9,13},{5,1},{13,9},{2,6},{10,14},... | collective-permute-start | bytes 294920 | tf_op jit(solution)/shard_map/ppermute | solution.py:573
  26.6 3.7 %collective-permute-start.6 = (bf16[8,512]{1,0:T(8,128)(2,1)S(1)}, bf16[8,512]{1,0:T(8,128)(2,1)S(1)}, u32[]{:S(2)}, u32[]{:S(2)}) collective-permute-start(bf16[8,512]{1,0:T(8,128)(2,1)S(1)} %get-tuple-element.36), channel_id=1, source_target_pairs={{0,8},{4,12},{8,0},{12,4},{1,9},{5,13},{9,1},{13,5},{2,10},{6,14},... | collective-permute-start | bytes 24584 | tf_op jit(solution)/shard_map/ppermute | solution.py:659

commit v7 on v6

--- a/solution.py
+++ b/solution.py
@@ -14,6 +14,7 @@
 LANES = 128
 PAD = 8
 CHUNK = 256
+GROUP = 256
 
 slope_resist = 4.0
 level_resist = 0.5
@@ -119,7 +120,6 @@
     phi_ref,
     freq_ref,
     mask_ref,
-    p_ref,
     row_freqs_ref,
     col_freqs_ref,
     sems,
@@ -138,16 +138,44 @@
     _, first, second, first_in, second_in = partners(strips)
 
     load_cols.wait()
+    load_rows.wait()
+    row_freq_lanes(row_freqs_ref, freq_ref)
+    down = freq_ref[...].T[:fr, :1]
+    spot = lax.broadcasted_iota(jnp.int32, (fr, 2 * rows), 1)
+    later = spot >= rows
+    spot = jnp.where(later, spot - rows, spot)
+    c, s = turn(down * (spot + MARGIN).astype(jnp.float32), float(window))
+    turn_c, turn_s = turn(jnp.broadcast_to(down, c.shape) * float(rows), float(window))
+
+    def rows_in(c, s, offset, keep):
+        at = spot + MARGIN - offset * rows
+        keep = keep & (at >= 0) & (at < window)
+        c = jnp.where(keep, c, 0.0)
+        s = jnp.where(keep, s, 0.0)
+        return jnp.concatenate([jnp.where(later, s, c), jnp.where(later, c, -s)], axis=0).astype(bf)
+
+    sign = -first.astype(jnp.float32)
+    turn_s = sign * turn_s
+    in_all = jnp.concatenate(
+        [
+            rows_in(c * turn_c + s * turn_s, s * turn_c - c * turn_s, second, second_in),
+            rows_in(c * turn_c - s * turn_s, s * turn_c + c * turn_s, first, first_in),
+            rows_in(c, s, 0, True),
+        ],
+        axis=0,
+    )
+
     freq_row = jnp.broadcast_to(col_freqs_ref[...].astype(jnp.float32), (8, fc))
     step_row_c, step_row_s = turn(freq_row * float(LANES), float(cols))
-    freqs, steps_c, steps_s = freq_row.T[:, :1], step_row_c.T[:, :1], step_row_s.T[:, :1]
+    kind = lax.broadcasted_iota(jnp.int32, (8, fc), 0)
+    packed = jnp.where(kind == 0, freq_row, jnp.where(kind == 1, step_row_c, step_row_s)).T
 
     def make_columns(start, number):
-        f = freqs[start : start + number]
+        f = packed[start : start + number, 0:1]
         spot = lax.broadcasted_iota(jnp.int32, (number, LANES), 1).astype(jnp.float32)
         c, s = turn(f * (2.0 * spot + 1.0), 2.0 * cols)
-        step_c = jnp.broadcast_to(steps_c[start : start + number], (number, LANES))
-        step_s = jnp.broadcast_to(steps_s[start : start + number], (number, LANES))
+        step_c = jnp.broadcast_to(packed[start : start + number, 1:2], (number, LANES))
+        step_s = jnp.broadcast_to(packed[start : start + number, 2:3], (number, LANES))
         twice = 2.0 * step_c
         c_old, s_old = c, s
         here = slice(start, start + number)
@@ -161,53 +189,26 @@
 
     def transform(start, number):
         here = slice(start, start + number)
-        p_ref[:rows, here] = dot_t(mask_ref[:, :half], table_ref[here, :half]).astype(bf)
-        p_ref[rows:, here] = (-dot_t(mask_ref[:, half:], table_ref[here, half:])).astype(bf)
-
-    group = fc // 2
-    piece = 64
-    for start in range(0, group, piece):
-        make_columns(start, piece)
-    load_rows.wait()
-    load_phi.wait()
-    for b in range(half // LANES):
-        left = jnp.tanh(phi_ref[:, b * LANES : (b + 1) * LANES])
-        right = mirrored(jnp.tanh(phi_ref[:, cols - (b + 1) * LANES : cols - b * LANES]))
-        mask_ref[:, b * LANES : (b + 1) * LANES] = (left + right).astype(bf)
-        mask_ref[:, half + b * LANES : half + (b + 1) * LANES] = (left - right).astype(bf)
-    transform(0, group)
-    for start in range(group, fc, piece):
-        make_columns(start, piece)
-    transform(group, fc - group)
-
-    row_freq_lanes(row_freqs_ref, freq_ref)
-    down = freq_ref[...].T[:fr, :1]
-    spot = lax.broadcasted_iota(jnp.int32, (fr, 2 * rows), 1)
-    later = spot >= rows
-    spot = jnp.where(later, spot - rows, spot)
-    c, s = turn(down * (spot + MARGIN).astype(jnp.float32), float(window))
-    turn_c, turn_s = turn(down * float(rows), float(window))
-    turn_c = jnp.broadcast_to(turn_c, c.shape)
-    turn_s = jnp.broadcast_to(turn_s, c.shape)
-
-    def rows_in(c, s, offset, keep):
-        at = spot + MARGIN - offset * rows
-        keep = keep & (at >= 0) & (at < window)
-        c = jnp.where(keep, c, 0.0)
-        s = jnp.where(keep, s, 0.0)
-        return jnp.concatenate([jnp.where(later, s, c), jnp.where(later, c, -s)], axis=0).astype(bf)
-
-    in_own = rows_in(c, s, 0, True)
-    sign = -first.astype(jnp.float32)
-    in_a = rows_in(c * turn_c - s * (sign * turn_s), s * turn_c + c * (sign * turn_s), first, first_in)
-    in_b = rows_in(
-        c * turn_c + s * (sign * turn_s), s * turn_c - c * (sign * turn_s), second, second_in
-    )
-
-    p = p_ref[...]
-    send_b_ref[: 2 * fr] = dot(in_b, p).astype(bf)
-    send_a_ref[: 2 * fr] = dot(in_a, p).astype(bf)
-    own_ref[...] = dot(in_own, p)
+        p_re = dot_t(mask_ref[:, :half], table_ref[here, :half])
+        p_im = -dot_t(mask_ref[:, half:], table_ref[here, half:])
+        spec = dot(in_all, jnp.concatenate([p_re, p_im], axis=0).astype(bf))
+        send_b_ref[: 2 * fr, here] = spec[: 2 * fr].astype(bf)
+        send_a_ref[: 2 * fr, here] = spec[2 * fr : 4 * fr].astype(bf)
+        own_ref[:, here] = spec[4 * fr :]
+
+    group = min(GROUP, fc)
+    piece = min(64, group)
+    for start in range(0, fc, group):
+        for part in range(start, start + group, piece):
+            make_columns(part, piece)
+        if start == 0:
+            load_phi.wait()
+            for b in range(half // LANES):
+                left = jnp.tanh(phi_ref[:, b * LANES : (b + 1) * LANES])
+                right = mirrored(jnp.tanh(phi_ref[:, cols - (b + 1) * LANES : cols - b * LANES]))
+                mask_ref[:, b * LANES : (b + 1) * LANES] = (left + right).astype(bf)
+                mask_ref[:, half + b * LANES : half + (b + 1) * LANES] = (left - right).astype(bf)
+        transform(start, group)
     tops = [phi_ref[i : i + 1, q : q + fc] for i in range(HALO) for q in range(0, cols, fc)]
     lows = [
         phi_ref[rows - HALO + i : rows - HALO + i + 1, q : q + fc]
@@ -221,28 +222,22 @@
 
 
 def second_kernel(
-    strips,
-    groups,
     defocus_ref,
     freq_ref,
-    phi_ref,
     kernels_hbm,
     psi_hbm,
     target_hbm,
     inner_ref,
     inner_t_ref,
-    tall_ref,
-    far_ref,
     k_re_ref,
     k_im_ref,
     goal_ref,
-    slope_ref,
     kernels_ref,
     psi_ref,
     target_ref,
     sems,
 ):
-    rows, cols = phi_ref.shape
+    rows, cols = target_ref.shape
     half = cols // 2
     fr = psi_ref.shape[0]
     load_psi = pltpu.make_async_copy(psi_hbm, psi_ref, sems.at[0])
@@ -253,7 +248,6 @@
     load_target.start()
     window = rows + 2 * MARGIN
     bf = jnp.bfloat16
-    place, first, second, first_in, second_in = partners(strips)
     across = freq_ref[0:1, :]
     down = freq_ref[...].T[: 2 * fr, :1]
 
@@ -261,16 +255,38 @@
     table = interleaved(across, (2 * rows, LANES), 1, fr, MARGIN, window)
     inner_t_ref[...] = table[:, : 2 * fr].astype(bf)
 
-    def rows_from(offset, keep, first_row, number):
+    load_psi.wait()
+    middle = (LEVELS - 1) / 2.0
+    defocus = (defocus_ref[0].astype(jnp.float32) - middle) * (1.0 / middle)
+    turn_c, turn_s = cos_sin(psi_ref[...] * defocus)
+    load_kernels.wait()
+    for k in range(kernels_ref.shape[1]):
+        k_re_ref[k] = kernels_ref[0, k] * turn_c - kernels_ref[1, k] * turn_s
+        k_im_ref[k] = kernels_ref[0, k] * turn_s + kernels_ref[1, k] * turn_c
+
+    load_target.wait()
+    goal_ref[:, :half] = target_ref[:, :half].astype(jnp.float32)
+    for b in range(half // LANES):
+        goal_ref[:, half + b * LANES : half + (b + 1) * LANES] = mirrored(
+            target_ref[:, cols - (b + 1) * LANES : cols - b * LANES].astype(jnp.float32)
+        )
+
+
+def third_kernel(strips, groups, freq_ref, phi_ref, part_ref, tall_ref, far_ref, slope_ref):
+    rows, cols = phi_ref.shape
+    fr = part_ref.shape[0] // 2
+    window = rows + 2 * MARGIN
+    bf = jnp.bfloat16
+    place, first, second, first_in, second_in = partners(strips)
+    across = freq_ref[0:1, :]
+
+    tall = rows + 2 * PAD
+    for index, (offset, keep) in enumerate(((0, True), (first, first_in), (second, second_in))):
         table, spot = rotation(
-            across, (2 * number, LANES), number, 1, fr, first_row - offset * rows + MARGIN, window
+            across, (2 * tall, LANES), tall, 1, fr, MARGIN - PAD - offset * rows, window
         )
         keep = keep & (spot >= 0) & (spot < window)
-        return jnp.where(keep, table, 0.0)
-
-    tall = rows + 2 * PAD
-    for index, (offset, keep) in enumerate(((0, True), (first, first_in), (second, second_in))):
-        tall_ref[index] = rows_from(offset, keep, -PAD, tall)[:, : 2 * fr].astype(bf)
+        tall_ref[index] = jnp.where(keep, table, 0.0)[:, : 2 * fr].astype(bf)
     shape = (4 * HALO, LANES)
     index = lax.broadcasted_iota(jnp.int32, shape, 0)
     imag_row = index >= 2 * HALO
@@ -291,22 +307,6 @@
     scale = 1.0 / float(window * cols) ** 0.5
     mask = jnp.tanh(phi_ref[...])
     slope_ref[...] = (step_size * scale) * (1.0 - mask * mask)
-
-    load_psi.wait()
-    load_kernels.wait()
-    middle = (LEVELS - 1) / 2.0
-    defocus = (defocus_ref[0].astype(jnp.float32) - middle) * (1.0 / middle)
-    turn_c, turn_s = cos_sin(psi_ref[...] * defocus)
-    for k in range(kernels_ref.shape[1]):
-        k_re_ref[k] = kernels_ref[0, k] * turn_c - kernels_ref[1, k] * turn_s
-        k_im_ref[k] = kernels_ref[0, k] * turn_s + kernels_ref[1, k] * turn_c
-
-    load_target.wait()
-    goal_ref[:, :half] = target_ref[:, :half].astype(jnp.float32)
-    for b in range(half // LANES):
-        goal_ref[:, half + b * LANES : half + (b + 1) * LANES] = mirrored(
-            target_ref[:, cols - (b + 1) * LANES : cols - b * LANES].astype(jnp.float32)
-        )
 
 
 def main_kernel(
@@ -567,10 +567,18 @@
 
 
 def pair_up(block, first):
-    count = lax.axis_size("strip")
-    low = range(0 if first else 1, count, 2)
-    pairs = [(i, (i + 1) % count) for i in low]
-    return lax.ppermute(block, "strip", pairs + [(b, a) for a, b in pairs])
+    strips, planes = lax.axis_size("strip"), lax.axis_size("focus")
+    moves = []
+    for strip in range(strips):
+        up = (strip % 2 == 0) == first
+        partner = strip + 1 if up else strip - 1
+        for plane in range(planes):
+            here = strip * planes + plane
+            if 0 <= partner < strips:
+                moves.append((here, partner * planes + plane))
+            else:
+                moves.append((here, strip * planes + (plane ^ 1 if planes > 1 else plane)))
+    return lax.ppermute(block, ("strip", "focus"), moves)
 
 
 def on_device(phi, target, defocus_ids, kernels, psi, row_freqs, col_freqs):
@@ -601,7 +609,6 @@
         kinds="hhh",
         scratch=[
             pltpu.VMEM((rows, cols), bf),
-            pltpu.VMEM((2 * rows, fc), bf),
             pltpu.VMEM((1, fr), jnp.int32),
             pltpu.VMEM((1, fc), jnp.int32),
             pltpu.SemaphoreType.DMA((3,)),
@@ -609,20 +616,17 @@
     )
     from_b = pair_up(send_b, False)
     from_a = pair_up(send_a, True)
-    inner, inner_t, tall_t, far_t, k_re, k_im, goal, slope = call(
-        functools.partial(second_kernel, strips, groups),
+    inner, inner_t, k_re, k_im, goal = call(
+        second_kernel,
         [
             shape((2 * fr, 2 * rows), bf),
             shape((2 * rows, 2 * fr), bf),
-            shape((3, 2 * tall, 2 * fr), bf),
-            shape((max(1, len(groups)), 4 * HALO, 2 * fr), bf),
             shape((count, fr, fc), f32),
             shape((count, fr, fc), f32),
             shape((rows, cols), f32),
-            shape((rows, cols), f32),
         ],
-        (defocus_ids, freqs, phi, kernels, psi, target),
-        kinds="svvhhh",
+        (defocus_ids, freqs, kernels, psi, target),
+        kinds="svhhh",
         scratch=[
             pltpu.VMEM(kernels.shape, f32),
             pltpu.VMEM(psi.shape, f32),
@@ -640,6 +644,16 @@
             pltpu.VMEM((count * 2 * rows, cols), bf),
         ],
         flops=4000000000,
+    )
+    tall_t, far_t, slope = call(
+        functools.partial(third_kernel, strips, groups),
+        [
+            shape((3, 2 * tall, 2 * fr), bf),
+            shape((max(1, len(groups)), 4 * HALO, 2 * fr), bf),
+            shape((rows, cols), f32),
+        ],
+        (freqs, phi, part),
+        flops=2000000000,
     )
     step = 1
     other = jnp.zeros_like(part)

time: 33.1 us -> 32 us (0.967)
  waiting for transfers between devices: 12.2 us -> 11.3 us
  starting transfers between devices: 9.64 us -> 8.97 us
  Pallas kernels: 10.3 us -> 10.8 us
    ppermute x2, waiting for transfers between devices: 8.05 us -> 7.18 us  [on_device(): other = lax.ppermute(part, 'focus', [(i, i ^ step) for i in range(planes)])]
    ppermute x4, starting transfers between devices: 4.78 us -> 4.09 us  [pair_up(): return lax.ppermute(block, ('strip', 'focus'), moves)]
    ppermute x4, waiting for transfers between devices: 1.03 us -> 0.5 us  [pair_up(): return lax.ppermute(block, ('strip', 'focus'), moves)]
    ppermute x2, starting transfers between devices: 4.35 us -> 4.87 us  [on_device(): other = lax.ppermute(part, 'focus', [(i, i ^ step) for i in range(planes)])]
    ppermute x1, starting transfers between devices: 0.51 us -> 0.01 us  [on_device(): lax.ppermute(payload, 'strip', [(i, (i - turn_by) % strips) for i in rang...]
    ppermute x1, waiting for transfers between devices: 3.15 us -> 3.65 us  [on_device(): lax.ppermute(payload, 'strip', [(i, (i - turn_by) % strips) for i in rang...]
    pallas_call x5 -> x6, Pallas kernels: 10.3 us -> 10.8 us  [call(): pl.pallas_call(kernel, out_shape=outs, in_specs=[spec(kind) for kind in k...]
  transfers between devices with their start and end apart: 7 -> 7, of which waited for: 4 -> 5; matrix products, arithmetic and copies ran while one was open for 0% -> 0% of each run, Pallas kernels for 5% -> 6%
where the time goes in v7:
time: 32 us; the launch traced here: 31.8 us
  waiting for transfers between devices  11.3 us (35%)
  Pallas kernels  10.8 us (34%)
  starting transfers between devices  8.97 us (28%)
  between operations  0.7 us (2%)
    pallas_call x6, Pallas kernels, call(): pl.pallas_call(kernel, out_shape=outs, in_specs=[spec(kind) for kind in k...  10.8 us
    ppermute x2, waiting for transfers between devices, on_device(): other = lax.ppermute(part, 'focus', [(i, i ^ step) for i in range(planes)])  7.18 us
    ppermute x2, starting transfers between devices, on_device(): other = lax.ppermute(part, 'focus', [(i, i ^ step) for i in range(planes)])  4.87 us
    ppermute x4, starting transfers between devices, pair_up(): return lax.ppermute(block, ('strip', 'focus'), moves)  4.09 us
    ppermute x1, waiting for transfers between devices, on_device(): lax.ppermute(payload, 'strip', [(i, (i - turn_by) % strips) for i in rang...  3.65 us
  transfers between devices with their start and end apart: 7, of which 5 were waited for; matrix products, arithmetic and copies ran while one was open for 0% of the time, Pallas kernels for 6%

profile of v7, /device:TPU:0, one launch (start us, length us, event | category | flops | bytes accessed | tf_op | source)
XLA Modules:
  0.0 31.8 jit_solution(87673556379177450)
XLA Ops:
  0.0 2.7 %shard_map.73 = (bf16[512,2048]{1,0:T(8,128)(2,1)S(1)}, f32[96,512]{1,0:T(8,128)S(1)}, bf16[104,512]{1,0:T(8,128)(2,1)S(1)}, bf16[104,512]{1,0:T(8,128)(2,1)S(1)...) custom-call(f32[64,2048]{1,0:T(8,128)} %phi_hbm.1, s32[1,48]{1,0:T(1,128)} %bitcast.3, s32[1,512]{1,0:T(1,128)} %bitcast.2), custom_call_target="tpu_custom_call" | custom-call | flops 1000000 | bytes 4194304 | tf_op jit(solution)/shard_map/pallas_call | solution.py:558
  2.7 0.6 %collective-permute-start = (bf16[104,512]{1,0:T(8,128)(2,1)S(1)}, bf16[104,512]{1,0:T(8,128)(2,1)S(1)}, u32[]{:S(2)}, u32[]{:S(2)}) collective-permute-start(bf16[104,512]{1,0:T(8,128)(2,1)S(1)} %get-tuple-element.24), channel_id=1, source_target_pairs={{0,4},{1,5},{2,6},{3,7},{4,0},{5,1},{6,2},{7,3},{8,12},{9,13},{10,... | collective-permute-start | bytes 319496 | tf_op jit(solution)/shard_map/ppermute | solution.py:581
  3.2 2.6 %collective-permute-start.1 = (bf16[104,512]{1,0:T(8,128)(2,1)S(1)}, bf16[104,512]{1,0:T(8,128)(2,1)S(1)}, u32[]{:S(2)}, u32[]{:S(2)}) collective-permute-start(bf16[104,512]{1,0:T(8,128)(2,1)S(1)} %get-tuple-element.25), channel_id=1, source_target_pairs={{0,1},{1,0},{2,3},{3,2},{4,8},{5,9},{6,10},{7,11},{8,4},{9,5},{10,... | collective-permute-start | bytes 319496 | tf_op jit(solution)/shard_map/ppermute | solution.py:581
  6.5 1.6 %shard_map.74 = (bf16[96,128]{1,0:T(8,128)(2,1)S(1)}, bf16[128,96]{1,0:T(8,128)(2,1)S(1)}, f32[4,48,512]{2,1,0:T(8,128)S(1)}, f32[4,48,512]{2,1,0:T(8,128)S(1)}, f32[64,2048]{1,0:T(8,128)S(1)}) custom-call(s32[1]{0:T(128)S(6)} %copy.8.defocus_ref, f32[8,128]{1,0:T(8,128)S(1)} %get-tuple-element.22.freq_ref, f32[2,4,48,512]{3,2,1,0:T(8,128)} %kernels_hbm.1, ...), custom_call_target="tpu_custom_call" | custom-call | flops 4000000000 | bytes 4194304 | tf_op jit(solution)/shard_map/pallas_call | solution.py:558
  8.1 0.0 collective-permute-done.from_a_ref
  8.1 0.4 %collective-permute-done.1.from_b_ref = bf16[104,512]{1,0:T(8,128)(2,1)S(1)} collective-permute-done((bf16[104,512]{1,0:T(8,128)(2,1)S(1)}, bf16[104,512]{1,0:T(8,128)(2,1)S(1)}, u32[]{:S(2)}, u32[]{:S(2)}) %collective-permute-start.1) | collective-permute-done | bytes 106528 | tf_op jit(solution)/shard_map/ppermute | solution.py:581
  8.6 3.3 %shard_map.75.part_ref = bf16[96,512]{1,0:T(8,128)(2,1)S(1)} custom-call(f32[96,512]{1,0:T(8,128)S(1)} %get-tuple-element.23.own_ref, bf16[104,512]{1,0:T(8,128)(2,1)S(1)} %collective-permute-done.from_a_ref, bf16[104,512]{1,0:T(8,128)(2,1)S(1)} %collective-permute-done.1.from_b_ref, f32[64,2048]{1,0:T(8,128)S(1)} %get-tuple-element.26.goal_ref, ...), custom_call_target="tpu_custom_call" | custom-call | flops 4000000000 | bytes 4194304 | tf_op jit(solution)/shard_map/pallas_call | solution.py:558
  11.8 2.1 %collective-permute-start.2 = (bf16[96,512]{1,0:T(8,128)(2,1)S(1)}, bf16[96,512]{1,0:T(8,128)(2,1)S(1)}, u32[]{:S(2)}, u32[]{:S(2)}) collective-permute-start(bf16[96,512]{1,0:T(8,128)(2,1)S(1)} %shard_map.75.part_ref), channel_id=1, source_target_pairs={{0,1},{1,0},{2,3},{3,2},{4,5},{5,4},{6,7},{7,6},{8,9},{9,8},{10,11... | collective-permute-start | bytes 294920 | tf_op jit(solution)/shard_map/ppermute | solution.py:665
  13.9 3.1 %collective-permute-done.2 = bf16[96,512]{1,0:T(8,128)(2,1)S(1)} collective-permute-done((bf16[96,512]{1,0:T(8,128)(2,1)S(1)}, bf16[96,512]{1,0:T(8,128)(2,1)S(1)}, u32[]{:S(2)}, u32[]{:S(2)}) %collective-permute-start.2) | collective-permute-done | bytes 98336 | tf_op jit(solution)/shard_map/ppermute | solution.py:665
  17.0 2.8 %collective-permute-start.3 = (bf16[96,512]{1,0:T(8,128)(2,1)S(1)}, bf16[96,512]{1,0:T(8,128)(2,1)S(1)}, u32[]{:S(2)}, u32[]{:S(2)}) collective-permute-start(bf16[96,512]{1,0:T(8,128)(2,1)S(1)} %add_convert_fusion.part_ref), channel_id=1, source_target_pairs={{0,2},{1,3},{2,0},{3,1},{4,6},{5,7},{6,4},{7,5},{8,10},{9,11},{10,... | collective-permute-start | bytes 294920 | tf_op jit(solution)/shard_map/ppermute | solution.py:665
  19.8 0.4 %shard_map.76 = (bf16[3,160,96]{2,1,0:T(8,128)(2,1)S(1)}, bf16[1,8,96]{2,1,0:T(8,128)(2,1)S(1)}, f32[64,2048]{1,0:T(8,128)S(1)}) custom-call(f32[8,128]{1,0:T(8,128)S(1)} %get-tuple-element.22.freq_ref, f32[64,2048]{1,0:T(8,128)S(1)} %get-tuple-element.21.phi_ref, bf16[96,512]{1,0:T(8,128)(2,1)S(1)} %shard_map.75.part_ref), custom_call_target="tpu_custom_call" | custom-call | flops 2000000000 | bytes 4194304 | tf_op jit(solution)/shard_map/pallas_call | solution.py:558
  20.3 4.1 %collective-permute-done.3.other_ref = bf16[96,512]{1,0:T(8,128)(2,1)S(1)} collective-permute-done((bf16[96,512]{1,0:T(8,128)(2,1)S(1)}, bf16[96,512]{1,0:T(8,128)(2,1)S(1)}, u32[]{:S(2)}, u32[]{:S(2)}) %collective-permute-start.3) | collective-permute-done | bytes 98336 | tf_op jit(solution)/shard_map/ppermute | solution.py:665
  24.3 0.1 shard_map.77
  24.5 0.5 %collective-permute-start.5 = (bf16[96,512]{1,0:T(8,128)(2,1)S(1)}, bf16[96,512]{1,0:T(8,128)(2,1)S(1)}, u32[]{:S(2)}, u32[]{:S(2)}) collective-permute-start(bf16[96,512]{1,0:T(8,128)(2,1)S(1)} %get-tuple-element.35.y_own_ref), channel_id=1, source_target_pairs={{0,1},{1,0},{2,3},{3,2},{4,8},{5,9},{6,10},{7,11},{8,4},{9,5},{10,... | collective-permute-start | bytes 294920 | tf_op jit(solution)/shard_map/ppermute | solution.py:581
  25.0 0.4 %collective-permute-start.4 = (bf16[96,512]{1,0:T(8,128)(2,1)S(1)}, bf16[96,512]{1,0:T(8,128)(2,1)S(1)}, u32[]{:S(2)}, u32[]{:S(2)}) collective-permute-start(bf16[96,512]{1,0:T(8,128)(2,1)S(1)} %get-tuple-element.35.y_own_ref), channel_id=1, source_target_pairs={{0,4},{1,5},{2,6},{3,7},{4,0},{5,1},{6,2},{7,3},{8,12},{9,13},{10,... | collective-permute-start | bytes 294920 | tf_op jit(solution)/shard_map/ppermute | solution.py:581
  25.4 0.0 collective-permute-start.6
  25.4 3.6 %collective-permute-done.6.rest_0_ = bf16[8,512]{1,0:T(8,128)(2,1)S(1)} collective-permute-done((bf16[8,512]{1,0:T(8,128)(2,1)S(1)}, bf16[8,512]{1,0:T(8,128)(2,1)S(1)}, u32[]{:S(2)}, u32[]{:S(2)}) %collective-permute-start.6) | collective-permute-done | bytes 8224 | tf_op jit(solution)/shard_map/ppermute | solution.py:673
  29.0 0.1 collective-permute-done.5.y_b_ref
  29.1 0.0 collective-permute-done.4.y_a_ref
  29.1 2.7 %shard_map.78 = f32[64,2048]{1,0:T(8,128)} custom-call(f32[64,2048]{1,0:T(8,128)S(1)} %get-tuple-element.21.phi_ref, f32[64,2048]{1,0:T(8,128)S(1)} %get-tuple-element.32.slope_ref, bf16[104,512]{1,0:T(8,128)(2,1)S(1)} %collective-permute-done.from_a_ref, bf16[104,512]{1,0:T(8,128)(2,1)S(1)} %collective-permute-done.1.from_b_ref, ...), custom_call_target="tpu_custom_call" | custom-call | flops 1000000 | bytes 4194304 | tf_op jit(solution)/shard_map/pallas_call | solution.py:558
  (1 shorter events, 0.0 us)
Async XLA Ops:
  2.7 5.4 %collective-permute-start = (bf16[104,512]{1,0:T(8,128)(2,1)S(1)}, bf16[104,512]{1,0:T(8,128)(2,1)S(1)}, u32[]{:S(2)}, u32[]{:S(2)}) collective-permute-start(bf16[104,512]{1,0:T(8,128)(2,1)S(1)} %get-tuple-element.24), channel_id=1, source_target_pairs={{0,4},{1,5},{2,6},{3,7},{4,0},{5,1},{6,2},{7,3},{8,12},{9,13},{10,... | collective-permute-start | bytes 319496 | tf_op jit(solution)/shard_map/ppermute | solution.py:581
  3.2 5.3 %collective-permute-start.1 = (bf16[104,512]{1,0:T(8,128)(2,1)S(1)}, bf16[104,512]{1,0:T(8,128)(2,1)S(1)}, u32[]{:S(2)}, u32[]{:S(2)}) collective-permute-start(bf16[104,512]{1,0:T(8,128)(2,1)S(1)} %get-tuple-element.25), channel_id=1, source_target_pairs={{0,1},{1,0},{2,3},{3,2},{4,8},{5,9},{6,10},{7,11},{8,4},{9,5},{10,... | collective-permute-start | bytes 319496 | tf_op jit(solution)/shard_map/ppermute | solution.py:581
  11.8 5.2 %collective-permute-start.2 = (bf16[96,512]{1,0:T(8,128)(2,1)S(1)}, bf16[96,512]{1,0:T(8,128)(2,1)S(1)}, u32[]{:S(2)}, u32[]{:S(2)}) collective-permute-start(bf16[96,512]{1,0:T(8,128)(2,1)S(1)} %shard_map.75.part_ref), channel_id=1, source_target_pairs={{0,1},{1,0},{2,3},{3,2},{4,5},{5,4},{6,7},{7,6},{8,9},{9,8},{10,11... | collective-permute-start | bytes 294920 | tf_op jit(solution)/shard_map/ppermute | solution.py:665
  17.0 7.3 %collective-permute-start.3 = (bf16[96,512]{1,0:T(8,128)(2,1)S(1)}, bf16[96,512]{1,0:T(8,128)(2,1)S(1)}, u32[]{:S(2)}, u32[]{:S(2)}) collective-permute-start(bf16[96,512]{1,0:T(8,128)(2,1)S(1)} %add_convert_fusion.part_ref), channel_id=1, source_target_pairs={{0,2},{1,3},{2,0},{3,1},{4,6},{5,7},{6,4},{7,5},{8,10},{9,11},{10,... | collective-permute-start | bytes 294920 | tf_op jit(solution)/shard_map/ppermute | solution.py:665
  24.5 4.6 %collective-permute-start.5 = (bf16[96,512]{1,0:T(8,128)(2,1)S(1)}, bf16[96,512]{1,0:T(8,128)(2,1)S(1)}, u32[]{:S(2)}, u32[]{:S(2)}) collective-permute-start(bf16[96,512]{1,0:T(8,128)(2,1)S(1)} %get-tuple-element.35.y_own_ref), channel_id=1, source_target_pairs={{0,1},{1,0},{2,3},{3,2},{4,8},{5,9},{6,10},{7,11},{8,4},{9,5},{10,... | collective-permute-start | bytes 294920 | tf_op jit(solution)/shard_map/ppermute | solution.py:581
  25.0 4.1 %collective-permute-start.4 = (bf16[96,512]{1,0:T(8,128)(2,1)S(1)}, bf16[96,512]{1,0:T(8,128)(2,1)S(1)}, u32[]{:S(2)}, u32[]{:S(2)}) collective-permute-start(bf16[96,512]{1,0:T(8,128)(2,1)S(1)} %get-tuple-element.35.y_own_ref), channel_id=1, source_target_pairs={{0,4},{1,5},{2,6},{3,7},{4,0},{5,1},{6,2},{7,3},{8,12},{9,13},{10,... | collective-permute-start | bytes 294920 | tf_op jit(solution)/shard_map/ppermute | solution.py:581
  25.4 3.7 %collective-permute-start.6 = (bf16[8,512]{1,0:T(8,128)(2,1)S(1)}, bf16[8,512]{1,0:T(8,128)(2,1)S(1)}, u32[]{:S(2)}, u32[]{:S(2)}) collective-permute-start(bf16[8,512]{1,0:T(8,128)(2,1)S(1)} %get-tuple-element.36), channel_id=1, source_target_pairs={{0,8},{4,12},{8,0},{12,4},{1,9},{5,13},{9,1},{13,5},{2,10},{6,14},... | collective-permute-start | bytes 24584 | tf_op jit(solution)/shard_map/ppermute | solution.py:673

commit v8 on v7

--- a/solution.py
+++ b/solution.py
@@ -14,33 +14,36 @@
 LANES = 128
 PAD = 8
 CHUNK = 256
-GROUP = 256
+GROUPS = (4, 4)
 
 slope_resist = 4.0
 level_resist = 0.5
 step_size = 1.0
 flow_rate = 0.2
 
-SIN_TERMS = (1.0, -1.0 / 6, 1.0 / 120, -1.0 / 5040, 1.0 / 362880, -1.0 / 39916800)
-COS_TERMS = (1.0, -0.5, 1.0 / 24, -1.0 / 720, 1.0 / 40320, -1.0 / 3628800, 1.0 / 479001600)
-
-
-def cos_sin(angle):
-    half = 0.5 * angle
-    square = half * half
-    s = jnp.full_like(half, SIN_TERMS[-1])
-    for term in SIN_TERMS[-2::-1]:
+SIN_TERMS = (3.1415926401307073, -5.167710083507878, 2.550077523214199, -0.5982912856179897, 0.07765766030124945)
+COS_TERMS = (0.9999999532476078, -4.934792830619626, 4.0584113528622625, -1.3318765680789622, 0.2196896110945085)
+
+
+def cos_sin(t):
+    square = t * t
+    s = SIN_TERMS[-1] * square + SIN_TERMS[-2]
+    for term in SIN_TERMS[-3::-1]:
         s = s * square + term
-    s = s * half
-    c = jnp.full_like(half, COS_TERMS[-1])
-    for term in COS_TERMS[-2::-1]:
+    s = s * t
+    c = COS_TERMS[-1] * square + COS_TERMS[-2]
+    for term in COS_TERMS[-3::-1]:
         c = c * square + term
-    return 1.0 - 2.0 * s * s, 2.0 * s * c
+    twice = s + s
+    return 1.0 - twice * s, twice * c
 
 
 def turn(product, period):
+    if float(period).is_integer() and int(period) & (int(period) - 1) == 0:
+        t = product * (1.0 / period)
+        return cos_sin(t - jnp.round(t))
     rest = product - jnp.round(product * (1.0 / period)) * period
-    return cos_sin(rest * (2.0 * jnp.pi / period))
+    return cos_sin(rest * (1.0 / period))
 
 
 def mirrored(block):
@@ -196,9 +199,10 @@
         send_a_ref[: 2 * fr, here] = spec[2 * fr : 4 * fr].astype(bf)
         own_ref[:, here] = spec[4 * fr :]
 
-    group = min(GROUP, fc)
-    piece = min(64, group)
-    for start in range(0, fc, group):
+    piece = 64
+    start = 0
+    for share in GROUPS:
+        group = fc * share // 8
         for part in range(start, start + group, piece):
             make_columns(part, piece)
         if start == 0:
@@ -209,6 +213,7 @@
                 mask_ref[:, b * LANES : (b + 1) * LANES] = (left + right).astype(bf)
                 mask_ref[:, half + b * LANES : half + (b + 1) * LANES] = (left - right).astype(bf)
         transform(start, group)
+        start += group
     tops = [phi_ref[i : i + 1, q : q + fc] for i in range(HALO) for q in range(0, cols, fc)]
     lows = [
         phi_ref[rows - HALO + i : rows - HALO + i + 1, q : q + fc]
@@ -258,7 +263,7 @@
     load_psi.wait()
     middle = (LEVELS - 1) / 2.0
     defocus = (defocus_ref[0].astype(jnp.float32) - middle) * (1.0 / middle)
-    turn_c, turn_s = cos_sin(psi_ref[...] * defocus)
+    turn_c, turn_s = cos_sin(psi_ref[...] * (defocus * (0.5 / jnp.pi)))
     load_kernels.wait()
     for k in range(kernels_ref.shape[1]):
         k_re_ref[k] = kernels_ref[0, k] * turn_c - kernels_ref[1, k] * turn_s
@@ -272,9 +277,22 @@
         )
 
 
-def third_kernel(strips, groups, freq_ref, phi_ref, part_ref, tall_ref, far_ref, slope_ref):
+def third_kernel(
+    strips,
+    groups,
+    freq_ref,
+    phi_ref,
+    from_a_ref,
+    from_b_ref,
+    part_ref,
+    tall_ref,
+    far_ref,
+    slope_ref,
+    halo_ref,
+    halo_slope_ref,
+):
     rows, cols = phi_ref.shape
-    fr = part_ref.shape[0] // 2
+    fr, fc = part_ref.shape[0] // 2, part_ref.shape[1]
     window = rows + 2 * MARGIN
     bf = jnp.bfloat16
     place, first, second, first_in, second_in = partners(strips)
@@ -308,6 +326,28 @@
     mask = jnp.tanh(phi_ref[...])
     slope_ref[...] = (step_size * scale) * (1.0 - mask * mask)
 
+    halo_ref[...] = jnp.zeros_like(halo_ref)
+    edges_a = from_a_ref[2 * fr :].astype(jnp.float32)
+    edges_b = from_b_ref[2 * fr :].astype(jnp.float32)
+    top_in = (place > 0).astype(jnp.float32)
+    low_in = (place < strips - 1).astype(jnp.float32)
+    above = jnp.where(first < 0, edges_a, edges_b) * top_in
+    below = jnp.where(first < 0, edges_b, edges_a) * low_in
+    per_row = cols // fc
+    for i in range(HALO):
+        for q in range(per_row):
+            here = slice(q * fc, (q + 1) * fc)
+            spot = i * per_row + q
+            halo_ref[PAD - HALO + i : PAD - HALO + i + 1, here] = above[spot : spot + 1]
+            halo_ref[PAD + i : PAD + i + 1, here] = below[spot : spot + 1]
+    for edge, inside in ((0, top_in), (PAD, low_in)):
+        mask = jnp.tanh(halo_ref[edge : edge + PAD])
+        halo_slope_ref[edge : edge + PAD] = (step_size * scale) * inside * (1.0 - mask * mask)
+
+
+def own_kernel(tall_ref, y_ref, z_ref):
+    z_ref[...] = dot(tall_ref[0], y_ref[...])
+
 
 def main_kernel(
     own_ref,
@@ -411,31 +451,27 @@
     strips,
     phi_ref,
     slope_ref,
-    from_a_ref,
-    from_b_ref,
+    halo_ref,
+    halo_slope_ref,
     table_ref,
     tall_ref,
-    y_own_ref,
+    z_own_ref,
     y_a_ref,
     y_b_ref,
     *rest,
 ):
-    payload_refs = rest[:-10]
-    out_hbm, halo_ref, out_ref, sems = rest[-10:-6]
+    payload_refs = rest[:-9]
+    out_hbm, out_ref, sems = rest[-9:-6]
     level_ref, level_across, level_both, next_ref, next_across, next_both = rest[-6:]
-    place, first, _, _, _ = partners(strips)
+    place, _, _, _, _ = partners(strips)
     rows, cols = phi_ref.shape
     half = cols // 2
     blocks = cols // LANES
     tall = rows + 2 * PAD
-    fc = y_own_ref.shape[1]
-    lead = y_own_ref.shape[0]
     bf = jnp.bfloat16
     f32 = jnp.float32
-    scale = 1.0 / float((rows + 2 * MARGIN) * cols) ** 0.5
-
-    z = dot(tall_ref[0], y_own_ref[...])
-    z = z + dot(tall_ref[1], y_a_ref[...]) + dot(tall_ref[2], y_b_ref[...])
+
+    z = z_own_ref[...] + dot(tall_ref[1], y_a_ref[...]) + dot(tall_ref[2], y_b_ref[...])
     if payload_refs:
         down = lax.broadcasted_iota(jnp.int32, (2 * tall, 4 * HALO), 0)
         index = lax.broadcasted_iota(jnp.int32, (2 * tall, 4 * HALO), 1)
@@ -450,18 +486,6 @@
     even = dot(z[:tall], table_ref[:, :half])
     odd = dot(z[tall:], table_ref[:, half:])
 
-    halo_ref[...] = jnp.zeros_like(halo_ref)
-    edges_a = from_a_ref[lead:].astype(f32)
-    edges_b = from_b_ref[lead:].astype(f32)
-    above = jnp.where(first < 0, edges_a, edges_b)
-    below = jnp.where(first < 0, edges_b, edges_a)
-    per_row = cols // fc
-    for i in range(HALO):
-        for q in range(per_row):
-            here = slice(q * fc, (q + 1) * fc)
-            spot = i * per_row + q
-            halo_ref[PAD - HALO + i : PAD - HALO + i + 1, here] = above[spot : spot + 1]
-            halo_ref[PAD + i : PAD + i + 1, here] = below[spot : spot + 1]
     top_in = place > 0
     low_in = place < strips - 1
 
@@ -470,13 +494,9 @@
         level_ref[b, PAD : PAD + rows] = phi_ref[:, here] - slope_ref[:, here] * grad[
             PAD : PAD + rows
         ]
-        for inside, edge, to in ((top_in, 0, 0), (low_in, PAD, PAD + rows)):
-            phi = halo_ref[edge : edge + PAD, here]
-            mask = jnp.tanh(phi)
-            slope = (step_size * scale) * (1.0 - mask * mask)
-            level_ref[b, to : to + PAD] = jnp.where(
-                inside, phi - slope * grad[to : to + PAD], 0.0
-            )
+        for edge, to in ((0, 0), (PAD, PAD + rows)):
+            step = halo_slope_ref[edge : edge + PAD, here] * grad[to : to + PAD]
+            level_ref[b, to : to + PAD] = halo_ref[edge : edge + PAD, here] - step
 
     for b in range(half // LANES):
         part = slice(b * LANES, (b + 1) * LANES)
@@ -518,12 +538,13 @@
             refs[1][b, at : at + 8] = difference
             refs[2][b, at : at + 8] = total
 
-    for at in range(0, tall, 8):
+    def cover(first_row, end):
+        starts = list(range(first_row, end - 7, 8))
+        return starts if starts[-1] + 8 >= end else starts + [end - 8]
+
+    for at in cover(PAD - 2, PAD + rows + 2):
         fill(levels, at, [level_ref[b, at : at + 8] for b in range(blocks)])
-    starts = list(range(PAD - 1, PAD + rows - 7, 8))
-    if starts[-1] + 8 < PAD + rows + 1:
-        starts.append(PAD + rows - 7)
-    for at in starts:
+    for at in cover(PAD - 1, PAD + rows + 1):
         values = [sweep(levels, at, b) for b in range(blocks)]
         if at < PAD or at + 8 > PAD + rows:
             spot = lax.broadcasted_iota(jnp.int32, (8, LANES), 0) + at
@@ -645,14 +666,16 @@
         ],
         flops=4000000000,
     )
-    tall_t, far_t, slope = call(
+    tall_t, far_t, slope, halo, halo_slope = call(
         functools.partial(third_kernel, strips, groups),
         [
             shape((3, 2 * tall, 2 * fr), bf),
             shape((max(1, len(groups)), 4 * HALO, 2 * fr), bf),
             shape((rows, cols), f32),
+            shape((2 * PAD, cols), f32),
+            shape((2 * PAD, cols), f32),
         ],
-        (freqs, phi, part),
+        (freqs, phi, from_a, from_b, part),
         flops=2000000000,
     )
     step = 1
@@ -675,13 +698,13 @@
     ]
     y_b = pair_up(total, False)
     y_a = pair_up(total, True)
+    (z_own,) = call(own_kernel, [shape((2 * tall, fc), f32)], (tall_t, total), flops=2000000000)
     return call(
         functools.partial(final_kernel, strips),
         [shape((rows, cols), f32)],
-        (phi, slope, from_a, from_b, table, tall_t, total, y_a, y_b, *far),
+        (phi, slope, halo, halo_slope, table, tall_t, z_own, y_a, y_b, *far),
         out_kinds="h",
         scratch=[
-            pltpu.VMEM((2 * PAD, cols), f32),
             pltpu.VMEM((rows, cols), f32),
             pltpu.SemaphoreType.DMA((rows // 8,)),
         ]

time: 32 us -> 31.7 us (level)
    pallas_call x6 -> x7, Pallas kernels: 10.8 us -> 10.7 us  [call(): pl.pallas_call(kernel, out_shape=outs, in_specs=[spec(kind) for kind in k...]
  transfers between devices with their start and end apart: 7 -> 7, of which waited for: 5 -> 5; matrix products, arithmetic and copies ran while one was open for 0% -> 0% of each run, Pallas kernels for 6% -> 7%
where the time goes in v8:
time: 31.7 us; the launch traced here: 31.6 us
  waiting for transfers between devices  11.1 us (35%)
  Pallas kernels  10.7 us (34%)
  starting transfers between devices  8.98 us (28%)
  between operations  0.7 us (2%)
    pallas_call x7, Pallas kernels, call(): pl.pallas_call(kernel, out_shape=outs, in_specs=[spec(kind) for kind in k...  10.7 us
    ppermute x2, waiting for transfers between devices, on_device(): other = lax.ppermute(part, 'focus', [(i, i ^ step) for i in range(planes)])  7.17 us
    ppermute x2, starting transfers between devices, on_device(): other = lax.ppermute(part, 'focus', [(i, i ^ step) for i in range(planes)])  4.89 us
    ppermute x4, starting transfers between devices, pair_up(): return lax.ppermute(block, ('strip', 'focus'), moves)  4.09 us
    ppermute x1, waiting for transfers between devices, on_device(): lax.ppermute(payload, 'strip', [(i, (i - turn_by) % strips) for i in rang...  3.48 us
  transfers between devices with their start and end apart: 7, of which 5 were waited for; matrix products, arithmetic and copies ran while one was open for 0% of the time, Pallas kernels for 7%

profile of v8, /device:TPU:0, one launch (start us, length us, event | category | flops | bytes accessed | tf_op | source)
XLA Modules:
  0.0 31.6 jit_solution(5117074208283160292)
XLA Ops:
  0.0 2.6 %shard_map.73 = (bf16[512,2048]{1,0:T(8,128)(2,1)S(1)}, f32[96,512]{1,0:T(8,128)S(1)}, bf16[104,512]{1,0:T(8,128)(2,1)S(1)}, bf16[104,512]{1,0:T(8,128)(2,1)S(1)...) custom-call(f32[64,2048]{1,0:T(8,128)} %phi_hbm.1, s32[1,48]{1,0:T(1,128)} %bitcast.3, s32[1,512]{1,0:T(1,128)} %bitcast.2), custom_call_target="tpu_custom_call" | custom-call | flops 1000000 | bytes 4194304 | tf_op jit(solution)/shard_map/pallas_call | solution.py:579
  2.6 0.6 %collective-permute-start = (bf16[104,512]{1,0:T(8,128)(2,1)S(1)}, bf16[104,512]{1,0:T(8,128)(2,1)S(1)}, u32[]{:S(2)}, u32[]{:S(2)}) collective-permute-start(bf16[104,512]{1,0:T(8,128)(2,1)S(1)} %get-tuple-element.25), channel_id=1, source_target_pairs={{0,4},{1,5},{2,6},{3,7},{4,0},{5,1},{6,2},{7,3},{8,12},{9,13},{10,... | collective-permute-start | bytes 319496 | tf_op jit(solution)/shard_map/ppermute | solution.py:602
  3.1 2.6 %collective-permute-start.1 = (bf16[104,512]{1,0:T(8,128)(2,1)S(1)}, bf16[104,512]{1,0:T(8,128)(2,1)S(1)}, u32[]{:S(2)}, u32[]{:S(2)}) collective-permute-start(bf16[104,512]{1,0:T(8,128)(2,1)S(1)} %get-tuple-element.26), channel_id=1, source_target_pairs={{0,1},{1,0},{2,3},{3,2},{4,8},{5,9},{6,10},{7,11},{8,4},{9,5},{10,... | collective-permute-start | bytes 319496 | tf_op jit(solution)/shard_map/ppermute | solution.py:602
  6.4 1.6 %shard_map.74 = (bf16[96,128]{1,0:T(8,128)(2,1)S(1)}, bf16[128,96]{1,0:T(8,128)(2,1)S(1)}, f32[4,48,512]{2,1,0:T(8,128)S(1)}, f32[4,48,512]{2,1,0:T(8,128)S(1)}, f32[64,2048]{1,0:T(8,128)S(1)}) custom-call(s32[1]{0:T(128)S(6)} %copy.8.defocus_ref, f32[8,128]{1,0:T(8,128)S(1)} %get-tuple-element.24.freq_ref, f32[2,4,48,512]{3,2,1,0:T(8,128)} %kernels_hbm.1, ...), custom_call_target="tpu_custom_call" | custom-call | flops 4000000000 | bytes 4194304 | tf_op jit(solution)/shard_map/pallas_call | solution.py:579
  8.0 0.0 collective-permute-done.from_a_ref
  8.0 0.4 %collective-permute-done.1.from_b_ref = bf16[104,512]{1,0:T(8,128)(2,1)S(1)} collective-permute-done((bf16[104,512]{1,0:T(8,128)(2,1)S(1)}, bf16[104,512]{1,0:T(8,128)(2,1)S(1)}, u32[]{:S(2)}, u32[]{:S(2)}) %collective-permute-start.1) | collective-permute-done | bytes 106528 | tf_op jit(solution)/shard_map/ppermute | solution.py:602
  8.4 3.2 %shard_map.75.part_ref = bf16[96,512]{1,0:T(8,128)(2,1)S(1)} custom-call(f32[96,512]{1,0:T(8,128)S(1)} %get-tuple-element.27.own_ref, bf16[104,512]{1,0:T(8,128)(2,1)S(1)} %collective-permute-done.from_a_ref, bf16[104,512]{1,0:T(8,128)(2,1)S(1)} %collective-permute-done.1.from_b_ref, f32[64,2048]{1,0:T(8,128)S(1)} %get-tuple-element.28.goal_ref, ...), custom_call_target="tpu_custom_call" | custom-call | flops 4000000000 | bytes 4194304 | tf_op jit(solution)/shard_map/pallas_call | solution.py:579
  11.6 2.1 %collective-permute-start.2 = (bf16[96,512]{1,0:T(8,128)(2,1)S(1)}, bf16[96,512]{1,0:T(8,128)(2,1)S(1)}, u32[]{:S(2)}, u32[]{:S(2)}) collective-permute-start(bf16[96,512]{1,0:T(8,128)(2,1)S(1)} %shard_map.75.part_ref), channel_id=1, source_target_pairs={{0,1},{1,0},{2,3},{3,2},{4,5},{5,4},{6,7},{7,6},{8,9},{9,8},{10,11... | collective-permute-start | bytes 294920 | tf_op jit(solution)/shard_map/ppermute | solution.py:688
  13.7 3.1 %collective-permute-done.2 = bf16[96,512]{1,0:T(8,128)(2,1)S(1)} collective-permute-done((bf16[96,512]{1,0:T(8,128)(2,1)S(1)}, bf16[96,512]{1,0:T(8,128)(2,1)S(1)}, u32[]{:S(2)}, u32[]{:S(2)}) %collective-permute-start.2) | collective-permute-done | bytes 98336 | tf_op jit(solution)/shard_map/ppermute | solution.py:688
  16.8 2.8 %collective-permute-start.3 = (bf16[96,512]{1,0:T(8,128)(2,1)S(1)}, bf16[96,512]{1,0:T(8,128)(2,1)S(1)}, u32[]{:S(2)}, u32[]{:S(2)}) collective-permute-start(bf16[96,512]{1,0:T(8,128)(2,1)S(1)} %add_convert_fusion.part_ref), channel_id=1, source_target_pairs={{0,2},{1,3},{2,0},{3,1},{4,6},{5,7},{6,4},{7,5},{8,10},{9,11},{10,... | collective-permute-start | bytes 294920 | tf_op jit(solution)/shard_map/ppermute | solution.py:688
  19.6 0.4 %shard_map.76 = (bf16[3,160,96]{2,1,0:T(8,128)(2,1)S(1)}, bf16[1,8,96]{2,1,0:T(8,128)(2,1)S(1)}, f32[64,2048]{1,0:T(8,128)S(1)}, f32[16,2048]{1,0:T(8,128)S(1)}, f32[16,2048]{1,0:T(8,128)S(1)}) custom-call(f32[8,128]{1,0:T(8,128)S(1)} %get-tuple-element.24.freq_ref, f32[64,2048]{1,0:T(8,128)S(1)} %get-tuple-element.23.phi_ref, ...), custom_call_target="tpu_custom_call" | custom-call | flops 2000000000 | bytes 4194304 | tf_op jit(solution)/shard_map/pallas_call | solution.py:579
  20.1 4.1 %collective-permute-done.3.other_ref = bf16[96,512]{1,0:T(8,128)(2,1)S(1)} collective-permute-done((bf16[96,512]{1,0:T(8,128)(2,1)S(1)}, bf16[96,512]{1,0:T(8,128)(2,1)S(1)}, u32[]{:S(2)}, u32[]{:S(2)}) %collective-permute-start.3) | collective-permute-done | bytes 98336 | tf_op jit(solution)/shard_map/ppermute | solution.py:688
  24.2 0.1 shard_map.77
  24.3 0.5 %collective-permute-start.5 = (bf16[96,512]{1,0:T(8,128)(2,1)S(1)}, bf16[96,512]{1,0:T(8,128)(2,1)S(1)}, u32[]{:S(2)}, u32[]{:S(2)}) collective-permute-start(bf16[96,512]{1,0:T(8,128)(2,1)S(1)} %get-tuple-element.39.y_ref), channel_id=1, source_target_pairs={{0,1},{1,0},{2,3},{3,2},{4,8},{5,9},{6,10},{7,11},{8,4},{9,5},{10,... | collective-permute-start | bytes 294920 | tf_op jit(solution)/shard_map/ppermute | solution.py:602
  24.8 0.4 %collective-permute-start.4 = (bf16[96,512]{1,0:T(8,128)(2,1)S(1)}, bf16[96,512]{1,0:T(8,128)(2,1)S(1)}, u32[]{:S(2)}, u32[]{:S(2)}) collective-permute-start(bf16[96,512]{1,0:T(8,128)(2,1)S(1)} %get-tuple-element.39.y_ref), channel_id=1, source_target_pairs={{0,4},{1,5},{2,6},{3,7},{4,0},{5,1},{6,2},{7,3},{8,12},{9,13},{10,... | collective-permute-start | bytes 294920 | tf_op jit(solution)/shard_map/ppermute | solution.py:602
  25.2 0.0 collective-permute-start.6
  25.2 0.2 shard_map.78.z_own_ref
  25.4 3.5 %collective-permute-done.6.rest_0_ = bf16[8,512]{1,0:T(8,128)(2,1)S(1)} collective-permute-done((bf16[8,512]{1,0:T(8,128)(2,1)S(1)}, bf16[8,512]{1,0:T(8,128)(2,1)S(1)}, u32[]{:S(2)}, u32[]{:S(2)}) %collective-permute-start.6) | collective-permute-done | bytes 8224 | tf_op jit(solution)/shard_map/ppermute | solution.py:696
  28.9 0.1 collective-permute-done.5.y_b_ref
  28.9 0.0 collective-permute-done.4.y_a_ref
  28.9 2.6 %shard_map.79 = f32[64,2048]{1,0:T(8,128)} custom-call(f32[64,2048]{1,0:T(8,128)S(1)} %get-tuple-element.23.phi_ref, f32[64,2048]{1,0:T(8,128)S(1)} %get-tuple-element.34.slope_ref, f32[16,2048]{1,0:T(8,128)S(1)} %get-tuple-element.35.halo_ref, f32[16,2048]{1,0:T(8,128)S(1)} %get-tuple-element.36.halo_slope_ref, ...), custom_call_target="tpu_custom_call" | custom-call | flops 1000000 | bytes 4194304 | tf_op jit(solution)/shard_map/pallas_call | solution.py:579
  (1 shorter events, 0.0 us)
Async XLA Ops:
  2.6 5.5 %collective-permute-start = (bf16[104,512]{1,0:T(8,128)(2,1)S(1)}, bf16[104,512]{1,0:T(8,128)(2,1)S(1)}, u32[]{:S(2)}, u32[]{:S(2)}) collective-permute-start(bf16[104,512]{1,0:T(8,128)(2,1)S(1)} %get-tuple-element.25), channel_id=1, source_target_pairs={{0,4},{1,5},{2,6},{3,7},{4,0},{5,1},{6,2},{7,3},{8,12},{9,13},{10,... | collective-permute-start | bytes 319496 | tf_op jit(solution)/shard_map/ppermute | solution.py:602
  3.1 5.3 %collective-permute-start.1 = (bf16[104,512]{1,0:T(8,128)(2,1)S(1)}, bf16[104,512]{1,0:T(8,128)(2,1)S(1)}, u32[]{:S(2)}, u32[]{:S(2)}) collective-permute-start(bf16[104,512]{1,0:T(8,128)(2,1)S(1)} %get-tuple-element.26), channel_id=1, source_target_pairs={{0,1},{1,0},{2,3},{3,2},{4,8},{5,9},{6,10},{7,11},{8,4},{9,5},{10,... | collective-permute-start | bytes 319496 | tf_op jit(solution)/shard_map/ppermute | solution.py:602
  11.6 5.2 %collective-permute-start.2 = (bf16[96,512]{1,0:T(8,128)(2,1)S(1)}, bf16[96,512]{1,0:T(8,128)(2,1)S(1)}, u32[]{:S(2)}, u32[]{:S(2)}) collective-permute-start(bf16[96,512]{1,0:T(8,128)(2,1)S(1)} %shard_map.75.part_ref), channel_id=1, source_target_pairs={{0,1},{1,0},{2,3},{3,2},{4,5},{5,4},{6,7},{7,6},{8,9},{9,8},{10,11... | collective-permute-start | bytes 294920 | tf_op jit(solution)/shard_map/ppermute | solution.py:688
  16.8 7.3 %collective-permute-start.3 = (bf16[96,512]{1,0:T(8,128)(2,1)S(1)}, bf16[96,512]{1,0:T(8,128)(2,1)S(1)}, u32[]{:S(2)}, u32[]{:S(2)}) collective-permute-start(bf16[96,512]{1,0:T(8,128)(2,1)S(1)} %add_convert_fusion.part_ref), channel_id=1, source_target_pairs={{0,2},{1,3},{2,0},{3,1},{4,6},{5,7},{6,4},{7,5},{8,10},{9,11},{10,... | collective-permute-start | bytes 294920 | tf_op jit(solution)/shard_map/ppermute | solution.py:688
  24.3 4.6 %collective-permute-start.5 = (bf16[96,512]{1,0:T(8,128)(2,1)S(1)}, bf16[96,512]{1,0:T(8,128)(2,1)S(1)}, u32[]{:S(2)}, u32[]{:S(2)}) collective-permute-start(bf16[96,512]{1,0:T(8,128)(2,1)S(1)} %get-tuple-element.39.y_ref), channel_id=1, source_target_pairs={{0,1},{1,0},{2,3},{3,2},{4,8},{5,9},{6,10},{7,11},{8,4},{9,5},{10,... | collective-permute-start | bytes 294920 | tf_op jit(solution)/shard_map/ppermute | solution.py:602
  24.8 4.1 %collective-permute-start.4 = (bf16[96,512]{1,0:T(8,128)(2,1)S(1)}, bf16[96,512]{1,0:T(8,128)(2,1)S(1)}, u32[]{:S(2)}, u32[]{:S(2)}) collective-permute-start(bf16[96,512]{1,0:T(8,128)(2,1)S(1)} %get-tuple-element.39.y_ref), channel_id=1, source_target_pairs={{0,4},{1,5},{2,6},{3,7},{4,0},{5,1},{6,2},{7,3},{8,12},{9,13},{10,... | collective-permute-start | bytes 294920 | tf_op jit(solution)/shard_map/ppermute | solution.py:602
  25.2 3.7 %collective-permute-start.6 = (bf16[8,512]{1,0:T(8,128)(2,1)S(1)}, bf16[8,512]{1,0:T(8,128)(2,1)S(1)}, u32[]{:S(2)}, u32[]{:S(2)}) collective-permute-start(bf16[8,512]{1,0:T(8,128)(2,1)S(1)} %get-tuple-element.40), channel_id=1, source_target_pairs={{0,8},{4,12},{8,0},{12,4},{1,9},{5,13},{9,1},{13,5},{2,10},{6,14},... | collective-permute-start | bytes 24584 | tf_op jit(solution)/shard_map/ppermute | solution.py:696

commit v9 on v8

--- a/solution.py
+++ b/solution.py
@@ -224,6 +224,20 @@
     lows = jnp.concatenate(lows, axis=0)
     send_a_ref[2 * fr :] = jnp.where(first > 0, lows, tops).astype(bf)
     send_b_ref[2 * fr :] = jnp.where(second > 0, lows, tops).astype(bf)
+
+
+def defocus_kernel(defocus_ref, after_ref, out_ref):
+    middle = (LEVELS - 1) / 2.0
+    defocus = (defocus_ref[0].astype(jnp.float32) - middle) * (1.0 / middle)
+    out_ref[...] = jnp.full(out_ref.shape, defocus, jnp.float32)
+
+
+def kernels_at(defocus_ref, psi_ref, kernels_ref, k_re_ref, k_im_ref):
+    cycles = psi_ref[...] * (defocus_ref[0:1, 0:1] * (0.5 / jnp.pi))
+    turn_c, turn_s = cos_sin(cycles)
+    for k in range(kernels_ref.shape[1]):
+        k_re_ref[k] = kernels_ref[0, k] * turn_c - kernels_ref[1, k] * turn_s
+        k_im_ref[k] = kernels_ref[0, k] * turn_s + kernels_ref[1, k] * turn_c
 
 
 def second_kernel(
@@ -261,13 +275,8 @@
     inner_t_ref[...] = table[:, : 2 * fr].astype(bf)
 
     load_psi.wait()
-    middle = (LEVELS - 1) / 2.0
-    defocus = (defocus_ref[0].astype(jnp.float32) - middle) * (1.0 / middle)
-    turn_c, turn_s = cos_sin(psi_ref[...] * (defocus * (0.5 / jnp.pi)))
     load_kernels.wait()
-    for k in range(kernels_ref.shape[1]):
-        k_re_ref[k] = kernels_ref[0, k] * turn_c - kernels_ref[1, k] * turn_s
-        k_im_ref[k] = kernels_ref[0, k] * turn_s + kernels_ref[1, k] * turn_c
+    kernels_at(defocus_ref, psi_ref, kernels_ref, k_re_ref, k_im_ref)
 
     load_target.wait()
     goal_ref[:, :half] = target_ref[:, :half].astype(jnp.float32)
@@ -359,9 +368,7 @@
     inner_t_ref,
     k_re_ref,
     k_im_ref,
-    out_ref,
-    q_ref,
-    x_ref,
+    *rest,
 ):
     rows, cols = goal_ref.shape
     half = cols // 2
@@ -369,28 +376,37 @@
     scale = 1.0 / float((rows + 2 * MARGIN) * cols) ** 0.5
     bf = jnp.bfloat16
     f32 = jnp.float32
+    if len(rest) == 3:
+        out_ref, q_ref, x_ref = rest
+        planes = [(k_re_ref, k_im_ref, q_ref, x_ref)]
+    else:
+        other_ref, psi_ref, kernels_ref, out_ref = rest[:4]
+        q_ref, x_ref, q2_ref, x2_ref, k2_re_ref, k2_im_ref = rest[4:]
+        kernels_at(other_ref, psi_ref, kernels_ref, k2_re_ref, k2_im_ref)
+        planes = [(k_re_ref, k_im_ref, q_ref, x_ref), (k2_re_ref, k2_im_ref, q2_ref, x2_ref)]
 
     spec = scale * (
         own_ref[...] + from_a_ref[: 2 * fr].astype(f32) + from_b_ref[: 2 * fr].astype(f32)
     )
     s_re, s_im = spec[:fr], spec[fr:]
     unit = 16 * count
-    for k in range(count):
-        k_re, k_im = k_re_ref[k], k_im_ref[k]
-        g = jnp.concatenate([k_re * s_re - k_im * s_im, k_re * s_im + k_im * s_re], axis=0)
-        q = dot(inner_t_ref[...], g.astype(bf)).astype(bf)
-        for r in range(rows // 8):
-            q_ref[r * unit + 16 * k : r * unit + 16 * k + 16] = q[16 * r : 16 * r + 16]
-
     gain = 4.0 * slope_resist / count * scale
     norm = scale * scale / count
+    width = min(CHUNK, half)
 
     def weight(intensity, goal):
         resist = jax.nn.sigmoid(slope_resist * (norm * intensity - level_resist))
         return gain * (resist - goal) * resist * (1.0 - resist)
 
-    width = min(CHUNK, half)
-    for start in range(0, half, width):
+    def fields(k_re_ref, k_im_ref, q_ref):
+        for k in range(count):
+            k_re, k_im = k_re_ref[k], k_im_ref[k]
+            g = jnp.concatenate([k_re * s_re - k_im * s_im, k_re * s_im + k_im * s_re], axis=0)
+            q = dot(inner_t_ref[...], g.astype(bf)).astype(bf)
+            for r in range(rows // 8):
+                q_ref[r * unit + 16 * k : r * unit + 16 * k + 16] = q[16 * r : 16 * r + 16]
+
+    def weighted(q_ref, x_ref, start):
         left_half = slice(start, start + width)
         right_half = slice(half + start, half + start + width)
         af = dot(q_ref[...], table_ref[:, left_half])
@@ -423,18 +439,33 @@
                     [p_w * d - q_w * f, q_w * a + p_w * b], axis=0
                 ).astype(bf)
 
-    q_ref[...] = dot_t(x_ref[...], table_ref[...]).astype(bf)
+    def adjoint(k_re_ref, k_im_ref, q_ref, x_ref):
+        q_ref[...] = dot_t(x_ref[...], table_ref[...]).astype(bf)
+        y_re = 0.0
+        y_im = 0.0
+        for k in range(count):
+            u = jnp.concatenate(
+                [q_ref[r * unit + 16 * k : r * unit + 16 * k + 16] for r in range(rows // 8)],
+                axis=0,
+            )
+            w = scale * dot(inner_ref[...], u)
+            w_re, w_im = w[:fr], w[fr:]
+            k_re, k_im = k_re_ref[k], k_im_ref[k]
+            y_re = y_re + (k_re * w_re + k_im * w_im)
+            y_im = y_im + (k_re * w_im - k_im * w_re)
+        return y_re, y_im
+
+    for k_re_ref, k_im_ref, q_ref, x_ref in planes:
+        fields(k_re_ref, k_im_ref, q_ref)
+    for _, _, q_ref, x_ref in planes:
+        for start in range(0, half, width):
+            weighted(q_ref, x_ref, start)
     y_re = 0.0
     y_im = 0.0
-    for k in range(count):
-        u = jnp.concatenate(
-            [q_ref[r * unit + 16 * k : r * unit + 16 * k + 16] for r in range(rows // 8)], axis=0
-        )
-        w = scale * dot(inner_ref[...], u)
-        w_re, w_im = w[:fr], w[fr:]
-        k_re, k_im = k_re_ref[k], k_im_ref[k]
-        y_re = y_re + (k_re * w_re + k_im * w_im)
-        y_im = y_im + (k_re * w_im - k_im * w_re)
+    for plane in planes:
+        part_re, part_im = adjoint(*plane)
+        y_re = y_re + part_re
+        y_im = y_im + part_im
     out_ref[:fr] = y_re.astype(bf)
     out_ref[fr:] = y_im.astype(bf)
 
@@ -635,9 +666,16 @@
             pltpu.SemaphoreType.DMA((3,)),
         ],
     )
+    (defocus,) = call(
+        defocus_kernel, [shape((8, LANES), f32)], (defocus_ids, freqs), kinds="sv"
+    )
+    paired = planes > 1
     from_b = pair_up(send_b, False)
     from_a = pair_up(send_a, True)
-    inner, inner_t, k_re, k_im, goal = call(
+    if paired:
+        swap = [(i, i ^ (planes // 2)) for i in range(planes)]
+        other_defocus = lax.ppermute(defocus, "focus", swap)
+    inner, inner_t, k_re, k_im, goal, kernels_v, psi_v = call(
         second_kernel,
         [
             shape((2 * fr, 2 * rows), bf),
@@ -645,25 +683,28 @@
             shape((count, fr, fc), f32),
             shape((count, fr, fc), f32),
             shape((rows, cols), f32),
+            shape(kernels.shape, f32),
+            shape(psi.shape, f32),
         ],
-        (defocus_ids, freqs, kernels, psi, target),
-        kinds="svhhh",
+        (defocus, freqs, kernels, psi, target),
+        kinds="vvhhh",
         scratch=[
-            pltpu.VMEM(kernels.shape, f32),
-            pltpu.VMEM(psi.shape, f32),
             pltpu.VMEM(target.shape, jnp.int32),
             pltpu.SemaphoreType.DMA((3,)),
         ],
         flops=4000000000,
     )
+    scratch = [
+        pltpu.VMEM((count * 2 * rows, fc), bf),
+        pltpu.VMEM((count * 2 * rows, cols), bf),
+    ]
     (part,) = call(
         main_kernel,
         [shape((2 * fr, fc), bf)],
-        (s_own, from_a, from_b, goal, table, inner, inner_t, k_re, k_im),
-        scratch=[
-            pltpu.VMEM((count * 2 * rows, fc), bf),
-            pltpu.VMEM((count * 2 * rows, cols), bf),
-        ],
+        (s_own, from_a, from_b, goal, table, inner, inner_t, k_re, k_im)
+        + ((other_defocus, psi_v, kernels_v) if paired else ()),
+        scratch=scratch * 2 + [pltpu.VMEM((count, fr, fc), f32)] * 2 if paired else scratch,
+        limit=40,
         flops=4000000000,
     )
     tall_t, far_t, slope, halo, halo_slope = call(
@@ -680,7 +721,7 @@
     )
     step = 1
     other = jnp.zeros_like(part)
-    while step < planes:
+    while step < planes // 2:
         if step > 1:
             part = lax.optimization_barrier(
                 (part.astype(f32) + other.astype(f32)).astype(bf)

time: 31.7 us -> 31.5 us (level)
  waiting for transfers between devices: 11.1 us -> 7.69 us
  Pallas kernels: 10.7 us -> 13.9 us
    ppermute x2 -> x1, waiting for transfers between devices: 7.17 us -> 2.78 us  [on_device(): other = lax.ppermute(part, 'focus', [(i, i ^ step) for i in range(planes)])]
    ppermute x0 -> x1, starting transfers between devices: none -> 4.13 us  [on_device(): other_defocus = lax.ppermute(defocus, 'focus', swap)]
    ppermute x2 -> x1, starting transfers between devices: 4.89 us -> 1.65 us  [on_device(): other = lax.ppermute(part, 'focus', [(i, i ^ step) for i in range(planes)])]
    pallas_call x7 -> x8, Pallas kernels: 10.7 us -> 13.9 us  [call(): pl.pallas_call(kernel, out_shape=outs, in_specs=[spec(kind) for kind in k...]
    ppermute x4, waiting for transfers between devices: 0.5 us -> 1.44 us  [pair_up(): return lax.ppermute(block, ('strip', 'focus'), moves)]
    ppermute x4, starting transfers between devices: 4.09 us -> 3.16 us  [pair_up(): return lax.ppermute(block, ('strip', 'focus'), moves)]
  transfers between devices with their start and end apart: 7 -> 7, of which waited for: 5 -> 3; matrix products, arithmetic and copies ran while one was open for 0% -> 0% of each run, Pallas kernels for 7% -> 7%
where the time goes in v9:
time: 31.5 us; the launch traced here: 31.3 us
  Pallas kernels  13.9 us (44%)
  starting transfers between devices  8.94 us (28%)
  waiting for transfers between devices  7.69 us (24%)
  between operations  0.71 us (2%)
    pallas_call x8, Pallas kernels, call(): pl.pallas_call(kernel, out_shape=outs, in_specs=[spec(kind) for kind in k...  13.9 us
    ppermute x1, starting transfers between devices, on_device(): other_defocus = lax.ppermute(defocus, 'focus', swap)  4.13 us
    ppermute x1, waiting for transfers between devices, on_device(): lax.ppermute(payload, 'strip', [(i, (i - turn_by) % strips) for i in rang...  3.47 us
    ppermute x4, starting transfers between devices, pair_up(): return lax.ppermute(block, ('strip', 'focus'), moves)  3.16 us
    ppermute x1, waiting for transfers between devices, on_device(): other = lax.ppermute(part, 'focus', [(i, i ^ step) for i in range(planes)])  2.78 us
    ppermute x1, starting transfers between devices, on_device(): other = lax.ppermute(part, 'focus', [(i, i ^ step) for i in range(planes)])  1.65 us
    ppermute x4, waiting for transfers between devices, pair_up(): return lax.ppermute(block, ('strip', 'focus'), moves)  1.44 us
  transfers between devices with their start and end apart: 7, of which 3 were waited for; matrix products, arithmetic and copies ran while one was open for 0% of the time, Pallas kernels for 7%

profile of v9, /device:TPU:0, one launch (start us, length us, event | category | flops | bytes accessed | tf_op | source)
XLA Modules:
  0.0 31.3 jit_solution(2594306642501616428)
XLA Ops:
  0.7 2.6 %shard_map.73 = (bf16[512,2048]{1,0:T(8,128)(2,1)S(1)}, f32[96,512]{1,0:T(8,128)S(1)}, bf16[104,512]{1,0:T(8,128)(2,1)S(1)}, bf16[104,512]{1,0:T(8,128)(2,1)S(1)...) custom-call(f32[64,2048]{1,0:T(8,128)} %phi_hbm.1, s32[1,48]{1,0:T(1,128)} %bitcast.3, s32[1,512]{1,0:T(1,128)} %bitcast.2), custom_call_target="tpu_custom_call" | custom-call | flops 1000000 | bytes 4194304 | tf_op jit(solution)/shard_map/pallas_call | solution.py:610
  3.2 4.1 %collective-permute-start.2 = (f32[8,128]{1,0:T(8,128)S(1)}, f32[8,128]{1,0:T(8,128)S(1)}, u32[]{:S(2)}, u32[]{:S(2)}) collective-permute-start(f32[8,128]{1,0:T(8,128)S(1)} %shard_map.74.defocus_ref), channel_id=1, source_target_pairs={{0,2},{1,3},{2,0},{3,1},{4,6},{5,7},{6,4},{7,5},{8,10},{9,11},{10,... | collective-permute-start | bytes 12296 | tf_op jit(solution)/shard_map/ppermute | solution.py:677
  7.4 0.0 collective-permute-start
  7.4 1.6 %collective-permute-start.1 = (bf16[104,512]{1,0:T(8,128)(2,1)S(1)}, bf16[104,512]{1,0:T(8,128)(2,1)S(1)}, u32[]{:S(2)}, u32[]{:S(2)}) collective-permute-start(bf16[104,512]{1,0:T(8,128)(2,1)S(1)} %get-tuple-element.28), channel_id=1, source_target_pairs={{0,1},{1,0},{2,3},{3,2},{4,8},{5,9},{6,10},{7,11},{8,4},{9,5},{10,... | collective-permute-start | bytes 319496 | tf_op jit(solution)/shard_map/ppermute | solution.py:633
  9.0 1.7 %shard_map.75 = (bf16[96,128]{1,0:T(8,128)(2,1)S(1)}, bf16[128,96]{1,0:T(8,128)(2,1)S(1)}, f32[4,48,512]{2,1,0:T(8,128)S(1)}, f32[4,48,512]{2,1,0:T(8,128)S(1)},...) custom-call(f32[8,128]{1,0:T(8,128)S(1)} %shard_map.74.defocus_ref, ...), custom_call_target="tpu_custom_call" | custom-call | flops 4000000000 | bytes 4194304 | tf_op jit(solution)/shard_map/pallas_call | solution.py:610
  10.6 0.0 collective-permute-done.2.rest_0_
  10.6 0.0 collective-permute-done.from_a_ref
  10.7 1.4 %collective-permute-done.1.from_b_ref = bf16[104,512]{1,0:T(8,128)(2,1)S(1)} collective-permute-done((bf16[104,512]{1,0:T(8,128)(2,1)S(1)}, bf16[104,512]{1,0:T(8,128)(2,1)S(1)}, u32[]{:S(2)}, u32[]{:S(2)}) %collective-permute-start.1) | collective-permute-done | bytes 106528 | tf_op jit(solution)/shard_map/ppermute | solution.py:633
  12.1 6.3 %shard_map.76.part_ref = bf16[96,512]{1,0:T(8,128)(2,1)S(1)} custom-call(f32[96,512]{1,0:T(8,128)S(1)} %get-tuple-element.29.own_ref, bf16[104,512]{1,0:T(8,128)(2,1)S(1)} %collective-permute-done.from_a_ref, bf16[104,512]{1,0:T(8,128)(2,1)S(1)} %collective-permute-done.1.from_b_ref, f32[64,2048]{1,0:T(8,128)S(1)} %get-tuple-element.30.goal_ref, ...), custom_call_target="tpu_custom_call" | custom-call | flops 4000000000 | bytes 4194304 | tf_op jit(solution)/shard_map/pallas_call | solution.py:610
  18.4 1.7 %collective-permute-start.3 = (bf16[96,512]{1,0:T(8,128)(2,1)S(1)}, bf16[96,512]{1,0:T(8,128)(2,1)S(1)}, u32[]{:S(2)}, u32[]{:S(2)}) collective-permute-start(bf16[96,512]{1,0:T(8,128)(2,1)S(1)} %shard_map.76.part_ref), channel_id=1, source_target_pairs={{0,1},{1,0},{2,3},{3,2},{4,5},{5,4},{6,7},{7,6},{8,9},{9,8},{10,11... | collective-permute-start | bytes 294920 | tf_op jit(solution)/shard_map/ppermute | solution.py:729
  20.0 0.4 %shard_map.77 = (bf16[3,160,96]{2,1,0:T(8,128)(2,1)S(1)}, bf16[1,8,96]{2,1,0:T(8,128)(2,1)S(1)}, f32[64,2048]{1,0:T(8,128)S(1)}, f32[16,2048]{1,0:T(8,128)S(1)}, f32[16,2048]{1,0:T(8,128)S(1)}) custom-call(f32[8,128]{1,0:T(8,128)S(1)} %get-tuple-element.26.after_ref.freq_ref, f32[64,2048]{1,0:T(8,128)S(1)} %get-tuple-element.25.phi_ref, ...), custom_call_target="tpu_custom_call" | custom-call | flops 2000000000 | bytes 4194304 | tf_op jit(solution)/shard_map/pallas_call | solution.py:610
  20.5 2.8 %collective-permute-done.3.other_ref = bf16[96,512]{1,0:T(8,128)(2,1)S(1)} collective-permute-done((bf16[96,512]{1,0:T(8,128)(2,1)S(1)}, bf16[96,512]{1,0:T(8,128)(2,1)S(1)}, u32[]{:S(2)}, u32[]{:S(2)}) %collective-permute-start.3) | collective-permute-done | bytes 98336 | tf_op jit(solution)/shard_map/ppermute | solution.py:729
  23.3 0.1 shard_map.78
  23.4 1.6 %collective-permute-start.5 = (bf16[96,512]{1,0:T(8,128)(2,1)S(1)}, bf16[96,512]{1,0:T(8,128)(2,1)S(1)}, u32[]{:S(2)}, u32[]{:S(2)}) collective-permute-start(bf16[96,512]{1,0:T(8,128)(2,1)S(1)} %get-tuple-element.43.y_ref), channel_id=1, source_target_pairs={{0,1},{1,0},{2,3},{3,2},{4,8},{5,9},{6,10},{7,11},{8,4},{9,5},{10,... | collective-permute-start | bytes 294920 | tf_op jit(solution)/shard_map/ppermute | solution.py:633
  25.0 0.0 collective-permute-start.4
  25.0 0.0 collective-permute-start.6
  25.0 0.2 shard_map.79.z_own_ref
  25.2 3.5 %collective-permute-done.6.rest_0_ = bf16[8,512]{1,0:T(8,128)(2,1)S(1)} collective-permute-done((bf16[8,512]{1,0:T(8,128)(2,1)S(1)}, bf16[8,512]{1,0:T(8,128)(2,1)S(1)}, u32[]{:S(2)}, u32[]{:S(2)}) %collective-permute-start.6) | collective-permute-done | bytes 8224 | tf_op jit(solution)/shard_map/ppermute | solution.py:737
  28.6 0.0 collective-permute-done.5.y_b_ref
  28.6 0.0 collective-permute-done.4.y_a_ref
  28.7 2.6 %shard_map.80 = f32[64,2048]{1,0:T(8,128)} custom-call(f32[64,2048]{1,0:T(8,128)S(1)} %get-tuple-element.25.phi_ref, f32[64,2048]{1,0:T(8,128)S(1)} %get-tuple-element.38.slope_ref, f32[16,2048]{1,0:T(8,128)S(1)} %get-tuple-element.39.halo_ref, f32[16,2048]{1,0:T(8,128)S(1)} %get-tuple-element.40.halo_slope_ref, ...), custom_call_target="tpu_custom_call" | custom-call | flops 1000000 | bytes 4194304 | tf_op jit(solution)/shard_map/pallas_call | solution.py:610
  (1 shorter events, 0.0 us)
Async XLA Ops:
  3.2 7.4 %collective-permute-start.2 = (f32[8,128]{1,0:T(8,128)S(1)}, f32[8,128]{1,0:T(8,128)S(1)}, u32[]{:S(2)}, u32[]{:S(2)}) collective-permute-start(f32[8,128]{1,0:T(8,128)S(1)} %shard_map.74.defocus_ref), channel_id=1, source_target_pairs={{0,2},{1,3},{2,0},{3,1},{4,6},{5,7},{6,4},{7,5},{8,10},{9,11},{10,... | collective-permute-start | bytes 12296 | tf_op jit(solution)/shard_map/ppermute | solution.py:677
  7.4 3.3 %collective-permute-start = (bf16[104,512]{1,0:T(8,128)(2,1)S(1)}, bf16[104,512]{1,0:T(8,128)(2,1)S(1)}, u32[]{:S(2)}, u32[]{:S(2)}) collective-permute-start(bf16[104,512]{1,0:T(8,128)(2,1)S(1)} %get-tuple-element.27), channel_id=1, source_target_pairs={{0,4},{1,5},{2,6},{3,7},{4,0},{5,1},{6,2},{7,3},{8,12},{9,13},{10,... | collective-permute-start | bytes 319496 | tf_op jit(solution)/shard_map/ppermute | solution.py:633
  7.4 4.7 %collective-permute-start.1 = (bf16[104,512]{1,0:T(8,128)(2,1)S(1)}, bf16[104,512]{1,0:T(8,128)(2,1)S(1)}, u32[]{:S(2)}, u32[]{:S(2)}) collective-permute-start(bf16[104,512]{1,0:T(8,128)(2,1)S(1)} %get-tuple-element.28), channel_id=1, source_target_pairs={{0,1},{1,0},{2,3},{3,2},{4,8},{5,9},{6,10},{7,11},{8,4},{9,5},{10,... | collective-permute-start | bytes 319496 | tf_op jit(solution)/shard_map/ppermute | solution.py:633
  18.4 4.9 %collective-permute-start.3 = (bf16[96,512]{1,0:T(8,128)(2,1)S(1)}, bf16[96,512]{1,0:T(8,128)(2,1)S(1)}, u32[]{:S(2)}, u32[]{:S(2)}) collective-permute-start(bf16[96,512]{1,0:T(8,128)(2,1)S(1)} %shard_map.76.part_ref), channel_id=1, source_target_pairs={{0,1},{1,0},{2,3},{3,2},{4,5},{5,4},{6,7},{7,6},{8,9},{9,8},{10,11... | collective-permute-start | bytes 294920 | tf_op jit(solution)/shard_map/ppermute | solution.py:729
  23.4 5.2 %collective-permute-start.5 = (bf16[96,512]{1,0:T(8,128)(2,1)S(1)}, bf16[96,512]{1,0:T(8,128)(2,1)S(1)}, u32[]{:S(2)}, u32[]{:S(2)}) collective-permute-start(bf16[96,512]{1,0:T(8,128)(2,1)S(1)} %get-tuple-element.43.y_ref), channel_id=1, source_target_pairs={{0,1},{1,0},{2,3},{3,2},{4,8},{5,9},{6,10},{7,11},{8,4},{9,5},{10,... | collective-permute-start | bytes 294920 | tf_op jit(solution)/shard_map/ppermute | solution.py:633
  25.0 3.7 %collective-permute-start.4 = (bf16[96,512]{1,0:T(8,128)(2,1)S(1)}, bf16[96,512]{1,0:T(8,128)(2,1)S(1)}, u32[]{:S(2)}, u32[]{:S(2)}) collective-permute-start(bf16[96,512]{1,0:T(8,128)(2,1)S(1)} %get-tuple-element.43.y_ref), channel_id=1, source_target_pairs={{0,4},{1,5},{2,6},{3,7},{4,0},{5,1},{6,2},{7,3},{8,12},{9,13},{10,... | collective-permute-start | bytes 294920 | tf_op jit(solution)/shard_map/ppermute | solution.py:633
  25.0 3.7 %collective-permute-start.6 = (bf16[8,512]{1,0:T(8,128)(2,1)S(1)}, bf16[8,512]{1,0:T(8,128)(2,1)S(1)}, u32[]{:S(2)}, u32[]{:S(2)}) collective-permute-start(bf16[8,512]{1,0:T(8,128)(2,1)S(1)} %get-tuple-element.44), channel_id=1, source_target_pairs={{0,8},{4,12},{8,0},{12,4},{1,9},{5,13},{9,1},{13,5},{2,10},{6,14},... | collective-permute-start | bytes 24584 | tf_op jit(solution)/shard_map/ppermute | solution.py:737

commit v10 on v9

--- a/solution.py
+++ b/solution.py
@@ -366,24 +366,20 @@
     table_ref,
     inner_ref,
     inner_t_ref,
-    k_re_ref,
-    k_im_ref,
     *rest,
 ):
     rows, cols = goal_ref.shape
     half = cols // 2
+    if len(rest) == 5:
+        base_refs, (k_re_ref, k_im_ref, out_ref, q_ref, x_ref) = (), rest
+    else:
+        base_refs, (defocus_ref, psi_ref, kernels_ref) = rest[:1], rest[1:4]
+        out_ref, q_ref, x_ref, k_re_ref, k_im_ref = rest[4:]
+        kernels_at(defocus_ref, psi_ref, kernels_ref, k_re_ref, k_im_ref)
     count, fr, _ = k_re_ref.shape
     scale = 1.0 / float((rows + 2 * MARGIN) * cols) ** 0.5
     bf = jnp.bfloat16
     f32 = jnp.float32
-    if len(rest) == 3:
-        out_ref, q_ref, x_ref = rest
-        planes = [(k_re_ref, k_im_ref, q_ref, x_ref)]
-    else:
-        other_ref, psi_ref, kernels_ref, out_ref = rest[:4]
-        q_ref, x_ref, q2_ref, x2_ref, k2_re_ref, k2_im_ref = rest[4:]
-        kernels_at(other_ref, psi_ref, kernels_ref, k2_re_ref, k2_im_ref)
-        planes = [(k_re_ref, k_im_ref, q_ref, x_ref), (k2_re_ref, k2_im_ref, q2_ref, x2_ref)]
 
     spec = scale * (
         own_ref[...] + from_a_ref[: 2 * fr].astype(f32) + from_b_ref[: 2 * fr].astype(f32)
@@ -455,19 +451,15 @@
             y_im = y_im + (k_re * w_im - k_im * w_re)
         return y_re, y_im
 
-    for k_re_ref, k_im_ref, q_ref, x_ref in planes:
-        fields(k_re_ref, k_im_ref, q_ref)
-    for _, _, q_ref, x_ref in planes:
-        for start in range(0, half, width):
-            weighted(q_ref, x_ref, start)
-    y_re = 0.0
-    y_im = 0.0
-    for plane in planes:
-        part_re, part_im = adjoint(*plane)
-        y_re = y_re + part_re
-        y_im = y_im + part_im
-    out_ref[:fr] = y_re.astype(bf)
-    out_ref[fr:] = y_im.astype(bf)
+    fields(k_re_ref, k_im_ref, q_ref)
+    for start in range(0, half, width):
+        weighted(q_ref, x_ref, start)
+    y_re, y_im = adjoint(k_re_ref, k_im_ref, q_ref, x_ref)
+    for base_ref in base_refs:
+        y_re = y_re + base_ref[:fr]
+        y_im = y_im + base_ref[fr:]
+    out_ref[:fr] = y_re.astype(out_ref.dtype)
+    out_ref[fr:] = y_im.astype(out_ref.dtype)
 
 
 def sum_kernel(part_ref, other_ref, far_ref, total_ref, *payload_refs):
@@ -698,15 +690,22 @@
         pltpu.VMEM((count * 2 * rows, fc), bf),
         pltpu.VMEM((count * 2 * rows, cols), bf),
     ]
+    common = (s_own, from_a, from_b, goal, table, inner, inner_t)
     (part,) = call(
         main_kernel,
-        [shape((2 * fr, fc), bf)],
-        (s_own, from_a, from_b, goal, table, inner, inner_t, k_re, k_im)
-        + ((other_defocus, psi_v, kernels_v) if paired else ()),
-        scratch=scratch * 2 + [pltpu.VMEM((count, fr, fc), f32)] * 2 if paired else scratch,
-        limit=40,
+        [shape((2 * fr, fc), f32 if paired else bf)],
+        common + (k_re, k_im),
+        scratch=scratch,
         flops=4000000000,
     )
+    if paired:
+        (part,) = call(
+            main_kernel,
+            [shape((2 * fr, fc), bf)],
+            common + (part, other_defocus, psi_v, kernels_v),
+            scratch=scratch + [pltpu.VMEM((count, fr, fc), f32)] * 2,
+            flops=4000000000,
+        )
     tall_t, far_t, slope, halo, halo_slope = call(
         functools.partial(third_kernel, strips, groups),
         [

time: 31.5 us -> 31.8 us (level)
    pallas_call x8 -> x9, Pallas kernels: 13.9 us -> 14.2 us  [call(): pl.pallas_call(kernel, out_shape=outs, in_specs=[spec(kind) for kind in k...]
  transfers between devices with their start and end apart: 7 -> 7, of which waited for: 3 -> 3; matrix products, arithmetic and copies ran while one was open for 0% -> 0% of each run, Pallas kernels for 7% -> 17%
where the time goes in v10:
time: 31.8 us; the launch traced here: 31.6 us
  Pallas kernels  14.2 us (45%)
  starting transfers between devices  8.92 us (28%)
  waiting for transfers between devices  7.74 us (24%)
  between operations  0.72 us (2%)
    pallas_call x9, Pallas kernels, call(): pl.pallas_call(kernel, out_shape=outs, in_specs=[spec(kind) for kind in k...  14.2 us
    ppermute x1, starting transfers between devices, on_device(): other_defocus = lax.ppermute(defocus, 'focus', swap)  4.13 us
    ppermute x1, waiting for transfers between devices, on_device(): lax.ppermute(payload, 'strip', [(i, (i - turn_by) % strips) for i in rang...  3.47 us
    ppermute x4, starting transfers between devices, pair_up(): return lax.ppermute(block, ('strip', 'focus'), moves)  3.16 us
    ppermute x1, waiting for transfers between devices, on_device(): other = lax.ppermute(part, 'focus', [(i, i ^ step) for i in range(planes)])  2.79 us
    ppermute x1, starting transfers between devices, on_device(): other = lax.ppermute(part, 'focus', [(i, i ^ step) for i in range(planes)])  1.63 us
    ppermute x4, waiting for transfers between devices, pair_up(): return lax.ppermute(block, ('strip', 'focus'), moves)  1.48 us
  transfers between devices with their start and end apart: 7, of which 3 were waited for; matrix products, arithmetic and copies ran while one was open for 0% of the time, Pallas kernels for 17%

profile of v10, /device:TPU:0, one launch (start us, length us, event | category | flops | bytes accessed | tf_op | source)
XLA Modules:
  0.0 31.6 jit_solution(1340549929742237042)
XLA Ops:
  0.7 2.6 %shard_map.73 = (bf16[512,2048]{1,0:T(8,128)(2,1)S(1)}, f32[96,512]{1,0:T(8,128)S(1)}, bf16[104,512]{1,0:T(8,128)(2,1)S(1)}, bf16[104,512]{1,0:T(8,128)(2,1)S(1)...) custom-call(f32[64,2048]{1,0:T(8,128)} %phi_hbm.1, s32[1,48]{1,0:T(1,128)} %bitcast.3, s32[1,512]{1,0:T(1,128)} %bitcast.2), custom_call_target="tpu_custom_call" | custom-call | flops 1000000 | bytes 4194304 | tf_op jit(solution)/shard_map/pallas_call | solution.py:602
  3.3 4.1 %collective-permute-start.2 = (f32[8,128]{1,0:T(8,128)S(1)}, f32[8,128]{1,0:T(8,128)S(1)}, u32[]{:S(2)}, u32[]{:S(2)}) collective-permute-start(f32[8,128]{1,0:T(8,128)S(1)} %shard_map.74.defocus_ref), channel_id=1, source_target_pairs={{0,2},{1,3},{2,0},{3,1},{4,6},{5,7},{6,4},{7,5},{8,10},{9,11},{10,... | collective-permute-start | bytes 12296 | tf_op jit(solution)/shard_map/ppermute | solution.py:669
  7.4 0.0 collective-permute-start
  7.4 1.6 %collective-permute-start.1 = (bf16[104,512]{1,0:T(8,128)(2,1)S(1)}, bf16[104,512]{1,0:T(8,128)(2,1)S(1)}, u32[]{:S(2)}, u32[]{:S(2)}) collective-permute-start(bf16[104,512]{1,0:T(8,128)(2,1)S(1)} %get-tuple-element.28), channel_id=1, source_target_pairs={{0,1},{1,0},{2,3},{3,2},{4,8},{5,9},{6,10},{7,11},{8,4},{9,5},{10,... | collective-permute-start | bytes 319496 | tf_op jit(solution)/shard_map/ppermute | solution.py:625
  9.0 1.6 %shard_map.75 = (bf16[96,128]{1,0:T(8,128)(2,1)S(1)}, bf16[128,96]{1,0:T(8,128)(2,1)S(1)}, f32[4,48,512]{2,1,0:T(8,128)S(1)}, f32[4,48,512]{2,1,0:T(8,128)S(1)},...) custom-call(f32[8,128]{1,0:T(8,128)S(1)} %shard_map.74.defocus_ref, ...), custom_call_target="tpu_custom_call" | custom-call | flops 4000000000 | bytes 4194304 | tf_op jit(solution)/shard_map/pallas_call | solution.py:602
  10.6 0.0 collective-permute-done.from_a_ref
  10.6 1.5 %collective-permute-done.1.from_b_ref = bf16[104,512]{1,0:T(8,128)(2,1)S(1)} collective-permute-done((bf16[104,512]{1,0:T(8,128)(2,1)S(1)}, bf16[104,512]{1,0:T(8,128)(2,1)S(1)}, u32[]{:S(2)}, u32[]{:S(2)}) %collective-permute-start.1) | collective-permute-done | bytes 106528 | tf_op jit(solution)/shard_map/ppermute | solution.py:625
  12.1 3.2 %shard_map.76.rest_0_ = f32[96,512]{1,0:T(8,128)S(1)} custom-call(f32[96,512]{1,0:T(8,128)S(1)} %get-tuple-element.29.own_ref, bf16[104,512]{1,0:T(8,128)(2,1)S(1)} %collective-permute-done.from_a_ref, bf16[104,512]{1,0:T(8,128)(2,1)S(1)} %collective-permute-done.1.from_b_ref, f32[64,2048]{1,0:T(8,128)S(1)} %get-tuple-element.30.goal_ref, ...), custom_call_target="tpu_custom_call" | custom-call | flops 4000000000 | bytes 4194304 | tf_op jit(solution)/shard_map/pallas_call | solution.py:602
  15.3 0.0 collective-permute-done.2.rest_1_
  15.3 3.4 %shard_map.77.part_ref = bf16[96,512]{1,0:T(8,128)(2,1)S(1)} custom-call(f32[96,512]{1,0:T(8,128)S(1)} %get-tuple-element.29.own_ref, bf16[104,512]{1,0:T(8,128)(2,1)S(1)} %collective-permute-done.from_a_ref, bf16[104,512]{1,0:T(8,128)(2,1)S(1)} %collective-permute-done.1.from_b_ref, f32[64,2048]{1,0:T(8,128)S(1)} %get-tuple-element.30.goal_ref, ...), custom_call_target="tpu_custom_call" | custom-call | flops 4000000000 | bytes 4194304 | tf_op jit(solution)/shard_map/pallas_call | solution.py:602
  18.7 1.6 %collective-permute-start.3 = (bf16[96,512]{1,0:T(8,128)(2,1)S(1)}, bf16[96,512]{1,0:T(8,128)(2,1)S(1)}, u32[]{:S(2)}, u32[]{:S(2)}) collective-permute-start(bf16[96,512]{1,0:T(8,128)(2,1)S(1)} %shard_map.77.part_ref), channel_id=1, source_target_pairs={{0,1},{1,0},{2,3},{3,2},{4,5},{5,4},{6,7},{7,6},{8,9},{9,8},{10,11... | collective-permute-start | bytes 294920 | tf_op jit(solution)/shard_map/ppermute | solution.py:728
  20.4 0.4 %shard_map.78 = (bf16[3,160,96]{2,1,0:T(8,128)(2,1)S(1)}, bf16[1,8,96]{2,1,0:T(8,128)(2,1)S(1)}, f32[64,2048]{1,0:T(8,128)S(1)}, f32[16,2048]{1,0:T(8,128)S(1)}, f32[16,2048]{1,0:T(8,128)S(1)}) custom-call(f32[8,128]{1,0:T(8,128)S(1)} %get-tuple-element.26.after_ref.freq_ref, f32[64,2048]{1,0:T(8,128)S(1)} %get-tuple-element.25.phi_ref, ...), custom_call_target="tpu_custom_call" | custom-call | flops 2000000000 | bytes 4194304 | tf_op jit(solution)/shard_map/pallas_call | solution.py:602
  20.8 2.8 %collective-permute-done.3.other_ref = bf16[96,512]{1,0:T(8,128)(2,1)S(1)} collective-permute-done((bf16[96,512]{1,0:T(8,128)(2,1)S(1)}, bf16[96,512]{1,0:T(8,128)(2,1)S(1)}, u32[]{:S(2)}, u32[]{:S(2)}) %collective-permute-start.3) | collective-permute-done | bytes 98336 | tf_op jit(solution)/shard_map/ppermute | solution.py:728
  23.6 0.1 shard_map.79
  23.7 1.6 %collective-permute-start.5 = (bf16[96,512]{1,0:T(8,128)(2,1)S(1)}, bf16[96,512]{1,0:T(8,128)(2,1)S(1)}, u32[]{:S(2)}, u32[]{:S(2)}) collective-permute-start(bf16[96,512]{1,0:T(8,128)(2,1)S(1)} %get-tuple-element.43.y_ref), channel_id=1, source_target_pairs={{0,1},{1,0},{2,3},{3,2},{4,8},{5,9},{6,10},{7,11},{8,4},{9,5},{10,... | collective-permute-start | bytes 294920 | tf_op jit(solution)/shard_map/ppermute | solution.py:625
  25.3 0.0 collective-permute-start.4
  25.3 0.0 collective-permute-start.6
  25.3 0.2 shard_map.80.z_own_ref
  25.5 3.5 %collective-permute-done.6.rest_0_ = bf16[8,512]{1,0:T(8,128)(2,1)S(1)} collective-permute-done((bf16[8,512]{1,0:T(8,128)(2,1)S(1)}, bf16[8,512]{1,0:T(8,128)(2,1)S(1)}, u32[]{:S(2)}, u32[]{:S(2)}) %collective-permute-start.6) | collective-permute-done | bytes 8224 | tf_op jit(solution)/shard_map/ppermute | solution.py:736
  29.0 0.0 collective-permute-done.5.y_b_ref
  29.0 0.0 collective-permute-done.4.y_a_ref
  29.0 2.6 %shard_map.81 = f32[64,2048]{1,0:T(8,128)} custom-call(f32[64,2048]{1,0:T(8,128)S(1)} %get-tuple-element.25.phi_ref, f32[64,2048]{1,0:T(8,128)S(1)} %get-tuple-element.38.slope_ref, f32[16,2048]{1,0:T(8,128)S(1)} %get-tuple-element.39.halo_ref, f32[16,2048]{1,0:T(8,128)S(1)} %get-tuple-element.40.halo_slope_ref, ...), custom_call_target="tpu_custom_call" | custom-call | flops 1000000 | bytes 4194304 | tf_op jit(solution)/shard_map/pallas_call | solution.py:602
  (1 shorter events, 0.0 us)
Async XLA Ops:
  3.3 12.1 %collective-permute-start.2 = (f32[8,128]{1,0:T(8,128)S(1)}, f32[8,128]{1,0:T(8,128)S(1)}, u32[]{:S(2)}, u32[]{:S(2)}) collective-permute-start(f32[8,128]{1,0:T(8,128)S(1)} %shard_map.74.defocus_ref), channel_id=1, source_target_pairs={{0,2},{1,3},{2,0},{3,1},{4,6},{5,7},{6,4},{7,5},{8,10},{9,11},{10,... | collective-permute-start | bytes 12296 | tf_op jit(solution)/shard_map/ppermute | solution.py:669
  7.4 3.2 %collective-permute-start = (bf16[104,512]{1,0:T(8,128)(2,1)S(1)}, bf16[104,512]{1,0:T(8,128)(2,1)S(1)}, u32[]{:S(2)}, u32[]{:S(2)}) collective-permute-start(bf16[104,512]{1,0:T(8,128)(2,1)S(1)} %get-tuple-element.27), channel_id=1, source_target_pairs={{0,4},{1,5},{2,6},{3,7},{4,0},{5,1},{6,2},{7,3},{8,12},{9,13},{10,... | collective-permute-start | bytes 319496 | tf_op jit(solution)/shard_map/ppermute | solution.py:625
  7.4 4.7 %collective-permute-start.1 = (bf16[104,512]{1,0:T(8,128)(2,1)S(1)}, bf16[104,512]{1,0:T(8,128)(2,1)S(1)}, u32[]{:S(2)}, u32[]{:S(2)}) collective-permute-start(bf16[104,512]{1,0:T(8,128)(2,1)S(1)} %get-tuple-element.28), channel_id=1, source_target_pairs={{0,1},{1,0},{2,3},{3,2},{4,8},{5,9},{6,10},{7,11},{8,4},{9,5},{10,... | collective-permute-start | bytes 319496 | tf_op jit(solution)/shard_map/ppermute | solution.py:625
  18.7 4.9 %collective-permute-start.3 = (bf16[96,512]{1,0:T(8,128)(2,1)S(1)}, bf16[96,512]{1,0:T(8,128)(2,1)S(1)}, u32[]{:S(2)}, u32[]{:S(2)}) collective-permute-start(bf16[96,512]{1,0:T(8,128)(2,1)S(1)} %shard_map.77.part_ref), channel_id=1, source_target_pairs={{0,1},{1,0},{2,3},{3,2},{4,5},{5,4},{6,7},{7,6},{8,9},{9,8},{10,11... | collective-permute-start | bytes 294920 | tf_op jit(solution)/shard_map/ppermute | solution.py:728
  23.7 5.2 %collective-permute-start.5 = (bf16[96,512]{1,0:T(8,128)(2,1)S(1)}, bf16[96,512]{1,0:T(8,128)(2,1)S(1)}, u32[]{:S(2)}, u32[]{:S(2)}) collective-permute-start(bf16[96,512]{1,0:T(8,128)(2,1)S(1)} %get-tuple-element.43.y_ref), channel_id=1, source_target_pairs={{0,1},{1,0},{2,3},{3,2},{4,8},{5,9},{6,10},{7,11},{8,4},{9,5},{10,... | collective-permute-start | bytes 294920 | tf_op jit(solution)/shard_map/ppermute | solution.py:625
  25.3 3.7 %collective-permute-start.4 = (bf16[96,512]{1,0:T(8,128)(2,1)S(1)}, bf16[96,512]{1,0:T(8,128)(2,1)S(1)}, u32[]{:S(2)}, u32[]{:S(2)}) collective-permute-start(bf16[96,512]{1,0:T(8,128)(2,1)S(1)} %get-tuple-element.43.y_ref), channel_id=1, source_target_pairs={{0,4},{1,5},{2,6},{3,7},{4,0},{5,1},{6,2},{7,3},{8,12},{9,13},{10,... | collective-permute-start | bytes 294920 | tf_op jit(solution)/shard_map/ppermute | solution.py:625
  25.3 3.7 %collective-permute-start.6 = (bf16[8,512]{1,0:T(8,128)(2,1)S(1)}, bf16[8,512]{1,0:T(8,128)(2,1)S(1)}, u32[]{:S(2)}, u32[]{:S(2)}) collective-permute-start(bf16[8,512]{1,0:T(8,128)(2,1)S(1)} %get-tuple-element.44), channel_id=1, source_target_pairs={{0,8},{4,12},{8,0},{12,4},{1,9},{5,13},{9,1},{13,5},{2,10},{6,14},... | collective-permute-start | bytes 24584 | tf_op jit(solution)/shard_map/ppermute | solution.py:736

commit v11 on v10

--- a/solution.py
+++ b/solution.py
@@ -116,12 +116,18 @@
     phi_hbm,
     row_freqs_hbm,
     col_freqs_hbm,
+    kernels_hbm,
+    psi_hbm,
+    target_hbm,
     table_ref,
     own_ref,
     send_a_ref,
     send_b_ref,
     phi_ref,
     freq_ref,
+    kernels_ref,
+    psi_ref,
+    target_ref,
     mask_ref,
     row_freqs_ref,
     col_freqs_ref,
@@ -138,6 +144,13 @@
     load_cols.start()
     load_rows.start()
     load_phi.start()
+    later_loads = [
+        pltpu.make_async_copy(psi_hbm, psi_ref, sems.at[3]),
+        pltpu.make_async_copy(kernels_hbm, kernels_ref, sems.at[4]),
+        pltpu.make_async_copy(target_hbm, target_ref, sems.at[5]),
+    ]
+    for load in later_loads:
+        load.start()
     _, first, second, first_in, second_in = partners(strips)
 
     load_cols.wait()
@@ -224,6 +237,8 @@
     lows = jnp.concatenate(lows, axis=0)
     send_a_ref[2 * fr :] = jnp.where(first > 0, lows, tops).astype(bf)
     send_b_ref[2 * fr :] = jnp.where(second > 0, lows, tops).astype(bf)
+    for load in later_loads:
+        load.wait()
 
 
 def defocus_kernel(defocus_ref, after_ref, out_ref):
@@ -243,28 +258,18 @@
 def second_kernel(
     defocus_ref,
     freq_ref,
-    kernels_hbm,
-    psi_hbm,
-    target_hbm,
+    kernels_ref,
+    psi_ref,
+    target_ref,
     inner_ref,
     inner_t_ref,
     k_re_ref,
     k_im_ref,
     goal_ref,
-    kernels_ref,
-    psi_ref,
-    target_ref,
-    sems,
 ):
     rows, cols = target_ref.shape
     half = cols // 2
     fr = psi_ref.shape[0]
-    load_psi = pltpu.make_async_copy(psi_hbm, psi_ref, sems.at[0])
-    load_kernels = pltpu.make_async_copy(kernels_hbm, kernels_ref, sems.at[1])
-    load_target = pltpu.make_async_copy(target_hbm, target_ref, sems.at[2])
-    load_psi.start()
-    load_kernels.start()
-    load_target.start()
     window = rows + 2 * MARGIN
     bf = jnp.bfloat16
     across = freq_ref[0:1, :]
@@ -274,11 +279,8 @@
     table = interleaved(across, (2 * rows, LANES), 1, fr, MARGIN, window)
     inner_t_ref[...] = table[:, : 2 * fr].astype(bf)
 
-    load_psi.wait()
-    load_kernels.wait()
     kernels_at(defocus_ref, psi_ref, kernels_ref, k_re_ref, k_im_ref)
 
-    load_target.wait()
     goal_ref[:, :half] = target_ref[:, :half].astype(jnp.float32)
     for b in range(half // LANES):
         goal_ref[:, half + b * LANES : half + (b + 1) * LANES] = mirrored(
@@ -639,7 +641,7 @@
     packet = shape((2 * fr + HALO * (cols // fc), fc), bf)
     row_freqs = row_freqs.reshape(1, fr)
 
-    table, s_own, send_a, send_b, phi, freqs = call(
+    table, s_own, send_a, send_b, phi, freqs, kernels_v, psi_v, target_v = call(
         functools.partial(first_kernel, strips),
         [
             shape((fc, cols), bf),
@@ -648,14 +650,17 @@
             packet,
             shape((rows, cols), f32),
             shape((8, LANES), f32),
+            shape(kernels.shape, f32),
+            shape(psi.shape, f32),
+            shape(target.shape, jnp.int32),
         ],
-        (phi, row_freqs, col_freqs.reshape(1, fc)),
-        kinds="hhh",
+        (phi, row_freqs, col_freqs.reshape(1, fc), kernels, psi, target),
+        kinds="hhhhhh",
         scratch=[
             pltpu.VMEM((rows, cols), bf),
             pltpu.VMEM((1, fr), jnp.int32),
             pltpu.VMEM((1, fc), jnp.int32),
-            pltpu.SemaphoreType.DMA((3,)),
+            pltpu.SemaphoreType.DMA((6,)),
         ],
     )
     (defocus,) = call(
@@ -667,7 +672,7 @@
     if paired:
         swap = [(i, i ^ (planes // 2)) for i in range(planes)]
         other_defocus = lax.ppermute(defocus, "focus", swap)
-    inner, inner_t, k_re, k_im, goal, kernels_v, psi_v = call(
+    inner, inner_t, k_re, k_im, goal = call(
         second_kernel,
         [
             shape((2 * fr, 2 * rows), bf),
@@ -675,15 +680,8 @@
             shape((count, fr, fc), f32),
             shape((count, fr, fc), f32),
             shape((rows, cols), f32),
-            shape(kernels.shape, f32),
-            shape(psi.shape, f32),
         ],
-        (defocus, freqs, kernels, psi, target),
-        kinds="vvhhh",
-        scratch=[
-            pltpu.VMEM(target.shape, jnp.int32),
-            pltpu.SemaphoreType.DMA((3,)),
-        ],
+        (defocus, freqs, kernels_v, psi_v, target_v),
         flops=4000000000,
     )
     scratch = [
@@ -732,12 +730,12 @@
         [shape((2 * fr, fc), bf)] + [shape((4 * HALO, fc), bf)] * len(groups),
         (part, other, far_t),
     )
+    y_b = pair_up(total, False)
+    y_a = pair_up(total, True)
     far = [
         lax.ppermute(payload, "strip", [(i, (i - turn_by) % strips) for i in range(strips)])
         for turn_by, payload in zip(groups, payloads)
     ]
-    y_b = pair_up(total, False)
-    y_a = pair_up(total, True)
     (z_own,) = call(own_kernel, [shape((2 * tall, fc), f32)], (tall_t, total), flops=2000000000)
     return call(
         functools.partial(final_kernel, strips),

time: 31.8 us -> 29 us (0.912)
  waiting for transfers between devices: 7.74 us -> 6.13 us
  Pallas kernels: 14.2 us -> 13.1 us
    ppermute x4, starting transfers between devices: 3.16 us -> 4.67 us  [pair_up(): return lax.ppermute(block, ('strip', 'focus'), moves)]
    ppermute x1, starting transfers between devices: 4.13 us -> 2.65 us  [on_device(): other_defocus = lax.ppermute(defocus, 'focus', swap)]
    ppermute x4, waiting for transfers between devices: 1.48 us -> 0.01 us  [pair_up(): return lax.ppermute(block, ('strip', 'focus'), moves)]
    pallas_call x9, Pallas kernels: 14.2 us -> 13.1 us  [call(): pl.pallas_call(kernel, out_shape=outs, in_specs=[spec(kind) for kind in k...]
    ppermute x1, starting transfers between devices: 1.63 us -> 0.92 us  [on_device(): other = lax.ppermute(part, 'focus', [(i, i ^ step) for i in range(planes)])]
    ppermute x1, starting transfers between devices: 0.01 us -> 0.67 us  [on_device(): lax.ppermute(payload, 'strip', [(i, (i - turn_by) % strips) for i in rang...]
    ppermute x1, waiting for transfers between devices: 3.47 us -> 2.8 us  [on_device(): lax.ppermute(payload, 'strip', [(i, (i - turn_by) % strips) for i in rang...]
    ppermute x1, waiting for transfers between devices: 2.79 us -> 3.32 us  [on_device(): other = lax.ppermute(part, 'focus', [(i, i ^ step) for i in range(planes)])]
  transfers between devices with their start and end apart: 7 -> 7, of which waited for: 3 -> 2; matrix products, arithmetic and copies ran while one was open for 0% -> 0% of each run, Pallas kernels for 17% -> 15%
where the time goes in v11:
time: 29 us; the launch traced here: 28.9 us
  Pallas kernels  13.1 us (45%)
  starting transfers between devices  8.91 us (31%)
  waiting for transfers between devices  6.13 us (21%)
  between operations  0.72 us (2%)
    pallas_call x9, Pallas kernels, call(): pl.pallas_call(kernel, out_shape=outs, in_specs=[spec(kind) for kind in k...  13.1 us
    ppermute x4, starting transfers between devices, pair_up(): return lax.ppermute(block, ('strip', 'focus'), moves)  4.67 us
    ppermute x1, waiting for transfers between devices, on_device(): other = lax.ppermute(part, 'focus', [(i, i ^ step) for i in range(planes)])  3.32 us
    ppermute x1, waiting for transfers between devices, on_device(): lax.ppermute(payload, 'strip', [(i, (i - turn_by) % strips) for i in rang...  2.8 us
    ppermute x1, starting transfers between devices, on_device(): other_defocus = lax.ppermute(defocus, 'focus', swap)  2.65 us
    ppermute x1, starting transfers between devices, on_device(): other = lax.ppermute(part, 'focus', [(i, i ^ step) for i in range(planes)])  0.92 us
    ppermute x1, starting transfers between devices, on_device(): lax.ppermute(payload, 'strip', [(i, (i - turn_by) % strips) for i in rang...  0.67 us
  transfers between devices with their start and end apart: 7, of which 2 were waited for; matrix products, arithmetic and copies ran while one was open for 0% of the time, Pallas kernels for 15%

profile of v11, /device:TPU:0, one launch (start us, length us, event | category | flops | bytes accessed | tf_op | source)
XLA Modules:
  0.0 28.9 jit_solution(17966236503863715657)
XLA Ops:
  0.0 2.6 %shard_map.73 = (bf16[512,2048]{1,0:T(8,128)(2,1)S(1)}, f32[96,512]{1,0:T(8,128)S(1)}, bf16[104,512]{1,0:T(8,128)(2,1)S(1)}, bf16[104,512]{1,0:T(8,128)(2,1)S(1)...) custom-call(f32[64,2048]{1,0:T(8,128)} %phi_hbm.1, ...), custom_call_target="tpu_custom_call" | custom-call | flops 1000000 | bytes 4194304 | tf_op jit(solution)/shard_map/pallas_call | solution.py:604
  2.6 0.6 %collective-permute-start = (bf16[104,512]{1,0:T(8,128)(2,1)S(1)}, bf16[104,512]{1,0:T(8,128)(2,1)S(1)}, u32[]{:S(2)}, u32[]{:S(2)}) collective-permute-start(bf16[104,512]{1,0:T(8,128)(2,1)S(1)} %get-tuple-element.28), channel_id=1, source_target_pairs={{0,4},{1,5},{2,6},{3,7},{4,0},{5,1},{6,2},{7,3},{8,12},{9,13},{10,... | collective-permute-start | bytes 319496 | tf_op jit(solution)/shard_map/ppermute | solution.py:627
  3.2 2.6 %collective-permute-start.1 = (bf16[104,512]{1,0:T(8,128)(2,1)S(1)}, bf16[104,512]{1,0:T(8,128)(2,1)S(1)}, u32[]{:S(2)}, u32[]{:S(2)}) collective-permute-start(bf16[104,512]{1,0:T(8,128)(2,1)S(1)} %get-tuple-element.29), channel_id=1, source_target_pairs={{0,1},{1,0},{2,3},{3,2},{4,8},{5,9},{6,10},{7,11},{8,4},{9,5},{10,... | collective-permute-start | bytes 319496 | tf_op jit(solution)/shard_map/ppermute | solution.py:627
  6.5 2.7 %collective-permute-start.2 = (f32[8,128]{1,0:T(8,128)S(1)}, f32[8,128]{1,0:T(8,128)S(1)}, u32[]{:S(2)}, u32[]{:S(2)}) collective-permute-start(f32[8,128]{1,0:T(8,128)S(1)} %shard_map.74.defocus_ref), channel_id=1, source_target_pairs={{0,2},{1,3},{2,0},{3,1},{4,6},{5,7},{6,4},{7,5},{8,10},{9,11},{10,... | collective-permute-start | bytes 12296 | tf_op jit(solution)/shard_map/ppermute | solution.py:674
  9.1 0.5 %shard_map.75 = (bf16[96,128]{1,0:T(8,128)(2,1)S(1)}, bf16[128,96]{1,0:T(8,128)(2,1)S(1)}, f32[4,48,512]{2,1,0:T(8,128)S(1)}, f32[4,48,512]{2,1,0:T(8,128)S(1)}, f32[64,2048]{1,0:T(8,128)S(1)}) custom-call(f32[8,128]{1,0:T(8,128)S(1)} %shard_map.74.defocus_ref, f32[8,128]{1,0:T(8,128)S(1)} %get-tuple-element.27.after_ref.freq_ref, ...), custom_call_target="tpu_custom_call" | custom-call | flops 4000000000 | bytes 4194304 | tf_op jit(solution)/shard_map/pallas_call | solution.py:604
  9.7 0.0 collective-permute-done.from_a_ref
  9.7 0.0 collective-permute-done.1.from_b_ref
  9.7 3.2 %shard_map.76.rest_0_ = f32[96,512]{1,0:T(8,128)S(1)} custom-call(f32[96,512]{1,0:T(8,128)S(1)} %get-tuple-element.30.own_ref, bf16[104,512]{1,0:T(8,128)(2,1)S(1)} %collective-permute-done.from_a_ref, bf16[104,512]{1,0:T(8,128)(2,1)S(1)} %collective-permute-done.1.from_b_ref, f32[64,2048]{1,0:T(8,128)S(1)} %get-tuple-element.34.goal_ref, ...), custom_call_target="tpu_custom_call" | custom-call | flops 4000000000 | bytes 4194304 | tf_op jit(solution)/shard_map/pallas_call | solution.py:604
  12.9 0.0 collective-permute-done.2.rest_1_
  12.9 3.4 %shard_map.77.part_ref = bf16[96,512]{1,0:T(8,128)(2,1)S(1)} custom-call(f32[96,512]{1,0:T(8,128)S(1)} %get-tuple-element.30.own_ref, bf16[104,512]{1,0:T(8,128)(2,1)S(1)} %collective-permute-done.from_a_ref, bf16[104,512]{1,0:T(8,128)(2,1)S(1)} %collective-permute-done.1.from_b_ref, f32[64,2048]{1,0:T(8,128)S(1)} %get-tuple-element.34.goal_ref, ...), custom_call_target="tpu_custom_call" | custom-call | flops 4000000000 | bytes 4194304 | tf_op jit(solution)/shard_map/pallas_call | solution.py:604
  16.3 0.9 %collective-permute-start.3 = (bf16[96,512]{1,0:T(8,128)(2,1)S(1)}, bf16[96,512]{1,0:T(8,128)(2,1)S(1)}, u32[]{:S(2)}, u32[]{:S(2)}) collective-permute-start(bf16[96,512]{1,0:T(8,128)(2,1)S(1)} %shard_map.77.part_ref), channel_id=1, source_target_pairs={{0,1},{1,0},{2,3},{3,2},{4,5},{5,4},{6,7},{7,6},{8,9},{9,8},{10,11... | collective-permute-start | bytes 294920 | tf_op jit(solution)/shard_map/ppermute | solution.py:726
  17.2 0.4 %shard_map.78 = (bf16[3,160,96]{2,1,0:T(8,128)(2,1)S(1)}, bf16[1,8,96]{2,1,0:T(8,128)(2,1)S(1)}, f32[64,2048]{1,0:T(8,128)S(1)}, f32[16,2048]{1,0:T(8,128)S(1)}, f32[16,2048]{1,0:T(8,128)S(1)}) custom-call(f32[8,128]{1,0:T(8,128)S(1)} %get-tuple-element.27.after_ref.freq_ref, f32[64,2048]{1,0:T(8,128)S(1)} %get-tuple-element.26.phi_ref, ...), custom_call_target="tpu_custom_call" | custom-call | flops 2000000000 | bytes 4194304 | tf_op jit(solution)/shard_map/pallas_call | solution.py:604
  17.6 3.3 %collective-permute-done.3.other_ref = bf16[96,512]{1,0:T(8,128)(2,1)S(1)} collective-permute-done((bf16[96,512]{1,0:T(8,128)(2,1)S(1)}, bf16[96,512]{1,0:T(8,128)(2,1)S(1)}, u32[]{:S(2)}, u32[]{:S(2)}) %collective-permute-start.3) | collective-permute-done | bytes 98336 | tf_op jit(solution)/shard_map/ppermute | solution.py:726
  21.0 0.1 shard_map.79
  21.1 0.0 collective-permute-start.4
  21.1 1.5 %collective-permute-start.5 = (bf16[96,512]{1,0:T(8,128)(2,1)S(1)}, bf16[96,512]{1,0:T(8,128)(2,1)S(1)}, u32[]{:S(2)}, u32[]{:S(2)}) collective-permute-start(bf16[96,512]{1,0:T(8,128)(2,1)S(1)} %get-tuple-element.45.y_ref), channel_id=1, source_target_pairs={{0,1},{1,0},{2,3},{3,2},{4,8},{5,9},{6,10},{7,11},{8,4},{9,5},{10,... | collective-permute-start | bytes 294920 | tf_op jit(solution)/shard_map/ppermute | solution.py:627
  22.6 0.7 %collective-permute-start.6 = (bf16[8,512]{1,0:T(8,128)(2,1)S(1)}, bf16[8,512]{1,0:T(8,128)(2,1)S(1)}, u32[]{:S(2)}, u32[]{:S(2)}) collective-permute-start(bf16[8,512]{1,0:T(8,128)(2,1)S(1)} %get-tuple-element.46), channel_id=1, source_target_pairs={{0,8},{4,12},{8,0},{12,4},{1,9},{5,13},{9,1},{13,5},{2,10},{6,14},... | collective-permute-start | bytes 24584 | tf_op jit(solution)/shard_map/ppermute | solution.py:736
  23.3 0.2 shard_map.80.z_own_ref
  23.4 2.8 %collective-permute-done.6.rest_0_ = bf16[8,512]{1,0:T(8,128)(2,1)S(1)} collective-permute-done((bf16[8,512]{1,0:T(8,128)(2,1)S(1)}, bf16[8,512]{1,0:T(8,128)(2,1)S(1)}, u32[]{:S(2)}, u32[]{:S(2)}) %collective-permute-start.6) | collective-permute-done | bytes 8224 | tf_op jit(solution)/shard_map/ppermute | solution.py:736
  26.2 0.0 collective-permute-done.4.y_a_ref
  26.2 0.0 collective-permute-done.5.y_b_ref
  26.2 2.6 %shard_map.81 = f32[64,2048]{1,0:T(8,128)} custom-call(f32[64,2048]{1,0:T(8,128)S(1)} %get-tuple-element.26.phi_ref, f32[64,2048]{1,0:T(8,128)S(1)} %get-tuple-element.40.slope_ref, f32[16,2048]{1,0:T(8,128)S(1)} %get-tuple-element.41.halo_ref, f32[16,2048]{1,0:T(8,128)S(1)} %get-tuple-element.42.halo_slope_ref, ...), custom_call_target="tpu_custom_call" | custom-call | flops 1000000 | bytes 4194304 | tf_op jit(solution)/shard_map/pallas_call | solution.py:604
  (1 shorter events, 0.0 us)
Async XLA Ops:
  2.6 7.0 %collective-permute-start = (bf16[104,512]{1,0:T(8,128)(2,1)S(1)}, bf16[104,512]{1,0:T(8,128)(2,1)S(1)}, u32[]{:S(2)}, u32[]{:S(2)}) collective-permute-start(bf16[104,512]{1,0:T(8,128)(2,1)S(1)} %get-tuple-element.28), channel_id=1, source_target_pairs={{0,4},{1,5},{2,6},{3,7},{4,0},{5,1},{6,2},{7,3},{8,12},{9,13},{10,... | collective-permute-start | bytes 319496 | tf_op jit(solution)/shard_map/ppermute | solution.py:627
  3.2 6.5 %collective-permute-start.1 = (bf16[104,512]{1,0:T(8,128)(2,1)S(1)}, bf16[104,512]{1,0:T(8,128)(2,1)S(1)}, u32[]{:S(2)}, u32[]{:S(2)}) collective-permute-start(bf16[104,512]{1,0:T(8,128)(2,1)S(1)} %get-tuple-element.29), channel_id=1, source_target_pairs={{0,1},{1,0},{2,3},{3,2},{4,8},{5,9},{6,10},{7,11},{8,4},{9,5},{10,... | collective-permute-start | bytes 319496 | tf_op jit(solution)/shard_map/ppermute | solution.py:627
  6.5 6.4 %collective-permute-start.2 = (f32[8,128]{1,0:T(8,128)S(1)}, f32[8,128]{1,0:T(8,128)S(1)}, u32[]{:S(2)}, u32[]{:S(2)}) collective-permute-start(f32[8,128]{1,0:T(8,128)S(1)} %shard_map.74.defocus_ref), channel_id=1, source_target_pairs={{0,2},{1,3},{2,0},{3,1},{4,6},{5,7},{6,4},{7,5},{8,10},{9,11},{10,... | collective-permute-start | bytes 12296 | tf_op jit(solution)/shard_map/ppermute | solution.py:674
  16.3 4.7 %collective-permute-start.3 = (bf16[96,512]{1,0:T(8,128)(2,1)S(1)}, bf16[96,512]{1,0:T(8,128)(2,1)S(1)}, u32[]{:S(2)}, u32[]{:S(2)}) collective-permute-start(bf16[96,512]{1,0:T(8,128)(2,1)S(1)} %shard_map.77.part_ref), channel_id=1, source_target_pairs={{0,1},{1,0},{2,3},{3,2},{4,5},{5,4},{6,7},{7,6},{8,9},{9,8},{10,11... | collective-permute-start | bytes 294920 | tf_op jit(solution)/shard_map/ppermute | solution.py:726
  21.1 5.1 %collective-permute-start.4 = (bf16[96,512]{1,0:T(8,128)(2,1)S(1)}, bf16[96,512]{1,0:T(8,128)(2,1)S(1)}, u32[]{:S(2)}, u32[]{:S(2)}) collective-permute-start(bf16[96,512]{1,0:T(8,128)(2,1)S(1)} %get-tuple-element.45.y_ref), channel_id=1, source_target_pairs={{0,4},{1,5},{2,6},{3,7},{4,0},{5,1},{6,2},{7,3},{8,12},{9,13},{10,... | collective-permute-start | bytes 294920 | tf_op jit(solution)/shard_map/ppermute | solution.py:627
  21.1 5.1 %collective-permute-start.5 = (bf16[96,512]{1,0:T(8,128)(2,1)S(1)}, bf16[96,512]{1,0:T(8,128)(2,1)S(1)}, u32[]{:S(2)}, u32[]{:S(2)}) collective-permute-start(bf16[96,512]{1,0:T(8,128)(2,1)S(1)} %get-tuple-element.45.y_ref), channel_id=1, source_target_pairs={{0,1},{1,0},{2,3},{3,2},{4,8},{5,9},{6,10},{7,11},{8,4},{9,5},{10,... | collective-permute-start | bytes 294920 | tf_op jit(solution)/shard_map/ppermute | solution.py:627
  22.6 3.7 %collective-permute-start.6 = (bf16[8,512]{1,0:T(8,128)(2,1)S(1)}, bf16[8,512]{1,0:T(8,128)(2,1)S(1)}, u32[]{:S(2)}, u32[]{:S(2)}) collective-permute-start(bf16[8,512]{1,0:T(8,128)(2,1)S(1)} %get-tuple-element.46), channel_id=1, source_target_pairs={{0,8},{4,12},{8,0},{12,4},{1,9},{5,13},{9,1},{13,5},{2,10},{6,14},... | collective-permute-start | bytes 24584 | tf_op jit(solution)/shard_map/ppermute | solution.py:736

commit v12 on v11

--- a/solution.py
+++ b/solution.py
@@ -508,8 +508,6 @@
         for payload_ref in payload_refs:
             z = z + dot(place_rows, payload_ref[...])
     z = z.astype(bf)
-    even = dot(z[:tall], table_ref[:, :half])
-    odd = dot(z[tall:], table_ref[:, half:])
 
     top_in = place > 0
     low_in = place < strips - 1
@@ -523,10 +521,15 @@
             step = halo_slope_ref[edge : edge + PAD, here] * grad[to : to + PAD]
             level_ref[b, to : to + PAD] = halo_ref[edge : edge + PAD, here] - step
 
-    for b in range(half // LANES):
-        part = slice(b * LANES, (b + 1) * LANES)
-        advance(b, even[:, part] - odd[:, part])
-        advance(blocks - 1 - b, mirrored(even[:, part] + odd[:, part]))
+    width = min(CHUNK, half)
+    for start in range(0, half, width):
+        even = dot(z[:tall], table_ref[:, start : start + width])
+        odd = dot(z[tall:], table_ref[:, half + start : half + start + width])
+        for b in range(width // LANES):
+            part = slice(b * LANES, (b + 1) * LANES)
+            spot = start // LANES + b
+            advance(spot, even[:, part] - odd[:, part])
+            advance(blocks - 1 - spot, mirrored(even[:, part] + odd[:, part]))
 
     lane = lax.broadcasted_iota(jnp.int32, (8, LANES), 1)
     nothing = jnp.zeros((8, LANES), f32)

time: 29 us -> 28.9 us (level)
  no operation moved by 1% of the time
where the time goes in v12:
time: 28.9 us; the launch traced here: 28.7 us
  Pallas kernels  13 us (45%)
  starting transfers between devices  8.91 us (31%)
  waiting for transfers between devices  6.13 us (21%)
  between operations  0.72 us (2%)
    pallas_call x9, Pallas kernels, call(): pl.pallas_call(kernel, out_shape=outs, in_specs=[spec(kind) for kind in k...  13 us
    ppermute x4, starting transfers between devices, pair_up(): return lax.ppermute(block, ('strip', 'focus'), moves)  4.67 us
    ppermute x1, waiting for transfers between devices, on_device(): other = lax.ppermute(part, 'focus', [(i, i ^ step) for i in range(planes)])  3.32 us
    ppermute x1, waiting for transfers between devices, on_device(): lax.ppermute(payload, 'strip', [(i, (i - turn_by) % strips) for i in rang...  2.8 us
    ppermute x1, starting transfers between devices, on_device(): other_defocus = lax.ppermute(defocus, 'focus', swap)  2.65 us
    ppermute x1, starting transfers between devices, on_device(): other = lax.ppermute(part, 'focus', [(i, i ^ step) for i in range(planes)])  0.92 us
    ppermute x1, starting transfers between devices, on_device(): lax.ppermute(payload, 'strip', [(i, (i - turn_by) % strips) for i in rang...  0.67 us
  transfers between devices with their start and end apart: 7, of which 2 were waited for; matrix products, arithmetic and copies ran while one was open for 0% of the time, Pallas kernels for 15%

profile of v12, /device:TPU:0, one launch (start us, length us, event | category | flops | bytes accessed | tf_op | source)
XLA Modules:
  0.0 28.7 jit_solution(17302398366293563226)
XLA Ops:
  0.0 2.6 %shard_map.73 = (bf16[512,2048]{1,0:T(8,128)(2,1)S(1)}, f32[96,512]{1,0:T(8,128)S(1)}, bf16[104,512]{1,0:T(8,128)(2,1)S(1)}, bf16[104,512]{1,0:T(8,128)(2,1)S(1)...) custom-call(f32[64,2048]{1,0:T(8,128)} %phi_hbm.1, ...), custom_call_target="tpu_custom_call" | custom-call | flops 1000000 | bytes 4194304 | tf_op jit(solution)/shard_map/pallas_call | solution.py:607
  2.6 0.6 %collective-permute-start = (bf16[104,512]{1,0:T(8,128)(2,1)S(1)}, bf16[104,512]{1,0:T(8,128)(2,1)S(1)}, u32[]{:S(2)}, u32[]{:S(2)}) collective-permute-start(bf16[104,512]{1,0:T(8,128)(2,1)S(1)} %get-tuple-element.28), channel_id=1, source_target_pairs={{0,4},{1,5},{2,6},{3,7},{4,0},{5,1},{6,2},{7,3},{8,12},{9,13},{10,... | collective-permute-start | bytes 319496 | tf_op jit(solution)/shard_map/ppermute | solution.py:630
  3.2 2.6 %collective-permute-start.1 = (bf16[104,512]{1,0:T(8,128)(2,1)S(1)}, bf16[104,512]{1,0:T(8,128)(2,1)S(1)}, u32[]{:S(2)}, u32[]{:S(2)}) collective-permute-start(bf16[104,512]{1,0:T(8,128)(2,1)S(1)} %get-tuple-element.29), channel_id=1, source_target_pairs={{0,1},{1,0},{2,3},{3,2},{4,8},{5,9},{6,10},{7,11},{8,4},{9,5},{10,... | collective-permute-start | bytes 319496 | tf_op jit(solution)/shard_map/ppermute | solution.py:630
  6.5 2.7 %collective-permute-start.2 = (f32[8,128]{1,0:T(8,128)S(1)}, f32[8,128]{1,0:T(8,128)S(1)}, u32[]{:S(2)}, u32[]{:S(2)}) collective-permute-start(f32[8,128]{1,0:T(8,128)S(1)} %shard_map.74.defocus_ref), channel_id=1, source_target_pairs={{0,2},{1,3},{2,0},{3,1},{4,6},{5,7},{6,4},{7,5},{8,10},{9,11},{10,... | collective-permute-start | bytes 12296 | tf_op jit(solution)/shard_map/ppermute | solution.py:677
  9.1 0.5 %shard_map.75 = (bf16[96,128]{1,0:T(8,128)(2,1)S(1)}, bf16[128,96]{1,0:T(8,128)(2,1)S(1)}, f32[4,48,512]{2,1,0:T(8,128)S(1)}, f32[4,48,512]{2,1,0:T(8,128)S(1)}, f32[64,2048]{1,0:T(8,128)S(1)}) custom-call(f32[8,128]{1,0:T(8,128)S(1)} %shard_map.74.defocus_ref, f32[8,128]{1,0:T(8,128)S(1)} %get-tuple-element.27.after_ref.freq_ref, ...), custom_call_target="tpu_custom_call" | custom-call | flops 4000000000 | bytes 4194304 | tf_op jit(solution)/shard_map/pallas_call | solution.py:607
  9.7 0.0 collective-permute-done.from_a_ref
  9.7 0.0 collective-permute-done.1.from_b_ref
  9.7 3.2 %shard_map.76.rest_0_ = f32[96,512]{1,0:T(8,128)S(1)} custom-call(f32[96,512]{1,0:T(8,128)S(1)} %get-tuple-element.30.own_ref, bf16[104,512]{1,0:T(8,128)(2,1)S(1)} %collective-permute-done.from_a_ref, bf16[104,512]{1,0:T(8,128)(2,1)S(1)} %collective-permute-done.1.from_b_ref, f32[64,2048]{1,0:T(8,128)S(1)} %get-tuple-element.34.goal_ref, ...), custom_call_target="tpu_custom_call" | custom-call | flops 4000000000 | bytes 4194304 | tf_op jit(solution)/shard_map/pallas_call | solution.py:607
  12.9 0.0 collective-permute-done.2.rest_1_
  12.9 3.4 %shard_map.77.part_ref = bf16[96,512]{1,0:T(8,128)(2,1)S(1)} custom-call(f32[96,512]{1,0:T(8,128)S(1)} %get-tuple-element.30.own_ref, bf16[104,512]{1,0:T(8,128)(2,1)S(1)} %collective-permute-done.from_a_ref, bf16[104,512]{1,0:T(8,128)(2,1)S(1)} %collective-permute-done.1.from_b_ref, f32[64,2048]{1,0:T(8,128)S(1)} %get-tuple-element.34.goal_ref, ...), custom_call_target="tpu_custom_call" | custom-call | flops 4000000000 | bytes 4194304 | tf_op jit(solution)/shard_map/pallas_call | solution.py:607
  16.3 0.9 %collective-permute-start.3 = (bf16[96,512]{1,0:T(8,128)(2,1)S(1)}, bf16[96,512]{1,0:T(8,128)(2,1)S(1)}, u32[]{:S(2)}, u32[]{:S(2)}) collective-permute-start(bf16[96,512]{1,0:T(8,128)(2,1)S(1)} %shard_map.77.part_ref), channel_id=1, source_target_pairs={{0,1},{1,0},{2,3},{3,2},{4,5},{5,4},{6,7},{7,6},{8,9},{9,8},{10,11... | collective-permute-start | bytes 294920 | tf_op jit(solution)/shard_map/ppermute | solution.py:729
  17.2 0.4 %shard_map.78 = (bf16[3,160,96]{2,1,0:T(8,128)(2,1)S(1)}, bf16[1,8,96]{2,1,0:T(8,128)(2,1)S(1)}, f32[64,2048]{1,0:T(8,128)S(1)}, f32[16,2048]{1,0:T(8,128)S(1)}, f32[16,2048]{1,0:T(8,128)S(1)}) custom-call(f32[8,128]{1,0:T(8,128)S(1)} %get-tuple-element.27.after_ref.freq_ref, f32[64,2048]{1,0:T(8,128)S(1)} %get-tuple-element.26.phi_ref, ...), custom_call_target="tpu_custom_call" | custom-call | flops 2000000000 | bytes 4194304 | tf_op jit(solution)/shard_map/pallas_call | solution.py:607
  17.6 3.3 %collective-permute-done.3.other_ref = bf16[96,512]{1,0:T(8,128)(2,1)S(1)} collective-permute-done((bf16[96,512]{1,0:T(8,128)(2,1)S(1)}, bf16[96,512]{1,0:T(8,128)(2,1)S(1)}, u32[]{:S(2)}, u32[]{:S(2)}) %collective-permute-start.3) | collective-permute-done | bytes 98336 | tf_op jit(solution)/shard_map/ppermute | solution.py:729
  21.0 0.1 shard_map.79
  21.1 0.0 collective-permute-start.4
  21.1 1.5 %collective-permute-start.5 = (bf16[96,512]{1,0:T(8,128)(2,1)S(1)}, bf16[96,512]{1,0:T(8,128)(2,1)S(1)}, u32[]{:S(2)}, u32[]{:S(2)}) collective-permute-start(bf16[96,512]{1,0:T(8,128)(2,1)S(1)} %get-tuple-element.45.y_ref), channel_id=1, source_target_pairs={{0,1},{1,0},{2,3},{3,2},{4,8},{5,9},{6,10},{7,11},{8,4},{9,5},{10,... | collective-permute-start | bytes 294920 | tf_op jit(solution)/shard_map/ppermute | solution.py:630
  22.6 0.7 %collective-permute-start.6 = (bf16[8,512]{1,0:T(8,128)(2,1)S(1)}, bf16[8,512]{1,0:T(8,128)(2,1)S(1)}, u32[]{:S(2)}, u32[]{:S(2)}) collective-permute-start(bf16[8,512]{1,0:T(8,128)(2,1)S(1)} %get-tuple-element.46), channel_id=1, source_target_pairs={{0,8},{4,12},{8,0},{12,4},{1,9},{5,13},{9,1},{13,5},{2,10},{6,14},... | collective-permute-start | bytes 24584 | tf_op jit(solution)/shard_map/ppermute | solution.py:739
  23.3 0.2 shard_map.80.z_own_ref
  23.4 2.8 %collective-permute-done.6.rest_0_ = bf16[8,512]{1,0:T(8,128)(2,1)S(1)} collective-permute-done((bf16[8,512]{1,0:T(8,128)(2,1)S(1)}, bf16[8,512]{1,0:T(8,128)(2,1)S(1)}, u32[]{:S(2)}, u32[]{:S(2)}) %collective-permute-start.6) | collective-permute-done | bytes 8224 | tf_op jit(solution)/shard_map/ppermute | solution.py:739
  26.2 0.0 collective-permute-done.4.y_a_ref
  26.2 0.0 collective-permute-done.5.y_b_ref
  26.2 2.5 %shard_map.81 = f32[64,2048]{1,0:T(8,128)} custom-call(f32[64,2048]{1,0:T(8,128)S(1)} %get-tuple-element.26.phi_ref, f32[64,2048]{1,0:T(8,128)S(1)} %get-tuple-element.40.slope_ref, f32[16,2048]{1,0:T(8,128)S(1)} %get-tuple-element.41.halo_ref, f32[16,2048]{1,0:T(8,128)S(1)} %get-tuple-element.42.halo_slope_ref, ...), custom_call_target="tpu_custom_call" | custom-call | flops 1000000 | bytes 4194304 | tf_op jit(solution)/shard_map/pallas_call | solution.py:607
  (1 shorter events, 0.0 us)
Async XLA Ops:
  2.6 7.0 %collective-permute-start = (bf16[104,512]{1,0:T(8,128)(2,1)S(1)}, bf16[104,512]{1,0:T(8,128)(2,1)S(1)}, u32[]{:S(2)}, u32[]{:S(2)}) collective-permute-start(bf16[104,512]{1,0:T(8,128)(2,1)S(1)} %get-tuple-element.28), channel_id=1, source_target_pairs={{0,4},{1,5},{2,6},{3,7},{4,0},{5,1},{6,2},{7,3},{8,12},{9,13},{10,... | collective-permute-start | bytes 319496 | tf_op jit(solution)/shard_map/ppermute | solution.py:630
  3.2 6.5 %collective-permute-start.1 = (bf16[104,512]{1,0:T(8,128)(2,1)S(1)}, bf16[104,512]{1,0:T(8,128)(2,1)S(1)}, u32[]{:S(2)}, u32[]{:S(2)}) collective-permute-start(bf16[104,512]{1,0:T(8,128)(2,1)S(1)} %get-tuple-element.29), channel_id=1, source_target_pairs={{0,1},{1,0},{2,3},{3,2},{4,8},{5,9},{6,10},{7,11},{8,4},{9,5},{10,... | collective-permute-start | bytes 319496 | tf_op jit(solution)/shard_map/ppermute | solution.py:630
  6.5 6.4 %collective-permute-start.2 = (f32[8,128]{1,0:T(8,128)S(1)}, f32[8,128]{1,0:T(8,128)S(1)}, u32[]{:S(2)}, u32[]{:S(2)}) collective-permute-start(f32[8,128]{1,0:T(8,128)S(1)} %shard_map.74.defocus_ref), channel_id=1, source_target_pairs={{0,2},{1,3},{2,0},{3,1},{4,6},{5,7},{6,4},{7,5},{8,10},{9,11},{10,... | collective-permute-start | bytes 12296 | tf_op jit(solution)/shard_map/ppermute | solution.py:677
  16.3 4.7 %collective-permute-start.3 = (bf16[96,512]{1,0:T(8,128)(2,1)S(1)}, bf16[96,512]{1,0:T(8,128)(2,1)S(1)}, u32[]{:S(2)}, u32[]{:S(2)}) collective-permute-start(bf16[96,512]{1,0:T(8,128)(2,1)S(1)} %shard_map.77.part_ref), channel_id=1, source_target_pairs={{0,1},{1,0},{2,3},{3,2},{4,5},{5,4},{6,7},{7,6},{8,9},{9,8},{10,11... | collective-permute-start | bytes 294920 | tf_op jit(solution)/shard_map/ppermute | solution.py:729
  21.1 5.1 %collective-permute-start.4 = (bf16[96,512]{1,0:T(8,128)(2,1)S(1)}, bf16[96,512]{1,0:T(8,128)(2,1)S(1)}, u32[]{:S(2)}, u32[]{:S(2)}) collective-permute-start(bf16[96,512]{1,0:T(8,128)(2,1)S(1)} %get-tuple-element.45.y_ref), channel_id=1, source_target_pairs={{0,4},{1,5},{2,6},{3,7},{4,0},{5,1},{6,2},{7,3},{8,12},{9,13},{10,... | collective-permute-start | bytes 294920 | tf_op jit(solution)/shard_map/ppermute | solution.py:630
  21.1 5.1 %collective-permute-start.5 = (bf16[96,512]{1,0:T(8,128)(2,1)S(1)}, bf16[96,512]{1,0:T(8,128)(2,1)S(1)}, u32[]{:S(2)}, u32[]{:S(2)}) collective-permute-start(bf16[96,512]{1,0:T(8,128)(2,1)S(1)} %get-tuple-element.45.y_ref), channel_id=1, source_target_pairs={{0,1},{1,0},{2,3},{3,2},{4,8},{5,9},{6,10},{7,11},{8,4},{9,5},{10,... | collective-permute-start | bytes 294920 | tf_op jit(solution)/shard_map/ppermute | solution.py:630
  22.6 3.7 %collective-permute-start.6 = (bf16[8,512]{1,0:T(8,128)(2,1)S(1)}, bf16[8,512]{1,0:T(8,128)(2,1)S(1)}, u32[]{:S(2)}, u32[]{:S(2)}) collective-permute-start(bf16[8,512]{1,0:T(8,128)(2,1)S(1)} %get-tuple-element.46), channel_id=1, source_target_pairs={{0,8},{4,12},{8,0},{12,4},{1,9},{5,13},{9,1},{13,5},{2,10},{6,14},... | collective-permute-start | bytes 24584 | tf_op jit(solution)/shard_map/ppermute | solution.py:739
